TPU v7x, 32 devices: a whole 2x2x4 slice. The times are simulated.
32 devices in a mesh: tm: 8 (over y, x, core), series: 4 (over z).
Axes of the slice: x: 2, y: 2, z: 4, core: 2. Of those that a mesh axis runs over, the one named last changes fastest.
Arguments:
- returns: bfloat16 [4096, 4096], P('tm', 'series'), may hold values from -120 to 120
- innovations: float32 [256, 2, 4096], P('series', None, 'tm'), may hold values from -6 to 6
- decay_rate: float32 [256, 4096], P('series', 'tm'), may hold values from 0.45 to 1
- innov_scale: float32 [256], P('series'), may hold values from 0.5 to 2
- loadings: bfloat16 [4096, 2, 256], P('series'), may hold values from -0.5 to 0.5
- noise_scale: float32 [4096], P('series'), may hold values from 0.5 to 2
Outputs:
- grad_innov: float32 [256, 2, 4096], P('series', None, 'tm')
- grad_load: float32 [4096, 2, 256], P('series')
- log_density: float32 [2], replicated
All inputs are finite; a program needn't handle non-finite values.
Results may differ from a plain program's by a relative error of at most 0.00066.
Values may be sent and summed in bfloat16 or wider, within the bound.
No kernel may reach another device: no remote copies, remote signals or barrier semaphores. Data moves between devices by JAX's collectives and lax.ppermute only.
A program may use at most 64 MiB of HBM per device.

v0:
```python
import functools
import math

import jax
import jax.numpy as jnp
from jax import lax
from jax.experimental import pallas as pl
from jax.experimental.pallas import tpu as pltpu
from jax.sharding import PartitionSpec as P


freedom = 5.0
LANES = 128
TAIL = 16
f32 = jnp.float32
bf16 = jnp.bfloat16
f16 = jnp.float16


def swap(value, axis, key):
    count = lax.axis_size(axis)
    return lax.ppermute(value, axis, [(i, i ^ key) for i in range(count)])


def eye(size):
    rows = lax.broadcasted_iota(jnp.int32, (size, size), 0)
    return rows == lax.broadcasted_iota(jnp.int32, (size, size), 1)


def to_column(row, same):
    return jnp.sum(jnp.where(same, row, 0.0), axis=1, keepdims=True)


def to_row(column, same):
    return jnp.sum(jnp.where(same, column, 0.0), axis=0, keepdims=True)


def tile_scan(decay, pushes, backward):
    lane = lax.broadcasted_iota(jnp.int32, decay.shape, 1)
    width = decay.shape[1]
    step = 1
    while step < width:
        turn = width - step if backward else step
        inside = lane < width - step if backward else lane >= step
        gate = jnp.where(inside, decay, 0.0)
        pushes = [p + gate * pltpu.roll(p, turn, 1) for p in pushes]
        decay = decay * jnp.where(inside, pltpu.roll(decay, turn, 1), 1.0)
        step *= 2
    return decay, pushes


def block_scan(decays, pushes, backward):
    tiles = len(decays)
    draws = len(pushes[0])
    order = range(tiles - 1, -1, -1) if backward else range(tiles)
    edge = slice(0, 1) if backward else slice(LANES - 1, LANES)
    run, out = [None] * tiles, [None] * tiles
    carry = None
    for j in order:
        a, b = tile_scan(decays[j], pushes[j], backward)
        if carry is not None:
            b = [b[d] + a * carry[1][d] for d in range(draws)]
            a = a * carry[0]
        run[j], out[j] = a, b
        carry = (a[:, edge], [x[:, edge] for x in b])
    return run, out, carry


def beyond_kernel(tiles, decay, spread, beyond, product):
    factors = decay.shape[0]
    lane = lax.broadcasted_iota(jnp.int32, (factors, LANES), 1)
    after = jnp.ones((factors, 1), f32)
    for j in range(tiles - 1, -1, -1):
        part = slice(j * LANES, (j + 1) * LANES)
        a = decay[:, part]
        spread[:, part] = jnp.sqrt((1.0 - a) * (1.0 + a))
        run, _ = tile_scan(a, [], True)
        beyond[:, part] = jnp.where(lane < LANES - 1, pltpu.roll(run, LANES - 1, 1), 1.0) * after
        after = after * run[:, 0:1]
    product[...] = to_row(after, eye(factors))


def edge_kernel(draws, tiles, innov, scale, spread, beyond, product, weight, summary, squares):
    factors = spread.shape[0]
    same = eye(factors)
    column = to_column(scale[...], same)
    total = [jnp.zeros((factors, LANES), f32)] * draws
    ends = [jnp.zeros((factors, LANES), f32)] * draws
    for j in range(tiles):
        part = slice(j * LANES, (j + 1) * LANES)
        w = spread[:, part] * column
        weight[:, part] = w
        for d in range(draws):
            x = innov[pl.ds(j * draws + d, factors, stride=tiles * draws), :]
            total[d] = total[d] + x * x
            ends[d] = ends[d] + w * x * beyond[:, part]
    summary[0:1, :] = product[...]
    for d in range(draws):
        summary[d + 1:d + 2, :] = to_row(jnp.sum(ends[d], axis=1, keepdims=True), same)
        squares[d:d + 1, :] = jnp.sum(total[d], axis=0, keepdims=True)


def forward_kernel(draws, tiles, innov, decay, weight, local, running):
    factors = decay.shape[0]
    decays, pushes = [], []
    for j in range(tiles):
        part = slice(j * LANES, (j + 1) * LANES)
        decays.append(decay[:, part])
        rows = lambda d: pl.ds(j * draws + d, factors, stride=tiles * draws)
        pushes.append([weight[:, part] * innov[rows(d), :] for d in range(draws)])
    run, out, _ = block_scan(decays, pushes, False)
    for j in range(tiles):
        running[:, j * LANES:(j + 1) * LANES] = run[j]
        for d in range(draws):
            local[d, :, j * LANES:(j + 1) * LANES] = out[j][d]


def seat(backward):
    count, mine = lax.axis_size("tm"), lax.axis_index("tm")
    return count - 1 - mine if backward else mine


def pair_kernel(rows, backward, summary, other, whole):
    later = seat(backward) % 2 == 1
    mine, theirs = summary[...], other[...]
    first, second = jnp.where(later, theirs, mine), jnp.where(later, mine, theirs)
    whole[0:1, :] = first[0:1] * second[0:1]
    whole[1:rows, :] = second[0:1] * first[1:rows] + second[1:rows]
    if rows < mine.shape[0]:
        whole[rows:, :] = first[rows:] + second[rows:]


def entered(rows, backward, other, totals):
    mine = seat(backward)
    later, pair, pairs = mine % 2 == 1, mine // 2, len(totals)
    theirs = other[...]
    values = [total[...] for total in totals]
    entering = jnp.zeros_like(theirs[1:rows])
    summed = jnp.zeros_like(theirs[rows:]) if rows < theirs.shape[0] else None
    for place in range(pairs):
        here = values[0]
        for key in range(1, pairs):
            here = jnp.where((pair ^ key) == place, values[key], here)
        entering = jnp.where(place < pair, here[0:1] * entering + here[1:rows], entering)
        if summed is not None:
            summed = summed + here[rows:]
    return jnp.where(later, theirs[0:1] * entering + theirs[1:rows], entering), summed


def enter_kernel(draws, local, running, other, *refs):
    totals, path = refs[:-1], refs[-1]
    same = eye(running.shape[0])
    entering, _ = entered(draws + 1, False, other, totals)
    for d in range(draws):
        column = to_column(entering[d:d + 1, :], same)
        path[d] = (local[d] + running[...] * column).astype(bf16)


def residual_kernel(draws, parts, *refs):
    pieces, (returns, loads, loads_t, noise, squares, grads, shares, paths, density, top) = refs[:parts], refs[parts:]
    factors = pieces[0].shape[1]
    step = pl.program_id(0)
    count = pl.num_programs(0)
    wide = paths.shape[1] // LANES
    side = step // (count // 2)
    base = (step % (count // 2)) * (returns.shape[0] * wide * draws)

    @pl.when(step == 0)
    def _():
        for n in range(parts):
            start = pl.multiple_of((lax.axis_index("series") ^ n) * factors, factors)
            paths[:, pl.ds(start, factors), :] = pieces[n][...]
        grads[...] = jnp.zeros_like(grads)
        density[...] = jnp.zeros_like(density)
        top[...] = jnp.zeros_like(top)

    seen = returns[...].astype(f32)
    rows = seen.shape[0]
    same = eye(LANES)
    groups = rows // LANES
    spread = [to_column(noise[pl.ds(step * groups + g, 1), :], same) for g in range(groups)]
    spread = jnp.concatenate(spread, axis=0)
    s2 = freedom * (spread * spread)
    inverse = 1.0 / s2
    tiles = seen.shape[1] // LANES
    half = rows // 2
    for d in range(draws):
        fitted = jnp.dot(loads[d], paths[d], preferred_element_type=f32)
        residual = seen - fitted
        square = residual * residual
        pulled = ((freedom + 1.0) * residual / (s2 + square)).astype(bf16)
        ratio = square * inverse
        first, second = ratio[:half], ratio[half:]
        both = jnp.log1p(first + second * (1.0 + first))
        both = jnp.sum(both, axis=0, keepdims=True)
        lanes = both[:, :LANES]
        for j in range(1, both.shape[1] // LANES):
            lanes = lanes + both[:, j * LANES:(j + 1) * LANES]
        density[d:d + 1, :] += lanes
        product = jnp.dot(loads_t[d], pulled, preferred_element_type=f32)
        for n in range(parts):
            for j in range(tiles):
                to = slice((d * tiles + j) * factors, (d * tiles + j + 1) * factors)
                grads[n, to, :] += product[n * factors:(n + 1) * factors, j * LANES:(j + 1) * LANES]
        share = lax.dot_general(pulled, paths[d], (((1,), (1,)), ((), ())), preferred_element_type=f32)
        most = top[...]
        for j in range(wide):
            tile = share[:, j * LANES:(j + 1) * LANES]
            shares[side, pl.ds(base + (j * draws + d), rows, stride=wide * draws), :] = tile
            most = jnp.maximum(most, jnp.max(jnp.abs(tile).reshape(rows // 8, 8, LANES), axis=0))
        top[...] = most

    @pl.when(step == pl.num_programs(0) - 1)
    def _():
        body = draws * tiles * factors
        cells = pl.num_programs(0) * rows * seen.shape[1]
        peak = jnp.zeros((1, LANES), f32)
        for n in range(parts):
            peak = jnp.maximum(peak, jnp.max(jnp.abs(grads[n, :body, :]), axis=0, keepdims=True))
        level = exponent(peak)
        tail = [level]
        for d in range(draws):
            value = -(freedom + 1.0) * 0.5 * density[d:d + 1, :] - 0.5 * squares[d:d + 1, :]
            tail += coded(jnp.sum(value, axis=1, keepdims=True) * (1.0 / cells))
        tail = stacked(tail)
        factor = jnp.exp2(15.0 - level)
        for n in range(parts):
            grads[n, :body, :] = grads[n, :body, :] * factor
            grads[n, body:, :] = tail
        half = shares.shape[1] - TAIL
        level = exponent(jnp.max(top[...], axis=0, keepdims=True))
        factor = jnp.exp2(15.0 - level)
        for n in range(2):
            shares[n, :half, :] = shares[n, :half, :] * factor
            shares[n, half:, :] = stacked([level])


def coded(value):
    value = jnp.broadcast_to(value, (1, LANES))
    level = exponent(jnp.abs(value))
    left = value * jnp.exp2(-level)
    codes = [level]
    unit = 1024.0
    for _ in range(3):
        code = (left * unit + 12582912.0) - 12582912.0
        codes.append(code)
        left = left - code * (1.0 / unit)
        unit = unit * 1024.0
    return codes


def decoded(rows):
    level, first, second, third = [rows[n:n + 1, :] for n in range(4)]
    small = 1.0 / 1024.0
    return jnp.exp2(level) * (first + (second + third * small) * small) * small


def stacked(rows):
    place = lax.broadcasted_iota(jnp.int32, (TAIL, LANES), 0)
    out = jnp.zeros((TAIL, LANES), f32)
    for n, row in enumerate(rows):
        out = jnp.where(place == n, row, out)
    return out


def exponent(lanes):
    top = jnp.maximum(jnp.max(lanes, axis=1, keepdims=True), 1e-30)
    return jnp.broadcast_to(jnp.ceil(jnp.log(top) * (1.0 / math.log(2.0))), lanes.shape)


def join_kernel(mine, other, out):
    core = lax.axis_index("tm") % 2
    body = other.shape[0] - TAIL
    chips = out.shape[0]
    piece = body // chips
    own, far = mine[core, body:body + 1, :], other[body:body + 1, :]
    level = jnp.maximum(own, far) + 1.0
    own, far = jnp.exp2(own - level), jnp.exp2(far - level)
    for n in range(chips):
        rows = slice(n * piece, (n + 1) * piece)
        out[n, :piece, :] = mine[core, rows, :] * own + other[rows, :] * far
        out[n, piece:, :] = stacked([level])


def total_kernel(lift, mine, *refs):
    others, (out, factor) = refs[:-2], refs[-2:]
    piece = out.shape[0]
    here = lax.axis_index("tm") // 2
    levels = [mine[here, piece:piece + 1, :]] + [other[piece:piece + 1, :] for other in others]
    top = levels[0]
    for level in levels[1:]:
        top = jnp.maximum(top, level)
    top = top + lift
    total = mine[here, :piece, :] * jnp.exp2(levels[0] - top)
    for level, other in zip(levels[1:], others):
        total = total + other[:piece, :] * jnp.exp2(level - top)
    out[...] = total
    factor[...] = jnp.exp2(top - 15.0)


def gather_kernel(draws, tiles, parts, running, products, mine, *refs):
    others, (gathered, summary) = refs[:-2], refs[-2:]
    factors = running.shape[0]
    body = draws * tiles * factors
    here = lax.axis_index("series")
    tails = [mine[here, body:, :]] + [other[body:, :] for other in others]
    scales = [jnp.exp2(rows[0:1, :] - 15.0) for rows in tails]
    same = eye(factors)
    summary[0:1, :] = products[0:1, :]
    for d in range(draws):
        known = [decoded(rows[1 + 4 * d:5 + 4 * d, :]) for rows in tails]
        density = jnp.zeros((1, LANES), f32)
        for place in range(parts):
            for n in range(parts):
                density = density + jnp.where((here ^ n) == place, known[n], 0.0)
        summary[draws + 1 + d:draws + 2 + d, :] = density[:, :factors]
        leaving = jnp.zeros((factors, LANES), f32)
        for j in range(tiles):
            rows = slice((d * tiles + j) * factors, (d * tiles + j + 1) * factors)
            value = mine[here, rows, :] * scales[0]
            for other, scale in zip(others, scales[1:]):
                value = value + other[rows, :] * scale
            gathered[rows, :] = value
            leaving = leaving + value * running[:, j * LANES:(j + 1) * LANES]
        summary[d + 1:d + 2, :] = to_row(jnp.sum(leaving, axis=1, keepdims=True), same)


def backward_kernel(draws, tiles, decay, grads, local, tail):
    factors = decay.shape[0]
    lane = lax.broadcasted_iota(jnp.int32, (factors, LANES), 1)
    decays, pushes = [], []
    for j in range(tiles):
        a = decay[:, j * LANES:(j + 1) * LANES]
        if j + 1 < tiles:
            after = decay[:, (j + 1) * LANES:(j + 2) * LANES][:, 0:1]
        else:
            after = jnp.ones((factors, 1), f32)
        decays.append(jnp.where(lane < LANES - 1, pltpu.roll(a, LANES - 1, 1), after))
        rows = lambda d: slice((d * tiles + j) * factors, (d * tiles + j + 1) * factors)
        pushes.append([grads[rows(d), :] for d in range(draws)])
    run, out, _ = block_scan(decays, pushes, True)
    for j in range(tiles):
        tail[:, j * LANES:(j + 1) * LANES] = run[j]
        for d in range(draws):
            local[d, :, j * LANES:(j + 1) * LANES] = out[j][d]


def leave_kernel(draws, tiles, local, tail, weight, innov, other, *refs):
    totals, (out, density) = refs[:-2], refs[-2:]
    factors = tail.shape[0]
    same = eye(factors)
    arriving, summed = entered(draws + 1, True, other, totals)
    density[...] = summed
    for d in range(draws):
        column = to_column(arriving[d:d + 1, :], same)
        for j in range(tiles):
            part = slice(j * LANES, (j + 1) * LANES)
            rows = pl.ds(j * draws + d, factors, stride=tiles * draws)
            adjoint = local[d, :, part] + tail[:, part] * column
            out[rows, :] = weight[:, part] * adjoint - innov[rows, :]


def room(mebibytes):
    return pltpu.CompilerParams(vmem_limit_bytes=mebibytes << 20)


def assemble_kernel(*refs):
    pieces, out = refs[:-1], refs[-1]
    rows = pieces[0].shape[0]
    for key, piece in enumerate(pieces):
        start = pl.multiple_of(((lax.axis_index("tm") // 2) ^ key) * rows, rows)
        out[pl.ds(start, rows), :] = piece[...]


def write_kernel(flip, value, factor, *refs):
    out, scaled, sem = refs[-3:]
    half = value.shape[0]
    scaled[...] = value[...] * factor[...]
    move = pltpu.make_async_copy(scaled, out.at[pl.ds(pl.multiple_of(((lax.axis_index("tm") + flip) % 2) * half, half), half), :], sem)
    move.start()
    move.wait()


def write_half(value, factor, flip, out, size):
    far = pl.BlockSpec(memory_space=pltpu.HBM)
    specs = [pl.BlockSpec(memory_space=pltpu.VMEM)] * 2
    return pl.pallas_call(
        functools.partial(write_kernel, flip),
        out_shape=shape((size, LANES), f32),
        in_specs=specs if out is None else specs + [far],
        out_specs=far,
        input_output_aliases={} if out is None else {2: 0},
        scratch_shapes=[pltpu.VMEM(value.shape, f32), pltpu.SemaphoreType.DMA],
        name="write_half",
        compiler_params=room(4),
    )(value, factor, *([] if out is None else [out]))


def shape(dims, kind):
    return jax.ShapeDtypeStruct(dims, kind)


def carried(summary, rows, backward):
    pairs = lax.axis_size("tm") // 2
    other = swap(summary, "tm", 1)
    whole = pl.pallas_call(
        functools.partial(pair_kernel, rows, backward),
        out_shape=shape(summary.shape, f32),
        compiler_params=room(1),
    )(summary, other)
    return [other, whole] + [swap(whole, "tm", 2 * key) for key in range(1, pairs)]


def local(returns, innovations, decay_rate, innov_scale, loadings, noise_scale):
    factors, draws, steps = innovations.shape
    series = returns.shape[1]
    parts, spans = lax.axis_size("series"), lax.axis_size("tm")
    where, when = lax.axis_index("series"), lax.axis_index("tm")
    tiles = steps // LANES
    all_factors = factors * parts
    wide = all_factors * draws // LANES

    innov = innovations.reshape(factors, draws, tiles, LANES).transpose(0, 2, 1, 3)
    innov = innov.reshape(factors * tiles * draws, LANES)
    numbers = [where ^ key for key in range(parts)] + [1 - when % 2]
    numbers += [(when // 2) ^ key for key in range(spans // 2)]
    decay_rate, numbers = lax.optimization_barrier((decay_rate, numbers))
    seats, far_core = numbers[:parts], numbers[parts]
    chips_at = numbers[parts + 1:]
    spread, beyond, product = pl.pallas_call(
        functools.partial(beyond_kernel, tiles),
        out_shape=(shape((factors, steps), f32), shape((factors, steps), f32), shape((1, factors), f32)),
        name="beyond",
        compiler_params=room(2),
    )(decay_rate)
    weight, summary, squares = pl.pallas_call(
        functools.partial(edge_kernel, draws, tiles),
        out_shape=(
            shape((factors, steps), f32),
            shape((draws + 1, factors), f32),
            shape((draws, LANES), f32),
        ),
        name="edge",
        compiler_params=room(3),
    )(innov, innov_scale.reshape(1, factors), spread, beyond, product)
    local_paths, running = pl.pallas_call(
        functools.partial(forward_kernel, draws, tiles),
        out_shape=(shape((draws, factors, steps), f32), shape((factors, steps), f32)),
        name="forward_scan",
        compiler_params=room(4),
    )(innov, decay_rate, weight)
    path_low = pl.pallas_call(
        functools.partial(enter_kernel, draws),
        out_shape=shape((draws, factors, steps), bf16),
        name="enter",
        compiler_params=room(2),
    )(local_paths, running, *carried(summary, draws + 1, False))

    pieces = [path_low] + [swap(path_low, "series", key) for key in range(1, parts)]
    noise = noise_scale.reshape(series // LANES, LANES)
    seen = returns.T
    loads = loadings.transpose(1, 0, 2)
    loads_t = loadings.transpose(1, 2, 0)
    rows = min(256, series // 2)
    body = draws * tiles * factors
    still = lambda dims: pl.BlockSpec(dims, lambda i: (0,) * len(dims))
    size = series * wide
    half, piece = size // 2, size // spans
    grads, load_share = pl.pallas_call(
        functools.partial(residual_kernel, draws, parts),
        out_shape=(
            shape((parts, body + TAIL, LANES), f32),
            shape((2, half + TAIL, LANES), f32),
        ),
        grid_spec=pl.GridSpec(
            grid=(series // rows,),
            in_specs=[still((draws, factors, steps))] * parts
            + [
                pl.BlockSpec((rows, steps), lambda i: (i, 0)),
                pl.BlockSpec((draws, rows, all_factors), lambda i: (0, i, 0)),
                pl.BlockSpec((draws, all_factors, rows), lambda i: (0, 0, i)),
                still((series // LANES, LANES)),
                still((draws, LANES)),
            ],
            out_specs=[
                still((parts, body + TAIL, LANES)),
                still((2, half + TAIL, LANES)),
            ],
            scratch_shapes=[
                pltpu.VMEM((draws, all_factors, steps), bf16),
                pltpu.VMEM((draws, LANES), f32),
                pltpu.VMEM((8, LANES), f32),
            ],
        ),
        name="residual",
        compiler_params=room(16),
    )(*pieces, seen, loads, loads_t, noise, squares)

    pick = lambda value, place: lax.dynamic_slice(value, (place, 0, 0), (1,) + value.shape[1:], allow_negative_indices=False)[0]
    sent = [pick(grads, place).astype(f16) for place in seats[1:]]
    arrived = [swap(value, "series", key + 1) for key, value in enumerate(sent)]

    chips = spans // 2
    whole = pl.BlockSpec(memory_space=pltpu.VMEM)
    other = swap(pick(load_share, far_core).astype(f16), "tm", 1).astype(f32)
    kept = pl.pallas_call(
        join_kernel,
        out_shape=shape((chips, piece + TAIL, LANES), f32),
        in_specs=[whole, whole],
        out_specs=whole,
        name="join",
        compiler_params=room(8),
    )(load_share, other)
    others = [swap(pick(kept, chips_at[key]).astype(f16), "tm", 2 * key).astype(f32) for key in range(1, chips)]
    total, factor = pl.pallas_call(
        functools.partial(total_kernel, float(math.ceil(math.log2(chips)))),
        out_shape=(shape((piece, LANES), f32), shape((1, LANES), f32)),
        in_specs=[whole] * chips,
        out_specs=(whole, whole),
        name="total",
        compiler_params=room(4),
    )(kept, *others)
    total = lax.optimization_barrier(total.astype(f16))
    totals = [total] + [swap(total, "tm", 2 * key) for key in range(1, chips)]
    mine = pl.pallas_call(
        assemble_kernel,
        out_shape=shape((half, LANES), f32),
        name="assemble",
        compiler_params=room(4),
    )(*[value.astype(f32) for value in totals])
    theirs = swap(mine.astype(f16), "tm", 1).astype(f32)
    grad_load = None
    for value, flip in ((mine, 0), (theirs, 1)):
        grad_load = write_half(value, factor, flip, grad_load, size)
    grad_load = grad_load.reshape(series, all_factors // LANES, draws, LANES).transpose(0, 2, 1, 3)
    grad_load = grad_load.reshape(series, draws, all_factors)

    path_grads, leaving = pl.pallas_call(
        functools.partial(gather_kernel, draws, tiles, parts),
        out_shape=(shape((body, LANES), f32), shape((2 * draws + 1, factors), f32)),
        name="gather",
        compiler_params=room(4),
    )(running, summary, grads, *[value.astype(f32) for value in arrived])
    local_adjoint, tail = pl.pallas_call(
        functools.partial(backward_kernel, draws, tiles),
        out_shape=(shape((draws, factors, steps), f32), shape((factors, steps), f32)),
        name="backward_scan",
        compiler_params=room(3),
    )(decay_rate, path_grads)
    grad_innov, density = pl.pallas_call(
        functools.partial(leave_kernel, draws, tiles),
        out_shape=(shape(innov.shape, f32), shape((draws, factors), f32)),
        name="leave",
        compiler_params=room(3),
    )(local_adjoint, tail, weight, innov, *carried(leaving, draws + 1, True))
    grad_innov = grad_innov.reshape(factors, tiles, draws, LANES).transpose(0, 2, 1, 3)
    grad_innov = grad_innov.reshape(factors, draws, steps)

    log_density = density[:, 0] / (spans * parts)
    return (grad_innov, grad_load, log_density)


def solution(mesh):
    placed = (
        P("tm", "series"),
        P("series", None, "tm"),
        P("series", "tm"),
        P("series"),
        P("series", None, None),
        P("series"),
    )

    return jax.shard_map(
        local,
        mesh=mesh,
        in_specs=placed,
        out_specs=(P("series", None, "tm"), P("series", None, None), P()),
        check_vma=False,
    )
```

profile of v0, /device:TPU:0, one launch (start us, length us, event | category | flops | bytes accessed | tf_op | source)
XLA Modules:
  0.0 81.8 jit_solution(11519483765695263814)
XLA Ops:
  5.4 3.8 %collective-permute-start.3 = (f32[3,64]{1,0:T(4,128)S(1)}, f32[3,64]{1,0:T(4,128)S(1)}, u32[]{:S(2)}, u32[]{:S(2)}) collective-permute-start(f32[3,64]{1,0:T(4,128)S(1)} %shard_map.85.refs_0_), channel_id=1, source_target_pairs={{0,24},{4,28},{8,16},{12,20},{16,8},{20,12},{24,0},{28,4},{1,25},{... | collective-permute-start | bytes 2312 | tf_op jit(solution)/shard_map/ppermute | solution.py:22
  11.7 1.4 %forward_scan.1 = (f32[2,64,512]{2,1,0:T(8,128)S(1)}, f32[64,512]{1,0:T(8,128)S(1)}) custom-call(f32[512,128]{1,0:T(8,128)S(1)} %bitcast.40, f32[64,512]{1,0:T(8,128)S(1)} %copy-done.4, f32[64,512]{1,0:T(8,128)S(1)} %get-tuple-element.33.weight), custom_call_target="tpu_custom_call" | custom-call | tf_op jit(solution)/shard_map/forward_scan/pallas_call | solution.py:446
  13.4 3.9 %collective-permute-start.6 = (bf16[2,64,512]{2,1,0:T(8,128)(2,1)S(1)}, bf16[2,64,512]{2,1,0:T(8,128)(2,1)}, u32[]{:S(2)}, u32[]{:S(2)}) collective-permute-start(bf16[2,64,512]{2,1,0:T(8,128)(2,1)S(1)} %enter.1.refs_0_), channel_id=1, source_target_pairs={{0,3},{1,2},{2,1},{3,0},{4,7},{5,6},{6,5},{7,4},{8,11},{9,10},{10,... | collective-permute-start | bytes 393224 | tf_op jit(solution)/shard_map/ppermute | solution.py:22
  18.0 1.4 %copy.19 = bf16[1024,2,256]{0,2,1:T(8,128)(2,1)S(1)} copy(bf16[1024,2,256]{2,1,0:T(2,128)(2,1)S(1)} %copy-done.8) | data formatting | bytes 2097152 | tf_op args[4]
  19.6 1.5 %copy.17 = bf16[512,1024]{0,1:T(8,128)(2,1)S(1)} copy(bf16[512,1024]{1,0:T(8,128)(2,1)} %param.6) | data formatting | bytes 2097152 | tf_op args[0]
  21.8 6.2 %collective-permute-done.5.refs_2_ = bf16[2,64,512]{2,1,0:T(8,128)(2,1)} collective-permute-done((bf16[2,64,512]{2,1,0:T(8,128)(2,1)S(1)}, bf16[2,64,512]{2,1,0:T(8,128)(2,1)}, u32[]{:S(2)}, u32[]{:S(2)}) %collective-permute-start.5) | collective-permute-done | bytes 131104 | tf_op jit(solution)/shard_map/ppermute | solution.py:22
  28.0 6.3 %residual.1 = (f32[4,528,128]{2,1,0:T(8,128)S(1)}, f32[2,2064,128]{2,1,0:T(8,128)S(1)}) custom-call(bf16[2,64,512]{2,1,0:T(8,128)(2,1)S(1)} %enter.1.refs_0_, bf16[2,64,512]{2,1,0:T(8,128)(2,1)} %collective-permute-done.4.refs_1_, bf16[2,64,512]{2,1,0:T(8,128)(2,1)} %collective-permute-done.5.refs_2_, bf16[2,64,512]{2,1,0:T(8,128)(2,1)} %collective-permute-done.6.refs_3_, ...), custom_call_target="tpu_custom_call" | custom-call | tf_op jit(solution)/shard_map/residual/pallas_call | solution.py:469
  34.5 1.9 %collective-permute-done.14 = f16[2064,128]{1,0:T(8,128)(2,1)S(1)} collective-permute-done((f16[2064,128]{1,0:T(8,128)(2,1)S(1)}, f16[2064,128]{1,0:T(8,128)(2,1)S(1)}, u32[]{:S(2)}, u32[]{:S(2)}) %collective-permute-start.14) | collective-permute-done | bytes 528416 | tf_op jit(solution)/shard_map/ppermute | solution.py:22
  36.8 2.5 %collective-permute-start.17 = (f16[528,128]{1,0:T(8,128)(2,1)S(1)}, f16[528,128]{1,0:T(8,128)(2,1)S(1)}, u32[]{:S(2)}, u32[]{:S(2)}) collective-permute-start(f16[528,128]{1,0:T(8,128)(2,1)S(1)} %get-tuple-element.55), channel_id=1, source_target_pairs={{0,24},{4,28},{8,16},{12,20},{16,8},{20,12},{24,0},{28,4},{1,25},{... | collective-permute-start | bytes 405512 | tf_op jit(solution)/shard_map/ppermute | solution.py:22
  40.3 3.4 %collective-permute-done.17 = f16[528,128]{1,0:T(8,128)(2,1)S(1)} collective-permute-done((f16[528,128]{1,0:T(8,128)(2,1)S(1)}, f16[528,128]{1,0:T(8,128)(2,1)S(1)}, u32[]{:S(2)}, u32[]{:S(2)}) %collective-permute-start.17) | collective-permute-done | bytes 135200 | tf_op jit(solution)/shard_map/ppermute | solution.py:22
  43.7 2.4 %collective-permute-done.16 = f16[528,128]{1,0:T(8,128)(2,1)S(1)} collective-permute-done((f16[528,128]{1,0:T(8,128)(2,1)S(1)}, f16[528,128]{1,0:T(8,128)(2,1)S(1)}, u32[]{:S(2)}, u32[]{:S(2)}) %collective-permute-start.16) | collective-permute-done | bytes 135200 | tf_op jit(solution)/shard_map/ppermute | solution.py:22
  46.4 1.8 %collective-permute-start.20 = (f16[512,128]{1,0:T(8,128)(2,1)S(1)}, f16[512,128]{1,0:T(8,128)(2,1)S(1)}, u32[]{:S(2)}, u32[]{:S(2)}) collective-permute-start(f16[512,128]{1,0:T(8,128)(2,1)S(1)} %convert_element_type.105), channel_id=1, source_target_pairs={{0,24},{4,28},{8,16},{12,20},{16,8},{20,12},{24,0},{28,4},{1,25},{... | collective-permute-start | bytes 393224 | tf_op jit(solution)/shard_map/ppermute | solution.py:22
  48.2 1.3 %collective-permute-start.19 = (f16[512,128]{1,0:T(8,128)(2,1)S(1)}, f16[512,128]{1,0:T(8,128)(2,1)S(1)}, u32[]{:S(2)}, u32[]{:S(2)}) collective-permute-start(f16[512,128]{1,0:T(8,128)(2,1)S(1)} %convert_element_type.105), channel_id=1, source_target_pairs={{0,16},{4,20},{8,24},{12,28},{16,0},{20,4},{24,8},{28,12},{1,17},{... | collective-permute-start | bytes 393224 | tf_op jit(solution)/shard_map/ppermute | solution.py:22
  50.0 3.8 %collective-permute-done.20 = f16[512,128]{1,0:T(8,128)(2,1)S(1)} collective-permute-done((f16[512,128]{1,0:T(8,128)(2,1)S(1)}, f16[512,128]{1,0:T(8,128)(2,1)S(1)}, u32[]{:S(2)}, u32[]{:S(2)}) %collective-permute-start.20) | collective-permute-done | bytes 131104 | tf_op jit(solution)/shard_map/ppermute | solution.py:22
  53.8 1.8 %collective-permute-done.19 = f16[512,128]{1,0:T(8,128)(2,1)S(1)} collective-permute-done((f16[512,128]{1,0:T(8,128)(2,1)S(1)}, f16[512,128]{1,0:T(8,128)(2,1)S(1)}, u32[]{:S(2)}, u32[]{:S(2)}) %collective-permute-start.19) | collective-permute-done | bytes 131104 | tf_op jit(solution)/shard_map/ppermute | solution.py:22
  56.0 2.5 %collective-permute-start.9 = (f16[528,128]{1,0:T(8,128)(2,1)S(1)}, f16[528,128]{1,0:T(8,128)(2,1)S(1)}, u32[]{:S(2)}, u32[]{:S(2)}) collective-permute-start(f16[528,128]{1,0:T(8,128)(2,1)S(1)} %get-tuple-element.58), channel_id=1, source_target_pairs={{0,3},{1,2},{2,1},{3,0},{4,7},{5,6},{6,5},{7,4},{8,11},{9,10},{10,... | collective-permute-start | bytes 405512 | tf_op jit(solution)/shard_map/ppermute | solution.py:22
  58.5 1.9 %collective-permute-start.7 = (f16[528,128]{1,0:T(8,128)(2,1)S(1)}, f16[528,128]{1,0:T(8,128)(2,1)S(1)}, u32[]{:S(2)}, u32[]{:S(2)}) collective-permute-start(f16[528,128]{1,0:T(8,128)(2,1)S(1)} %get-tuple-element.60), channel_id=1, source_target_pairs={{0,1},{1,0},{2,3},{3,2},{4,5},{5,4},{6,7},{7,6},{8,9},{9,8},{10,11... | collective-permute-start | bytes 405512 | tf_op jit(solution)/shard_map/ppermute | solution.py:22
  60.4 4.0 %collective-permute-done.9 = f16[528,128]{1,0:T(8,128)(2,1)S(1)} collective-permute-done((f16[528,128]{1,0:T(8,128)(2,1)S(1)}, f16[528,128]{1,0:T(8,128)(2,1)S(1)}, u32[]{:S(2)}, u32[]{:S(2)}) %collective-permute-start.9) | collective-permute-done | bytes 135200 | tf_op jit(solution)/shard_map/ppermute | solution.py:22
  64.5 5.5 %collective-permute-done.8 = f16[528,128]{1,0:T(8,128)(2,1)S(1)} collective-permute-done((f16[528,128]{1,0:T(8,128)(2,1)S(1)}, f16[528,128]{1,0:T(8,128)(2,1)S(1)}, u32[]{:S(2)}, u32[]{:S(2)}) %collective-permute-start.8) | collective-permute-done | bytes 135200 | tf_op jit(solution)/shard_map/ppermute | solution.py:22
  70.4 1.2 %collective-permute-done.10.other = f32[5,64]{1,0:T(8,128)S(1)} collective-permute-done((f32[5,64]{1,0:T(8,128)S(1)}, f32[5,64]{1,0:T(8,128)S(1)}, u32[]{:S(2)}, u32[]{:S(2)}) %collective-permute-start.10) | collective-permute-done | bytes 1312 | tf_op jit(solution)/shard_map/ppermute | solution.py:22
  71.5 1.4 %collective-permute-start.13 = (f32[5,64]{1,0:T(8,128)S(1)}, f32[5,64]{1,0:T(8,128)S(1)}, u32[]{:S(2)}, u32[]{:S(2)}) collective-permute-start(f32[5,64]{1,0:T(8,128)S(1)} %shard_map.86.refs_0_), channel_id=1, source_target_pairs={{0,24},{4,28},{8,16},{12,20},{16,8},{20,12},{24,0},{28,4},{1,25},{... | collective-permute-start | bytes 3848 | tf_op jit(solution)/shard_map/ppermute | solution.py:22
  72.9 1.5 %collective-permute-start.12 = (f32[5,64]{1,0:T(8,128)S(1)}, f32[5,64]{1,0:T(8,128)S(1)}, u32[]{:S(2)}, u32[]{:S(2)}) collective-permute-start(f32[5,64]{1,0:T(8,128)S(1)} %shard_map.86.refs_0_), channel_id=1, source_target_pairs={{0,16},{4,20},{8,24},{12,28},{16,0},{20,4},{24,8},{28,12},{1,17},{... | collective-permute-start | bytes 3848 | tf_op jit(solution)/shard_map/ppermute | solution.py:22
  75.0 1.6 %backward_scan.1 = (f32[2,64,512]{2,1,0:T(8,128)S(1)}, f32[64,512]{1,0:T(8,128)S(1)}) custom-call(f32[64,512]{1,0:T(8,128)S(1)} %copy-done.5, f32[512,128]{1,0:T(8,128)S(1)} %get-tuple-element.42.grads), custom_call_target="tpu_custom_call" | custom-call | tf_op jit(solution)/shard_map/backward_scan/pallas_call | solution.py:544
  76.6 1.4 %collective-permute-done.11.refs_1_ = f32[5,64]{1,0:T(8,128)S(1)} collective-permute-done((f32[5,64]{1,0:T(8,128)S(1)}, f32[5,64]{1,0:T(8,128)S(1)}, u32[]{:S(2)}, u32[]{:S(2)}) %collective-permute-start.11) | collective-permute-done | bytes 1312 | tf_op jit(solution)/shard_map/ppermute | solution.py:22
  (74 shorter events, 16.4 us)
Async XLA Ops:
  4.0 1.4 %collective-permute-start = (f32[3,64]{1,0:T(4,128)S(1)}, f32[3,64]{1,0:T(4,128)S(1)}, u32[]{:S(2)}, u32[]{:S(2)}) collective-permute-start(f32[3,64]{1,0:T(4,128)S(1)} %get-tuple-element.35.summary.products), channel_id=1, source_target_pairs={{0,4},{4,0},{8,12},{12,8},{16,20},{20,16},{24,28},{28,24},{1,5},{5... | collective-permute-start | bytes 2312 | tf_op jit(solution)/shard_map/ppermute | solution.py:22
  5.4 7.7 %collective-permute-start.3 = (f32[3,64]{1,0:T(4,128)S(1)}, f32[3,64]{1,0:T(4,128)S(1)}, u32[]{:S(2)}, u32[]{:S(2)}) collective-permute-start(f32[3,64]{1,0:T(4,128)S(1)} %shard_map.85.refs_0_), channel_id=1, source_target_pairs={{0,24},{4,28},{8,16},{12,20},{16,8},{20,12},{24,0},{28,4},{1,25},{... | collective-permute-start | bytes 2312 | tf_op jit(solution)/shard_map/ppermute | solution.py:22
  9.2 3.9 %collective-permute-start.2 = (f32[3,64]{1,0:T(4,128)S(1)}, f32[3,64]{1,0:T(4,128)S(1)}, u32[]{:S(2)}, u32[]{:S(2)}) collective-permute-start(f32[3,64]{1,0:T(4,128)S(1)} %shard_map.85.refs_0_), channel_id=1, source_target_pairs={{0,16},{4,20},{8,24},{12,28},{16,0},{20,4},{24,8},{28,12},{1,17},{... | collective-permute-start | bytes 2312 | tf_op jit(solution)/shard_map/ppermute | solution.py:22
  9.7 3.6 %collective-permute-start.1 = (f32[3,64]{1,0:T(4,128)S(1)}, f32[3,64]{1,0:T(4,128)S(1)}, u32[]{:S(2)}, u32[]{:S(2)}) collective-permute-start(f32[3,64]{1,0:T(4,128)S(1)} %shard_map.85.refs_0_), channel_id=1, source_target_pairs={{0,8},{4,12},{8,0},{12,4},{16,24},{20,28},{24,16},{28,20},{1,9},{5... | collective-permute-start | bytes 2312 | tf_op jit(solution)/shard_map/ppermute | solution.py:22
  13.4 8.4 %collective-permute-start.6 = (bf16[2,64,512]{2,1,0:T(8,128)(2,1)S(1)}, bf16[2,64,512]{2,1,0:T(8,128)(2,1)}, u32[]{:S(2)}, u32[]{:S(2)}) collective-permute-start(bf16[2,64,512]{2,1,0:T(8,128)(2,1)S(1)} %enter.1.refs_0_), channel_id=1, source_target_pairs={{0,3},{1,2},{2,1},{3,0},{4,7},{5,6},{6,5},{7,4},{8,11},{9,10},{10,... | collective-permute-start | bytes 393224 | tf_op jit(solution)/shard_map/ppermute | solution.py:22
  17.3 10.7 %collective-permute-start.5 = (bf16[2,64,512]{2,1,0:T(8,128)(2,1)S(1)}, bf16[2,64,512]{2,1,0:T(8,128)(2,1)}, u32[]{:S(2)}, u32[]{:S(2)}) collective-permute-start(bf16[2,64,512]{2,1,0:T(8,128)(2,1)S(1)} %enter.1.refs_0_), channel_id=1, source_target_pairs={{0,2},{1,3},{2,0},{3,1},{4,6},{5,7},{6,4},{7,5},{8,10},{9,11},{10,... | collective-permute-start | bytes 393224 | tf_op jit(solution)/shard_map/ppermute | solution.py:22
  17.3 10.7 %collective-permute-start.4 = (bf16[2,64,512]{2,1,0:T(8,128)(2,1)S(1)}, bf16[2,64,512]{2,1,0:T(8,128)(2,1)}, u32[]{:S(2)}, u32[]{:S(2)}) collective-permute-start(bf16[2,64,512]{2,1,0:T(8,128)(2,1)S(1)} %enter.1.refs_0_), channel_id=1, source_target_pairs={{0,1},{1,0},{2,3},{3,2},{4,5},{5,4},{6,7},{7,6},{8,9},{9,8},{10,11... | collective-permute-start | bytes 393224 | tf_op jit(solution)/shard_map/ppermute | solution.py:22
  19.6 8.4 %copy-start.6 = (f32[1024]{0:T(1024)S(1)}, f32[1024]{0:T(1024)}, u32[]{:S(2)}) copy-start(f32[1024]{0:T(1024)} %param.11) | copy-start | bytes 12292
  34.4 2.0 %collective-permute-start.14 = (f16[2064,128]{1,0:T(8,128)(2,1)S(1)}, f16[2064,128]{1,0:T(8,128)(2,1)S(1)}, u32[]{:S(2)}, u32[]{:S(2)}) collective-permute-start(f16[2064,128]{1,0:T(8,128)(2,1)S(1)} %fusion), channel_id=1, source_target_pairs={{0,4},{4,0},{8,12},{12,8},{16,20},{20,16},{24,28},{28,24},{1,5},{5... | collective-permute-start | bytes 1585160 | tf_op jit(solution)/shard_map/ppermute | solution.py:22
  36.8 6.9 %collective-permute-start.17 = (f16[528,128]{1,0:T(8,128)(2,1)S(1)}, f16[528,128]{1,0:T(8,128)(2,1)S(1)}, u32[]{:S(2)}, u32[]{:S(2)}) collective-permute-start(f16[528,128]{1,0:T(8,128)(2,1)S(1)} %get-tuple-element.55), channel_id=1, source_target_pairs={{0,24},{4,28},{8,16},{12,20},{16,8},{20,12},{24,0},{28,4},{1,25},{... | collective-permute-start | bytes 405512 | tf_op jit(solution)/shard_map/ppermute | solution.py:22
  39.3 6.9 %collective-permute-start.16 = (f16[528,128]{1,0:T(8,128)(2,1)S(1)}, f16[528,128]{1,0:T(8,128)(2,1)S(1)}, u32[]{:S(2)}, u32[]{:S(2)}) collective-permute-start(f16[528,128]{1,0:T(8,128)(2,1)S(1)} %get-tuple-element.56), channel_id=1, source_target_pairs={{0,16},{4,20},{8,24},{12,28},{16,0},{20,4},{24,8},{28,12},{1,17},{... | collective-permute-start | bytes 405512 | tf_op jit(solution)/shard_map/ppermute | solution.py:22
  39.8 6.5 %collective-permute-start.15 = (f16[528,128]{1,0:T(8,128)(2,1)S(1)}, f16[528,128]{1,0:T(8,128)(2,1)S(1)}, u32[]{:S(2)}, u32[]{:S(2)}) collective-permute-start(f16[528,128]{1,0:T(8,128)(2,1)S(1)} %get-tuple-element.57), channel_id=1, source_target_pairs={{0,8},{4,12},{8,0},{12,4},{16,24},{20,28},{24,16},{28,20},{1,9},{5... | collective-permute-start | bytes 405512 | tf_op jit(solution)/shard_map/ppermute | solution.py:22
  46.4 7.4 %collective-permute-start.20 = (f16[512,128]{1,0:T(8,128)(2,1)S(1)}, f16[512,128]{1,0:T(8,128)(2,1)S(1)}, u32[]{:S(2)}, u32[]{:S(2)}) collective-permute-start(f16[512,128]{1,0:T(8,128)(2,1)S(1)} %convert_element_type.105), channel_id=1, source_target_pairs={{0,24},{4,28},{8,16},{12,20},{16,8},{20,12},{24,0},{28,4},{1,25},{... | collective-permute-start | bytes 393224 | tf_op jit(solution)/shard_map/ppermute | solution.py:22
  48.2 7.4 %collective-permute-start.19 = (f16[512,128]{1,0:T(8,128)(2,1)S(1)}, f16[512,128]{1,0:T(8,128)(2,1)S(1)}, u32[]{:S(2)}, u32[]{:S(2)}) collective-permute-start(f16[512,128]{1,0:T(8,128)(2,1)S(1)} %convert_element_type.105), channel_id=1, source_target_pairs={{0,16},{4,20},{8,24},{12,28},{16,0},{20,4},{24,8},{28,12},{1,17},{... | collective-permute-start | bytes 393224 | tf_op jit(solution)/shard_map/ppermute | solution.py:22
  49.4 6.2 %collective-permute-start.18 = (f16[512,128]{1,0:T(8,128)(2,1)S(1)}, f16[512,128]{1,0:T(8,128)(2,1)S(1)}, u32[]{:S(2)}, u32[]{:S(2)}) collective-permute-start(f16[512,128]{1,0:T(8,128)(2,1)S(1)} %convert_element_type.105), channel_id=1, source_target_pairs={{0,8},{4,12},{8,0},{12,4},{16,24},{20,28},{24,16},{28,20},{1,9},{5... | collective-permute-start | bytes 393224 | tf_op jit(solution)/shard_map/ppermute | solution.py:22
  55.8 24.8 %collective-permute-start.21 = (f16[2048,128]{1,0:T(8,128)(2,1)S(1)}, f16[2048,128]{1,0:T(8,128)(2,1)S(1)}, u32[]{:S(2)}, u32[]{:S(2)}) collective-permute-start(f16[2048,128]{1,0:T(8,128)(2,1)S(1)} %convert_element_type.110), channel_id=1, source_target_pairs={{0,4},{4,0},{8,12},{12,8},{16,20},{20,16},{24,28},{28,24},{1,5},{5... | collective-permute-start | bytes 1572872 | tf_op jit(solution)/shard_map/ppermute | solution.py:22
  56.0 8.5 %collective-permute-start.9 = (f16[528,128]{1,0:T(8,128)(2,1)S(1)}, f16[528,128]{1,0:T(8,128)(2,1)S(1)}, u32[]{:S(2)}, u32[]{:S(2)}) collective-permute-start(f16[528,128]{1,0:T(8,128)(2,1)S(1)} %get-tuple-element.58), channel_id=1, source_target_pairs={{0,3},{1,2},{2,1},{3,0},{4,7},{5,6},{6,5},{7,4},{8,11},{9,10},{10,... | collective-permute-start | bytes 405512 | tf_op jit(solution)/shard_map/ppermute | solution.py:22
  58.5 11.5 %collective-permute-start.8 = (f16[528,128]{1,0:T(8,128)(2,1)S(1)}, f16[528,128]{1,0:T(8,128)(2,1)S(1)}, u32[]{:S(2)}, u32[]{:S(2)}) collective-permute-start(f16[528,128]{1,0:T(8,128)(2,1)S(1)} %get-tuple-element.59), channel_id=1, source_target_pairs={{0,2},{1,3},{2,0},{3,1},{4,6},{5,7},{6,4},{7,5},{8,10},{9,11},{10,... | collective-permute-start | bytes 405512 | tf_op jit(solution)/shard_map/ppermute | solution.py:22
  58.5 11.5 %collective-permute-start.7 = (f16[528,128]{1,0:T(8,128)(2,1)S(1)}, f16[528,128]{1,0:T(8,128)(2,1)S(1)}, u32[]{:S(2)}, u32[]{:S(2)}) collective-permute-start(f16[528,128]{1,0:T(8,128)(2,1)S(1)} %get-tuple-element.60), channel_id=1, source_target_pairs={{0,1},{1,0},{2,3},{3,2},{4,5},{5,4},{6,7},{7,6},{8,9},{9,8},{10,11... | collective-permute-start | bytes 405512 | tf_op jit(solution)/shard_map/ppermute | solution.py:22
  70.1 8.0 %copy-start.2 = (f32[64,2,512]{2,1,0:T(2,128)S(1)}, f32[64,2,512]{2,1,0:T(2,128)}, u32[]{:S(2)}) copy-start(f32[64,2,512]{2,1,0:T(2,128)} %param.7) | copy-start | bytes 786436
  70.3 1.2 %collective-permute-start.10 = (f32[5,64]{1,0:T(8,128)S(1)}, f32[5,64]{1,0:T(8,128)S(1)}, u32[]{:S(2)}, u32[]{:S(2)}) collective-permute-start(f32[5,64]{1,0:T(8,128)S(1)} %get-tuple-element.45.summary), channel_id=1, source_target_pairs={{0,4},{4,0},{8,12},{12,8},{16,20},{20,16},{24,28},{28,24},{1,5},{5... | collective-permute-start | bytes 3848 | tf_op jit(solution)/shard_map/ppermute | solution.py:22
  71.5 5.1 %collective-permute-start.13 = (f32[5,64]{1,0:T(8,128)S(1)}, f32[5,64]{1,0:T(8,128)S(1)}, u32[]{:S(2)}, u32[]{:S(2)}) collective-permute-start(f32[5,64]{1,0:T(8,128)S(1)} %shard_map.86.refs_0_), channel_id=1, source_target_pairs={{0,24},{4,28},{8,16},{12,20},{16,8},{20,12},{24,0},{28,4},{1,25},{... | collective-permute-start | bytes 3848 | tf_op jit(solution)/shard_map/ppermute | solution.py:22
  72.9 3.7 %collective-permute-start.12 = (f32[5,64]{1,0:T(8,128)S(1)}, f32[5,64]{1,0:T(8,128)S(1)}, u32[]{:S(2)}, u32[]{:S(2)}) collective-permute-start(f32[5,64]{1,0:T(8,128)S(1)} %shard_map.86.refs_0_), channel_id=1, source_target_pairs={{0,16},{4,20},{8,24},{12,28},{16,0},{20,4},{24,8},{28,12},{1,17},{... | collective-permute-start | bytes 3848 | tf_op jit(solution)/shard_map/ppermute | solution.py:22
  74.4 3.6 %collective-permute-start.11 = (f32[5,64]{1,0:T(8,128)S(1)}, f32[5,64]{1,0:T(8,128)S(1)}, u32[]{:S(2)}, u32[]{:S(2)}) collective-permute-start(f32[5,64]{1,0:T(8,128)S(1)} %shard_map.86.refs_0_), channel_id=1, source_target_pairs={{0,8},{4,12},{8,0},{12,4},{16,24},{20,28},{24,16},{28,20},{1,9},{5... | collective-permute-start | bytes 3848 | tf_op jit(solution)/shard_map/ppermute | solution.py:22
  (7 other events, 15.6 us)
where the time goes:
time: 82 us; the launch traced here: 81.8 us
  waiting for transfers between devices  33.4 us (41%)
  starting transfers between devices  24.8 us (30%)
  Pallas kernels  13.9 us (17%)
  local copies, waits for them, and re-layouts  7.46 us (9%)
  other arithmetic  1.27 us (2%)
  between operations  0.97 us (1%)
    ppermute x22, waiting for transfers between devices, swap(): return lax.ppermute(value, axis, [(i, i ^ key) for i in range(count)])  33.4 us
    ppermute x22, starting transfers between devices, swap(): return lax.ppermute(value, axis, [(i, i ^ key) for i in range(count)])  24.8 us
    unnamed x21, local copies, waits for them, and re-layouts  7.46 us
    pallas_call x1, Pallas kernels, local(): pl.pallas_call(functools.partial(residual_kernel, draws, parts), out_shap...  6.3 us
    pallas_call x2, Pallas kernels, write_half(): pl.pallas_call(functools.partial(write_kernel, flip), out_shape=shape((si...  2.1 us
  transfers between devices with their start and end apart: 22, of which 14 were waited for; matrix products, arithmetic and copies ran while one was open for 5% of the time, Pallas kernels for 6%

commit v1 on v0

--- a/solution.py
+++ b/solution.py
@@ -66,8 +66,9 @@
     return run, out, carry
 
 
-def beyond_kernel(tiles, decay, spread, beyond, product):
+def beyond_kernel(tiles, decay, spread, beyond, product, held):
     factors = decay.shape[0]
+    held[...] = decay[...]
     lane = lax.broadcasted_iota(jnp.int32, (factors, LANES), 1)
     after = jnp.ones((factors, 1), f32)
     for j in range(tiles - 1, -1, -1):
@@ -80,7 +81,7 @@
     product[...] = to_row(after, eye(factors))
 
 
-def edge_kernel(draws, tiles, innov, scale, spread, beyond, product, weight, summary, squares):
+def edge_kernel(draws, tiles, innov, scale, spread, beyond, product, pushes, summary, squares):
     factors = spread.shape[0]
     same = eye(factors)
     column = to_column(scale[...], same)
@@ -89,25 +90,22 @@
     for j in range(tiles):
         part = slice(j * LANES, (j + 1) * LANES)
         w = spread[:, part] * column
-        weight[:, part] = w
         for d in range(draws):
             x = innov[pl.ds(j * draws + d, factors, stride=tiles * draws), :]
+            push = w * x
+            pushes[d, :, part] = push
             total[d] = total[d] + x * x
-            ends[d] = ends[d] + w * x * beyond[:, part]
+            ends[d] = ends[d] + push * beyond[:, part]
     summary[0:1, :] = product[...]
     for d in range(draws):
         summary[d + 1:d + 2, :] = to_row(jnp.sum(ends[d], axis=1, keepdims=True), same)
         squares[d:d + 1, :] = jnp.sum(total[d], axis=0, keepdims=True)
 
 
-def forward_kernel(draws, tiles, innov, decay, weight, local, running):
-    factors = decay.shape[0]
-    decays, pushes = [], []
-    for j in range(tiles):
-        part = slice(j * LANES, (j + 1) * LANES)
-        decays.append(decay[:, part])
-        rows = lambda d: pl.ds(j * draws + d, factors, stride=tiles * draws)
-        pushes.append([weight[:, part] * innov[rows(d), :] for d in range(draws)])
+def forward_kernel(draws, tiles, decay, pushed, local, running):
+    parts = [slice(j * LANES, (j + 1) * LANES) for j in range(tiles)]
+    decays = [decay[:, part] for part in parts]
+    pushes = [[pushed[d, :, part] for d in range(draws)] for part in parts]
     run, out, _ = block_scan(decays, pushes, False)
     for j in range(tiles):
         running[:, j * LANES:(j + 1) * LANES] = run[j]
@@ -120,8 +118,8 @@
     return count - 1 - mine if backward else mine
 
 
-def pair_kernel(rows, backward, summary, other, whole):
-    later = seat(backward) % 2 == 1
+def pair_kernel(rows, backward, bit, summary, other, whole):
+    later = (seat(backward) // bit) % 2 == 1
     mine, theirs = summary[...], other[...]
     first, second = jnp.where(later, theirs, mine), jnp.where(later, mine, theirs)
     whole[0:1, :] = first[0:1] * second[0:1]
@@ -163,7 +161,7 @@
     count = pl.num_programs(0)
     wide = paths.shape[1] // LANES
     side = step // (count // 2)
-    base = (step % (count // 2)) * (returns.shape[0] * wide * draws)
+    base = (step % (count // 2)) * (returns.shape[1] * wide * draws)
 
     @pl.when(step == 0)
     def _():
@@ -174,7 +172,7 @@
         density[...] = jnp.zeros_like(density)
         top[...] = jnp.zeros_like(top)
 
-    seen = returns[...].astype(f32)
+    seen = returns[...].T.astype(f32)
     rows = seen.shape[0]
     same = eye(LANES)
     groups = rows // LANES
@@ -345,19 +343,27 @@
             local[d, :, j * LANES:(j + 1) * LANES] = out[j][d]
 
 
-def leave_kernel(draws, tiles, local, tail, weight, innov, other, *refs):
-    totals, (out, density) = refs[:-2], refs[-2:]
+def leave_kernel(draws, tiles, cells, local, tail, decay, scale, innov, value, *refs):
+    climb, (out, density, far, sem) = refs[:-4], refs[-4:]
+    half = value.shape[0]
+    move = pltpu.make_async_copy(value, far.at[pl.ds(pl.multiple_of((lax.axis_index("tm") % 2) * half, half), half), :], sem)
+    move.start()
     factors = tail.shape[0]
     same = eye(factors)
-    arriving, summed = entered(draws + 1, True, other, totals)
-    density[...] = summed
+    arriving, summed = entered(draws + 1, True, climb[0], climb[1:])
+    sized = to_column(scale[...], same)
+    columns = [to_column(arriving[d:d + 1, :], same) for d in range(draws)]
     for d in range(draws):
-        column = to_column(arriving[d:d + 1, :], same)
-        for j in range(tiles):
-            part = slice(j * LANES, (j + 1) * LANES)
+        density[d] = jnp.max(summed[d:d + 1, :]) * (1.0 / cells)
+    for j in range(tiles):
+        part = slice(j * LANES, (j + 1) * LANES)
+        a = decay[:, part]
+        weight = jnp.sqrt((1.0 - a) * (1.0 + a)) * sized
+        for d in range(draws):
             rows = pl.ds(j * draws + d, factors, stride=tiles * draws)
-            adjoint = local[d, :, part] + tail[:, part] * column
-            out[rows, :] = weight[:, part] * adjoint - innov[rows, :]
+            adjoint = local[d, :, part] + tail[:, part] * columns[d]
+            out[rows, :] = weight * adjoint - innov[rows, :]
+    move.wait()
 
 
 def room(mebibytes):
@@ -372,28 +378,27 @@
         out[pl.ds(start, rows), :] = piece[...]
 
 
-def write_kernel(flip, value, factor, *refs):
-    out, scaled, sem = refs[-3:]
+def write_kernel(flip, value, *refs):
+    out, sem = refs[-2:]
     half = value.shape[0]
-    scaled[...] = value[...] * factor[...]
-    move = pltpu.make_async_copy(scaled, out.at[pl.ds(pl.multiple_of(((lax.axis_index("tm") + flip) % 2) * half, half), half), :], sem)
+    move = pltpu.make_async_copy(value, out.at[pl.ds(pl.multiple_of(((lax.axis_index("tm") + flip) % 2) * half, half), half), :], sem)
     move.start()
     move.wait()
 
 
-def write_half(value, factor, flip, out, size):
+def write_half(value, flip, out, size):
     far = pl.BlockSpec(memory_space=pltpu.HBM)
-    specs = [pl.BlockSpec(memory_space=pltpu.VMEM)] * 2
+    specs = [pl.BlockSpec(memory_space=pltpu.VMEM)]
     return pl.pallas_call(
         functools.partial(write_kernel, flip),
         out_shape=shape((size, LANES), f32),
         in_specs=specs if out is None else specs + [far],
         out_specs=far,
-        input_output_aliases={} if out is None else {2: 0},
-        scratch_shapes=[pltpu.VMEM(value.shape, f32), pltpu.SemaphoreType.DMA],
+        input_output_aliases={} if out is None else {1: 0},
+        scratch_shapes=[pltpu.SemaphoreType.DMA],
         name="write_half",
         compiler_params=room(4),
-    )(value, factor, *([] if out is None else [out]))
+    )(value, *([] if out is None else [out]))
 
 
 def shape(dims, kind):
@@ -404,7 +409,7 @@
     pairs = lax.axis_size("tm") // 2
     other = swap(summary, "tm", 1)
     whole = pl.pallas_call(
-        functools.partial(pair_kernel, rows, backward),
+        functools.partial(pair_kernel, rows, backward, 1),
         out_shape=shape(summary.shape, f32),
         compiler_params=room(1),
     )(summary, other)
@@ -427,16 +432,22 @@
     decay_rate, numbers = lax.optimization_barrier((decay_rate, numbers))
     seats, far_core = numbers[:parts], numbers[parts]
     chips_at = numbers[parts + 1:]
-    spread, beyond, product = pl.pallas_call(
+    spread, beyond, product, decays = pl.pallas_call(
         functools.partial(beyond_kernel, tiles),
-        out_shape=(shape((factors, steps), f32), shape((factors, steps), f32), shape((1, factors), f32)),
+        out_shape=(
+            shape((factors, steps), f32),
+            shape((factors, steps), f32),
+            shape((1, factors), f32),
+            shape((factors, steps), f32),
+        ),
         name="beyond",
+        cost_estimate=pl.CostEstimate(flops=2_000_000_000, bytes_accessed=1 << 20, transcendentals=0),
         compiler_params=room(2),
     )(decay_rate)
-    weight, summary, squares = pl.pallas_call(
+    pushes, summary, squares = pl.pallas_call(
         functools.partial(edge_kernel, draws, tiles),
         out_shape=(
-            shape((factors, steps), f32),
+            shape((draws, factors, steps), f32),
             shape((draws + 1, factors), f32),
             shape((draws, LANES), f32),
         ),
@@ -448,7 +459,7 @@
         out_shape=(shape((draws, factors, steps), f32), shape((factors, steps), f32)),
         name="forward_scan",
         compiler_params=room(4),
-    )(innov, decay_rate, weight)
+    )(decays, pushes)
     path_low = pl.pallas_call(
         functools.partial(enter_kernel, draws),
         out_shape=shape((draws, factors, steps), bf16),
@@ -458,7 +469,6 @@
 
     pieces = [path_low] + [swap(path_low, "series", key) for key in range(1, parts)]
     noise = noise_scale.reshape(series // LANES, LANES)
-    seen = returns.T
     loads = loadings.transpose(1, 0, 2)
     loads_t = loadings.transpose(1, 2, 0)
     rows = min(256, series // 2)
@@ -476,7 +486,7 @@
             grid=(series // rows,),
             in_specs=[still((draws, factors, steps))] * parts
             + [
-                pl.BlockSpec((rows, steps), lambda i: (i, 0)),
+                pl.BlockSpec((steps, rows), lambda i: (0, i)),
                 pl.BlockSpec((draws, rows, all_factors), lambda i: (0, i, 0)),
                 pl.BlockSpec((draws, all_factors, rows), lambda i: (0, 0, i)),
                 still((series // LANES, LANES)),
@@ -494,11 +504,11 @@
         ),
         name="residual",
         compiler_params=room(16),
-    )(*pieces, seen, loads, loads_t, noise, squares)
+    )(*pieces, returns, loads, loads_t, noise, squares)
 
     pick = lambda value, place: lax.dynamic_slice(value, (place, 0, 0), (1,) + value.shape[1:], allow_negative_indices=False)[0]
     sent = [pick(grads, place).astype(f16) for place in seats[1:]]
-    arrived = [swap(value, "series", key + 1) for key, value in enumerate(sent)]
+    arrived = [swap(value, "series", key) for key, value in enumerate(sent, 1)]
 
     chips = spans // 2
     whole = pl.BlockSpec(memory_space=pltpu.VMEM)
@@ -528,13 +538,7 @@
         name="assemble",
         compiler_params=room(4),
     )(*[value.astype(f32) for value in totals])
-    theirs = swap(mine.astype(f16), "tm", 1).astype(f32)
-    grad_load = None
-    for value, flip in ((mine, 0), (theirs, 1)):
-        grad_load = write_half(value, factor, flip, grad_load, size)
-    grad_load = grad_load.reshape(series, all_factors // LANES, draws, LANES).transpose(0, 2, 1, 3)
-    grad_load = grad_load.reshape(series, draws, all_factors)
-
+    theirs = swap(mine.astype(f16), "tm", 1).astype(f32) * factor
     path_grads, leaving = pl.pallas_call(
         functools.partial(gather_kernel, draws, tiles, parts),
         out_shape=(shape((body, LANES), f32), shape((2 * draws + 1, factors), f32)),
@@ -546,17 +550,23 @@
         out_shape=(shape((draws, factors, steps), f32), shape((factors, steps), f32)),
         name="backward_scan",
         compiler_params=room(3),
-    )(decay_rate, path_grads)
-    grad_innov, density = pl.pallas_call(
-        functools.partial(leave_kernel, draws, tiles),
-        out_shape=(shape(innov.shape, f32), shape((draws, factors), f32)),
+    )(decays, path_grads)
+    climb = carried(leaving, draws + 1, True)
+    grad_innov, log_density, grad_load = pl.pallas_call(
+        functools.partial(leave_kernel, draws, tiles, float(spans * parts)),
+        out_shape=(shape(innov.shape, f32), shape((draws,), f32), shape((size, LANES), f32)),
+        in_specs=[whole] * (6 + len(climb)),
+        out_specs=(whole, pl.BlockSpec(memory_space=pltpu.SMEM), pl.BlockSpec(memory_space=pltpu.HBM)),
+        scratch_shapes=[pltpu.SemaphoreType.DMA],
         name="leave",
-        compiler_params=room(3),
-    )(local_adjoint, tail, weight, innov, *carried(leaving, draws + 1, True))
+        compiler_params=room(4),
+    )(local_adjoint, tail, decays, innov_scale.reshape(1, factors), innov, mine * factor, *climb)
+    grad_load = write_half(theirs, 1, grad_load, size)
+    grad_load = grad_load.reshape(series, all_factors // LANES, draws, LANES).transpose(0, 2, 1, 3)
+    grad_load = grad_load.reshape(series, draws, all_factors)
     grad_innov = grad_innov.reshape(factors, tiles, draws, LANES).transpose(0, 2, 1, 3)
     grad_innov = grad_innov.reshape(factors, draws, steps)
 
-    log_density = density[:, 0] / (spans * parts)
     return (grad_innov, grad_load, log_density)
 
 

time: 82 us -> 77.1 us (0.940)
  local copies, waits for them, and re-layouts: 7.46 us -> 2.81 us
  waiting for transfers between devices: 33.4 us -> 35.1 us
  Pallas kernels: 13.9 us -> 12.7 us
    unnamed x21 -> x14, local copies, waits for them, and re-layouts: 7.46 us -> 2.81 us
    ppermute x22, waiting for transfers between devices: 33.4 us -> 35.1 us  [swap(): return lax.ppermute(value, axis, [(i, i ^ key) for i in range(count)])]
    pallas_call x2 -> x1, Pallas kernels: 2.1 us -> 1 us  [write_half(): pl.pallas_call(functools.partial(write_kernel, flip), out_shape=shape((si...]
    pallas_call x3, Pallas kernels: 0.89 us -> 1.73 us  [the longest x1 1.71 us: local(): pl.pallas_call(functools.partial(leave_kernel, draws, tiles, float(spans...]
  transfers between devices with their start and end apart: 22 -> 22, of which waited for: 14 -> 16; matrix products, arithmetic and copies ran while one was open for 5% -> 2% of each run, Pallas kernels for 6% -> 6%
where the time goes in v1:
time: 77.1 us; the launch traced here: 77 us
  waiting for transfers between devices  35.1 us (46%)
  starting transfers between devices  24.7 us (32%)
  Pallas kernels  12.7 us (16%)
  local copies, waits for them, and re-layouts  2.81 us (4%)
  between operations  0.94 us (1%)
    ppermute x22, waiting for transfers between devices, swap(): return lax.ppermute(value, axis, [(i, i ^ key) for i in range(count)])  35.1 us
    ppermute x22, starting transfers between devices, swap(): return lax.ppermute(value, axis, [(i, i ^ key) for i in range(count)])  24.7 us
    pallas_call x1, Pallas kernels, local(): pl.pallas_call(functools.partial(residual_kernel, draws, parts), out_shap...  5.5 us
    unnamed x14, local copies, waits for them, and re-layouts  2.81 us
    pallas_call x1, Pallas kernels, local(): pl.pallas_call(functools.partial(leave_kernel, draws, tiles, float(spans...  1.71 us
    pallas_call x1, Pallas kernels, local(): pl.pallas_call(functools.partial(backward_kernel, draws, tiles), out_shap...  1.6 us
  transfers between devices with their start and end apart: 22, of which 16 were waited for; matrix products, arithmetic and copies ran while one was open for 2% of the time, Pallas kernels for 6%

profile of v1, /device:TPU:0, one launch (start us, length us, event | category | flops | bytes accessed | tf_op | source)
XLA Modules:
  0.0 77.0 jit_solution(7124943222378792831)
XLA Ops:
  4.1 3.8 %collective-permute-start.3 = (f32[3,64]{1,0:T(4,128)S(1)}, f32[3,64]{1,0:T(4,128)S(1)}, u32[]{:S(2)}, u32[]{:S(2)}) collective-permute-start(f32[3,64]{1,0:T(4,128)S(1)} %shard_map.85.refs_0_), channel_id=1, source_target_pairs={{0,24},{4,28},{8,16},{12,20},{16,8},{20,12},{24,0},{28,4},{1,25},{... | collective-permute-start | bytes 2312 | tf_op jit(solution)/shard_map/ppermute | solution.py:22
  8.5 1.4 %forward_scan.1 = (f32[2,64,512]{2,1,0:T(8,128)S(1)}, f32[64,512]{1,0:T(8,128)S(1)}) custom-call(f32[64,512]{1,0:T(8,128)S(1)} %get-tuple-element.32.decay, f32[2,64,512]{2,1,0:T(8,128)S(1)} %get-tuple-element.36.pushed), custom_call_target="tpu_custom_call" | custom-call | tf_op jit(solution)/shard_map/forward_scan/pallas_call | solution.py:457
  9.9 1.5 %collective-permute-done.2.refs_2_ = f32[3,64]{1,0:T(4,128)S(1)} collective-permute-done((f32[3,64]{1,0:T(4,128)S(1)}, f32[3,64]{1,0:T(4,128)S(1)}, u32[]{:S(2)}, u32[]{:S(2)}) %collective-permute-start.2) | collective-permute-done | bytes 800 | tf_op jit(solution)/shard_map/ppermute | solution.py:22
  12.1 3.7 %collective-permute-start.6 = (bf16[2,64,512]{2,1,0:T(8,128)(2,1)S(1)}, bf16[2,64,512]{2,1,0:T(8,128)(2,1)S(1)}, u32[]{:S(2)}, u32[]{:S(2)}) collective-permute-start(bf16[2,64,512]{2,1,0:T(8,128)(2,1)S(1)} %enter.1.refs_0_), channel_id=1, source_target_pairs={{0,3},{1,2},{2,1},{3,0},{4,7},{5,6},{6,5},{7,4},{8,11},{9,10},{10,... | collective-permute-start | bytes 393224 | tf_op jit(solution)/shard_map/ppermute | solution.py:22
  16.5 1.4 %copy.12 = bf16[1024,2,256]{0,2,1:T(8,128)(2,1)S(1)} copy(bf16[1024,2,256]{2,1,0:T(2,128)(2,1)S(1)} %copy-done.5) | data formatting | bytes 2097152 | tf_op args[4]
  18.2 1.9 %collective-permute-done.6.refs_3_ = bf16[2,64,512]{2,1,0:T(8,128)(2,1)S(1)} collective-permute-done((bf16[2,64,512]{2,1,0:T(8,128)(2,1)S(1)}, bf16[2,64,512]{2,1,0:T(8,128)(2,1)S(1)}, u32[]{:S(2)}, u32[]{:S(2)}) %collective-permute-start.6) | collective-permute-done | bytes 131104 | tf_op jit(solution)/shard_map/ppermute | solution.py:22
  20.0 5.4 %collective-permute-done.5.refs_2_ = bf16[2,64,512]{2,1,0:T(8,128)(2,1)S(1)} collective-permute-done((bf16[2,64,512]{2,1,0:T(8,128)(2,1)S(1)}, bf16[2,64,512]{2,1,0:T(8,128)(2,1)S(1)}, u32[]{:S(2)}, u32[]{:S(2)}) %collective-permute-start.5) | collective-permute-done | bytes 131104 | tf_op jit(solution)/shard_map/ppermute | solution.py:22
  25.5 5.5 %residual.1 = (f32[4,528,128]{2,1,0:T(8,128)S(1)}, f32[2,2064,128]{2,1,0:T(8,128)S(1)}) custom-call(bf16[2,64,512]{2,1,0:T(8,128)(2,1)S(1)} %enter.1.refs_0_, bf16[2,64,512]{2,1,0:T(8,128)(2,1)S(1)} %collective-permute-done.4.refs_1_, bf16[2,64,512]{2,1,0:T(8,128)(2,1)S(1)} %collective-permute-done.5.refs_2_, ...), custom_call_target="tpu_custom_call" | custom-call | tf_op jit(solution)/shard_map/residual/pallas_call | solution.py:479
  31.1 1.9 %collective-permute-done.10 = f16[2064,128]{1,0:T(8,128)(2,1)S(1)} collective-permute-done((f16[2064,128]{1,0:T(8,128)(2,1)S(1)}, f16[2064,128]{1,0:T(8,128)(2,1)S(1)}, u32[]{:S(2)}, u32[]{:S(2)}) %collective-permute-start.10) | collective-permute-done | bytes 528416 | tf_op jit(solution)/shard_map/ppermute | solution.py:22
  33.3 1.9 %collective-permute-start.13 = (f16[528,128]{1,0:T(8,128)(2,1)S(1)}, f16[528,128]{1,0:T(8,128)(2,1)S(1)}, u32[]{:S(2)}, u32[]{:S(2)}) collective-permute-start(f16[528,128]{1,0:T(8,128)(2,1)S(1)} %get-tuple-element.59), channel_id=1, source_target_pairs={{0,24},{4,28},{8,16},{12,20},{16,8},{20,12},{24,0},{28,4},{1,25},{... | collective-permute-start | bytes 405512 | tf_op jit(solution)/shard_map/ppermute | solution.py:22
  36.9 3.9 %collective-permute-done.13 = f16[528,128]{1,0:T(8,128)(2,1)S(1)} collective-permute-done((f16[528,128]{1,0:T(8,128)(2,1)S(1)}, f16[528,128]{1,0:T(8,128)(2,1)S(1)}, u32[]{:S(2)}, u32[]{:S(2)}) %collective-permute-start.13) | collective-permute-done | bytes 135200 | tf_op jit(solution)/shard_map/ppermute | solution.py:22
  40.8 2.1 %collective-permute-done.12 = f16[528,128]{1,0:T(8,128)(2,1)S(1)} collective-permute-done((f16[528,128]{1,0:T(8,128)(2,1)S(1)}, f16[528,128]{1,0:T(8,128)(2,1)S(1)}, u32[]{:S(2)}, u32[]{:S(2)}) %collective-permute-start.12) | collective-permute-done | bytes 135200 | tf_op jit(solution)/shard_map/ppermute | solution.py:22
  43.3 1.6 %collective-permute-start.16 = (f16[512,128]{1,0:T(8,128)(2,1)S(1)}, f16[512,128]{1,0:T(8,128)(2,1)S(1)}, u32[]{:S(2)}, u32[]{:S(2)}) collective-permute-start(f16[512,128]{1,0:T(8,128)(2,1)S(1)} %convert_element_type.105), channel_id=1, source_target_pairs={{0,24},{4,28},{8,16},{12,20},{16,8},{20,12},{24,0},{28,4},{1,25},{... | collective-permute-start | bytes 393224 | tf_op jit(solution)/shard_map/ppermute | solution.py:22
  45.5 1.3 %collective-permute-start.14 = (f16[512,128]{1,0:T(8,128)(2,1)S(1)}, f16[512,128]{1,0:T(8,128)(2,1)S(1)}, u32[]{:S(2)}, u32[]{:S(2)}) collective-permute-start(f16[512,128]{1,0:T(8,128)(2,1)S(1)} %convert_element_type.105), channel_id=1, source_target_pairs={{0,8},{4,12},{8,0},{12,4},{16,24},{20,28},{24,16},{28,20},{1,9},{5... | collective-permute-start | bytes 393224 | tf_op jit(solution)/shard_map/ppermute | solution.py:22
  46.9 3.7 %collective-permute-done.16 = f16[512,128]{1,0:T(8,128)(2,1)S(1)} collective-permute-done((f16[512,128]{1,0:T(8,128)(2,1)S(1)}, f16[512,128]{1,0:T(8,128)(2,1)S(1)}, u32[]{:S(2)}, u32[]{:S(2)}) %collective-permute-start.16) | collective-permute-done | bytes 131104 | tf_op jit(solution)/shard_map/ppermute | solution.py:22
  50.6 1.7 %collective-permute-done.15 = f16[512,128]{1,0:T(8,128)(2,1)S(1)} collective-permute-done((f16[512,128]{1,0:T(8,128)(2,1)S(1)}, f16[512,128]{1,0:T(8,128)(2,1)S(1)}, u32[]{:S(2)}, u32[]{:S(2)}) %collective-permute-start.15) | collective-permute-done | bytes 131104 | tf_op jit(solution)/shard_map/ppermute | solution.py:22
  52.8 2.5 %collective-permute-start.9 = (f16[528,128]{1,0:T(8,128)(2,1)S(1)}, f16[528,128]{1,0:T(8,128)(2,1)S(1)}, u32[]{:S(2)}, u32[]{:S(2)}) collective-permute-start(f16[528,128]{1,0:T(8,128)(2,1)S(1)} %get-tuple-element.62), channel_id=1, source_target_pairs={{0,3},{1,2},{2,1},{3,0},{4,7},{5,6},{6,5},{7,4},{8,11},{9,10},{10,... | collective-permute-start | bytes 405512 | tf_op jit(solution)/shard_map/ppermute | solution.py:22
  55.3 1.9 %collective-permute-start.7 = (f16[528,128]{1,0:T(8,128)(2,1)S(1)}, f16[528,128]{1,0:T(8,128)(2,1)S(1)}, u32[]{:S(2)}, u32[]{:S(2)}) collective-permute-start(f16[528,128]{1,0:T(8,128)(2,1)S(1)} %get-tuple-element.64), channel_id=1, source_target_pairs={{0,1},{1,0},{2,3},{3,2},{4,5},{5,4},{6,7},{7,6},{8,9},{9,8},{10,11... | collective-permute-start | bytes 405512 | tf_op jit(solution)/shard_map/ppermute | solution.py:22
  57.2 4.0 %collective-permute-done.9 = f16[528,128]{1,0:T(8,128)(2,1)S(1)} collective-permute-done((f16[528,128]{1,0:T(8,128)(2,1)S(1)}, f16[528,128]{1,0:T(8,128)(2,1)S(1)}, u32[]{:S(2)}, u32[]{:S(2)}) %collective-permute-start.9) | collective-permute-done | bytes 135200 | tf_op jit(solution)/shard_map/ppermute | solution.py:22
  61.2 5.5 %collective-permute-done.8 = f16[528,128]{1,0:T(8,128)(2,1)S(1)} collective-permute-done((f16[528,128]{1,0:T(8,128)(2,1)S(1)}, f16[528,128]{1,0:T(8,128)(2,1)S(1)}, u32[]{:S(2)}, u32[]{:S(2)}) %collective-permute-start.8) | collective-permute-done | bytes 135200 | tf_op jit(solution)/shard_map/ppermute | solution.py:22
  68.3 1.7 %collective-permute-start.20 = (f32[5,64]{1,0:T(8,128)S(1)}, f32[5,64]{1,0:T(8,128)S(1)}, u32[]{:S(2)}, u32[]{:S(2)}) collective-permute-start(f32[5,64]{1,0:T(8,128)S(1)} %shard_map.86.refs_1_), channel_id=1, source_target_pairs={{0,24},{4,28},{8,16},{12,20},{16,8},{20,12},{24,0},{28,4},{1,25},{... | collective-permute-start | bytes 3848 | tf_op jit(solution)/shard_map/ppermute | solution.py:22
  70.6 1.2 %collective-permute-start.18 = (f32[5,64]{1,0:T(8,128)S(1)}, f32[5,64]{1,0:T(8,128)S(1)}, u32[]{:S(2)}, u32[]{:S(2)}) collective-permute-start(f32[5,64]{1,0:T(8,128)S(1)} %shard_map.86.refs_1_), channel_id=1, source_target_pairs={{0,8},{4,12},{8,0},{12,4},{16,24},{20,28},{24,16},{28,20},{1,9},{5... | collective-permute-start | bytes 3848 | tf_op jit(solution)/shard_map/ppermute | solution.py:22
  71.8 1.6 %backward_scan.1 = (f32[2,64,512]{2,1,0:T(8,128)S(1)}, f32[64,512]{1,0:T(8,128)S(1)}) custom-call(f32[64,512]{1,0:T(8,128)S(1)} %get-tuple-element.32.decay, f32[512,128]{1,0:T(8,128)S(1)} %get-tuple-element.45.grads), custom_call_target="tpu_custom_call" | custom-call | tf_op jit(solution)/shard_map/backward_scan/pallas_call | solution.py:548
  74.2 1.7 %leave.1 = (f32[512,128]{1,0:T(8,128)}, f32[2]{0:T(128)}, f32[4096,128]{1,0:T(8,128)}) custom-call(f32[2,64,512]{2,1,0:T(8,128)S(1)} %get-tuple-element.46.local, f32[64,512]{1,0:T(8,128)S(1)} %get-tuple-element.47.tail, f32[64,512]{1,0:T(8,128)S(1)} %get-tuple-element.32.decay, f32[1,64]{1,0:T(1,128)S(1)} %bitcast.44, f32[512,128]{1,0:T(8,128)S(1)} %bitcast.39, ...), custom_call_target="tpu_custom_call" | custom-call | tf_op jit(solution)/shard_map/leave/pallas_call | solution.py:555
  (65 shorter events, 13.1 us)
Async XLA Ops:
  2.2 14.3 %copy-start.5 = (bf16[1024,2,256]{2,1,0:T(2,128)(2,1)S(1)}, bf16[1024,2,256]{2,1,0:T(2,128)(2,1)}, u32[]{:S(2)}) copy-start(bf16[1024,2,256]{2,1,0:T(2,128)(2,1)} %param.10) | copy-start | bytes 3145732
  2.7 1.4 %collective-permute-start = (f32[3,64]{1,0:T(4,128)S(1)}, f32[3,64]{1,0:T(4,128)S(1)}, u32[]{:S(2)}, u32[]{:S(2)}) collective-permute-start(f32[3,64]{1,0:T(4,128)S(1)} %get-tuple-element.38.summary.products), channel_id=1, source_target_pairs={{0,4},{4,0},{8,12},{12,8},{16,20},{20,16},{24,28},{28,24},{1,5},{5... | collective-permute-start | bytes 2312 | tf_op jit(solution)/shard_map/ppermute | solution.py:22
  4.1 5.8 %collective-permute-start.3 = (f32[3,64]{1,0:T(4,128)S(1)}, f32[3,64]{1,0:T(4,128)S(1)}, u32[]{:S(2)}, u32[]{:S(2)}) collective-permute-start(f32[3,64]{1,0:T(4,128)S(1)} %shard_map.85.refs_0_), channel_id=1, source_target_pairs={{0,24},{4,28},{8,16},{12,20},{16,8},{20,12},{24,0},{28,4},{1,25},{... | collective-permute-start | bytes 2312 | tf_op jit(solution)/shard_map/ppermute | solution.py:22
  7.9 3.6 %collective-permute-start.2 = (f32[3,64]{1,0:T(4,128)S(1)}, f32[3,64]{1,0:T(4,128)S(1)}, u32[]{:S(2)}, u32[]{:S(2)}) collective-permute-start(f32[3,64]{1,0:T(4,128)S(1)} %shard_map.85.refs_0_), channel_id=1, source_target_pairs={{0,16},{4,20},{8,24},{12,28},{16,0},{20,4},{24,8},{28,12},{1,17},{... | collective-permute-start | bytes 2312 | tf_op jit(solution)/shard_map/ppermute | solution.py:22
  8.4 3.6 %collective-permute-start.1 = (f32[3,64]{1,0:T(4,128)S(1)}, f32[3,64]{1,0:T(4,128)S(1)}, u32[]{:S(2)}, u32[]{:S(2)}) collective-permute-start(f32[3,64]{1,0:T(4,128)S(1)} %shard_map.85.refs_0_), channel_id=1, source_target_pairs={{0,8},{4,12},{8,0},{12,4},{16,24},{20,28},{24,16},{28,20},{1,9},{5... | collective-permute-start | bytes 2312 | tf_op jit(solution)/shard_map/ppermute | solution.py:22
  12.1 8.0 %collective-permute-start.6 = (bf16[2,64,512]{2,1,0:T(8,128)(2,1)S(1)}, bf16[2,64,512]{2,1,0:T(8,128)(2,1)S(1)}, u32[]{:S(2)}, u32[]{:S(2)}) collective-permute-start(bf16[2,64,512]{2,1,0:T(8,128)(2,1)S(1)} %enter.1.refs_0_), channel_id=1, source_target_pairs={{0,3},{1,2},{2,1},{3,0},{4,7},{5,6},{6,5},{7,4},{8,11},{9,10},{10,... | collective-permute-start | bytes 393224 | tf_op jit(solution)/shard_map/ppermute | solution.py:22
  15.8 9.7 %collective-permute-start.5 = (bf16[2,64,512]{2,1,0:T(8,128)(2,1)S(1)}, bf16[2,64,512]{2,1,0:T(8,128)(2,1)S(1)}, u32[]{:S(2)}, u32[]{:S(2)}) collective-permute-start(bf16[2,64,512]{2,1,0:T(8,128)(2,1)S(1)} %enter.1.refs_0_), channel_id=1, source_target_pairs={{0,2},{1,3},{2,0},{3,1},{4,6},{5,7},{6,4},{7,5},{8,10},{9,11},{10,... | collective-permute-start | bytes 393224 | tf_op jit(solution)/shard_map/ppermute | solution.py:22
  15.8 9.7 %collective-permute-start.4 = (bf16[2,64,512]{2,1,0:T(8,128)(2,1)S(1)}, bf16[2,64,512]{2,1,0:T(8,128)(2,1)S(1)}, u32[]{:S(2)}, u32[]{:S(2)}) collective-permute-start(bf16[2,64,512]{2,1,0:T(8,128)(2,1)S(1)} %enter.1.refs_0_), channel_id=1, source_target_pairs={{0,1},{1,0},{2,3},{3,2},{4,5},{5,4},{6,7},{7,6},{8,9},{9,8},{10,11... | collective-permute-start | bytes 393224 | tf_op jit(solution)/shard_map/ppermute | solution.py:22
  18.0 7.5 %copy-start = (bf16[512,1024]{1,0:T(8,128)(2,1)S(1)}, bf16[512,1024]{1,0:T(8,128)(2,1)}, u32[]{:S(2)}) copy-start(bf16[512,1024]{1,0:T(8,128)(2,1)} %refs_4_.1) | copy-start | bytes 3145732
  31.1 2.0 %collective-permute-start.10 = (f16[2064,128]{1,0:T(8,128)(2,1)S(1)}, f16[2064,128]{1,0:T(8,128)(2,1)S(1)}, u32[]{:S(2)}, u32[]{:S(2)}) collective-permute-start(f16[2064,128]{1,0:T(8,128)(2,1)S(1)} %fusion), channel_id=1, source_target_pairs={{0,4},{4,0},{8,12},{12,8},{16,20},{20,16},{24,28},{28,24},{1,5},{5... | collective-permute-start | bytes 1585160 | tf_op jit(solution)/shard_map/ppermute | solution.py:22
  33.3 7.4 %collective-permute-start.13 = (f16[528,128]{1,0:T(8,128)(2,1)S(1)}, f16[528,128]{1,0:T(8,128)(2,1)S(1)}, u32[]{:S(2)}, u32[]{:S(2)}) collective-permute-start(f16[528,128]{1,0:T(8,128)(2,1)S(1)} %get-tuple-element.59), channel_id=1, source_target_pairs={{0,24},{4,28},{8,16},{12,20},{16,8},{20,12},{24,0},{28,4},{1,25},{... | collective-permute-start | bytes 405512 | tf_op jit(solution)/shard_map/ppermute | solution.py:22
  35.2 7.7 %collective-permute-start.12 = (f16[528,128]{1,0:T(8,128)(2,1)S(1)}, f16[528,128]{1,0:T(8,128)(2,1)S(1)}, u32[]{:S(2)}, u32[]{:S(2)}) collective-permute-start(f16[528,128]{1,0:T(8,128)(2,1)S(1)} %get-tuple-element.60), channel_id=1, source_target_pairs={{0,16},{4,20},{8,24},{12,28},{16,0},{20,4},{24,8},{28,12},{1,17},{... | collective-permute-start | bytes 405512 | tf_op jit(solution)/shard_map/ppermute | solution.py:22
  35.7 7.5 %collective-permute-start.11 = (f16[528,128]{1,0:T(8,128)(2,1)S(1)}, f16[528,128]{1,0:T(8,128)(2,1)S(1)}, u32[]{:S(2)}, u32[]{:S(2)}) collective-permute-start(f16[528,128]{1,0:T(8,128)(2,1)S(1)} %get-tuple-element.61), channel_id=1, source_target_pairs={{0,8},{4,12},{8,0},{12,4},{16,24},{20,28},{24,16},{28,20},{1,9},{5... | collective-permute-start | bytes 405512 | tf_op jit(solution)/shard_map/ppermute | solution.py:22
  43.3 7.3 %collective-permute-start.16 = (f16[512,128]{1,0:T(8,128)(2,1)S(1)}, f16[512,128]{1,0:T(8,128)(2,1)S(1)}, u32[]{:S(2)}, u32[]{:S(2)}) collective-permute-start(f16[512,128]{1,0:T(8,128)(2,1)S(1)} %convert_element_type.105), channel_id=1, source_target_pairs={{0,24},{4,28},{8,16},{12,20},{16,8},{20,12},{24,0},{28,4},{1,25},{... | collective-permute-start | bytes 393224 | tf_op jit(solution)/shard_map/ppermute | solution.py:22
  44.9 7.4 %collective-permute-start.15 = (f16[512,128]{1,0:T(8,128)(2,1)S(1)}, f16[512,128]{1,0:T(8,128)(2,1)S(1)}, u32[]{:S(2)}, u32[]{:S(2)}) collective-permute-start(f16[512,128]{1,0:T(8,128)(2,1)S(1)} %convert_element_type.105), channel_id=1, source_target_pairs={{0,16},{4,20},{8,24},{12,28},{16,0},{20,4},{24,8},{28,12},{1,17},{... | collective-permute-start | bytes 393224 | tf_op jit(solution)/shard_map/ppermute | solution.py:22
  45.5 6.8 %collective-permute-start.14 = (f16[512,128]{1,0:T(8,128)(2,1)S(1)}, f16[512,128]{1,0:T(8,128)(2,1)S(1)}, u32[]{:S(2)}, u32[]{:S(2)}) collective-permute-start(f16[512,128]{1,0:T(8,128)(2,1)S(1)} %convert_element_type.105), channel_id=1, source_target_pairs={{0,8},{4,12},{8,0},{12,4},{16,24},{20,28},{24,16},{28,20},{1,9},{5... | collective-permute-start | bytes 393224 | tf_op jit(solution)/shard_map/ppermute | solution.py:22
  52.6 23.3 %collective-permute-start.21 = (f16[2048,128]{1,0:T(8,128)(2,1)S(1)}, f16[2048,128]{1,0:T(8,128)(2,1)S(1)}, u32[]{:S(2)}, u32[]{:S(2)}) collective-permute-start(f16[2048,128]{1,0:T(8,128)(2,1)S(1)} %get-tuple-element.65), channel_id=1, source_target_pairs={{0,4},{4,0},{8,12},{12,8},{16,20},{20,16},{24,28},{28,24},{1,5},{5... | collective-permute-start | bytes 1572872 | tf_op jit(solution)/shard_map/ppermute | solution.py:22
  52.8 8.5 %collective-permute-start.9 = (f16[528,128]{1,0:T(8,128)(2,1)S(1)}, f16[528,128]{1,0:T(8,128)(2,1)S(1)}, u32[]{:S(2)}, u32[]{:S(2)}) collective-permute-start(f16[528,128]{1,0:T(8,128)(2,1)S(1)} %get-tuple-element.62), channel_id=1, source_target_pairs={{0,3},{1,2},{2,1},{3,0},{4,7},{5,6},{6,5},{7,4},{8,11},{9,10},{10,... | collective-permute-start | bytes 405512 | tf_op jit(solution)/shard_map/ppermute | solution.py:22
  55.3 11.5 %collective-permute-start.8 = (f16[528,128]{1,0:T(8,128)(2,1)S(1)}, f16[528,128]{1,0:T(8,128)(2,1)S(1)}, u32[]{:S(2)}, u32[]{:S(2)}) collective-permute-start(f16[528,128]{1,0:T(8,128)(2,1)S(1)} %get-tuple-element.63), channel_id=1, source_target_pairs={{0,2},{1,3},{2,0},{3,1},{4,6},{5,7},{6,4},{7,5},{8,10},{9,11},{10,... | collective-permute-start | bytes 405512 | tf_op jit(solution)/shard_map/ppermute | solution.py:22
  55.3 11.5 %collective-permute-start.7 = (f16[528,128]{1,0:T(8,128)(2,1)S(1)}, f16[528,128]{1,0:T(8,128)(2,1)S(1)}, u32[]{:S(2)}, u32[]{:S(2)}) collective-permute-start(f16[528,128]{1,0:T(8,128)(2,1)S(1)} %get-tuple-element.64), channel_id=1, source_target_pairs={{0,1},{1,0},{2,3},{3,2},{4,5},{5,4},{6,7},{7,6},{8,9},{9,8},{10,11... | collective-permute-start | bytes 405512 | tf_op jit(solution)/shard_map/ppermute | solution.py:22
  67.0 1.2 %collective-permute-start.17 = (f32[5,64]{1,0:T(8,128)S(1)}, f32[5,64]{1,0:T(8,128)S(1)}, u32[]{:S(2)}, u32[]{:S(2)}) collective-permute-start(f32[5,64]{1,0:T(8,128)S(1)} %get-tuple-element.55.summary), channel_id=1, source_target_pairs={{0,4},{4,0},{8,12},{12,8},{16,20},{20,16},{24,28},{28,24},{1,5},{5... | collective-permute-start | bytes 3848 | tf_op jit(solution)/shard_map/ppermute | solution.py:22
  68.3 5.1 %collective-permute-start.20 = (f32[5,64]{1,0:T(8,128)S(1)}, f32[5,64]{1,0:T(8,128)S(1)}, u32[]{:S(2)}, u32[]{:S(2)}) collective-permute-start(f32[5,64]{1,0:T(8,128)S(1)} %shard_map.86.refs_1_), channel_id=1, source_target_pairs={{0,24},{4,28},{8,16},{12,20},{16,8},{20,12},{24,0},{28,4},{1,25},{... | collective-permute-start | bytes 3848 | tf_op jit(solution)/shard_map/ppermute | solution.py:22
  70.0 3.6 %collective-permute-start.19 = (f32[5,64]{1,0:T(8,128)S(1)}, f32[5,64]{1,0:T(8,128)S(1)}, u32[]{:S(2)}, u32[]{:S(2)}) collective-permute-start(f32[5,64]{1,0:T(8,128)S(1)} %shard_map.86.refs_1_), channel_id=1, source_target_pairs={{0,16},{4,20},{8,24},{12,28},{16,0},{20,4},{24,8},{28,12},{1,17},{... | collective-permute-start | bytes 3848 | tf_op jit(solution)/shard_map/ppermute | solution.py:22
  70.6 3.6 %collective-permute-start.18 = (f32[5,64]{1,0:T(8,128)S(1)}, f32[5,64]{1,0:T(8,128)S(1)}, u32[]{:S(2)}, u32[]{:S(2)}) collective-permute-start(f32[5,64]{1,0:T(8,128)S(1)} %shard_map.86.refs_1_), channel_id=1, source_target_pairs={{0,8},{4,12},{8,0},{12,4},{16,24},{20,28},{24,16},{28,20},{1,9},{5... | collective-permute-start | bytes 3848 | tf_op jit(solution)/shard_map/ppermute | solution.py:22
  (4 other events, 10.3 us)

commit v2 on v1

--- a/solution.py
+++ b/solution.py
@@ -323,82 +323,79 @@
         summary[d + 1:d + 2, :] = to_row(jnp.sum(leaving, axis=1, keepdims=True), same)
 
 
-def backward_kernel(draws, tiles, decay, grads, local, tail):
+def unwind_kernel(tiles, decay, scale, gates, inner, weight, fade):
     factors = decay.shape[0]
     lane = lax.broadcasted_iota(jnp.int32, (factors, LANES), 1)
-    decays, pushes = [], []
-    for j in range(tiles):
-        a = decay[:, j * LANES:(j + 1) * LANES]
+    sized = to_column(scale[...], eye(factors))
+    beyond = jnp.ones((factors, 1), f32)
+    for j in range(tiles - 1, -1, -1):
+        part = slice(j * LANES, (j + 1) * LANES)
+        a = decay[:, part]
+        w = jnp.sqrt((1.0 - a) * (1.0 + a)) * sized
+        weight[:, part] = w
         if j + 1 < tiles:
             after = decay[:, (j + 1) * LANES:(j + 2) * LANES][:, 0:1]
         else:
             after = jnp.ones((factors, 1), f32)
-        decays.append(jnp.where(lane < LANES - 1, pltpu.roll(a, LANES - 1, 1), after))
+        run = jnp.where(lane < LANES - 1, pltpu.roll(a, LANES - 1, 1), after)
+        for level in range(gates.shape[0]):
+            step = 1 << level
+            inside = lane < LANES - step
+            gates[level, :, part] = jnp.where(inside, run, 0.0)
+            run = run * jnp.where(inside, pltpu.roll(run, LANES - step, 1), 1.0)
+        inner[:, part] = run
+        fade[:, part] = w * run * beyond
+        beyond = beyond * run[:, 0:1]
+
+
+def backward_kernel(draws, tiles, gates, inner, grads, local):
+    factors = inner.shape[0]
+    carry = None
+    for j in range(tiles - 1, -1, -1):
+        part = slice(j * LANES, (j + 1) * LANES)
         rows = lambda d: slice((d * tiles + j) * factors, (d * tiles + j + 1) * factors)
-        pushes.append([grads[rows(d), :] for d in range(draws)])
-    run, out, _ = block_scan(decays, pushes, True)
-    for j in range(tiles):
-        tail[:, j * LANES:(j + 1) * LANES] = run[j]
+        values = [grads[rows(d), :] for d in range(draws)]
+        for level in range(gates.shape[0]):
+            gate = gates[level, :, part]
+            values = [p + gate * pltpu.roll(p, LANES - (1 << level), 1) for p in values]
+        if carry is not None:
+            values = [values[d] + inner[:, part] * carry[d] for d in range(draws)]
         for d in range(draws):
-            local[d, :, j * LANES:(j + 1) * LANES] = out[j][d]
-
-
-def leave_kernel(draws, tiles, cells, local, tail, decay, scale, innov, value, *refs):
-    climb, (out, density, far, sem) = refs[:-4], refs[-4:]
-    half = value.shape[0]
-    move = pltpu.make_async_copy(value, far.at[pl.ds(pl.multiple_of((lax.axis_index("tm") % 2) * half, half), half), :], sem)
-    move.start()
-    factors = tail.shape[0]
+            local[d, :, part] = values[d]
+        carry = [p[:, 0:1] for p in values]
+
+
+def leave_kernel(draws, tiles, cells, count, *refs):
+    pieces, refs = refs[:count], refs[count:]
+    (local, fade, weight, innov), climb, (near, density, far, out, sems) = refs[:4], refs[4:-5], refs[-5:]
+    lines, chips = pieces[0].shape[0], count // 2
+    mine = lax.axis_index("tm")
+    moves = []
+    for n, piece in enumerate(pieces):
+        side = (mine + n // chips) % 2
+        start = pl.multiple_of((side * chips + ((mine // 2) ^ (n % chips))) * lines, lines)
+        moves.append(pltpu.make_async_copy(piece, far.at[pl.ds(start, lines), :], sems.at[n]))
+    for move in moves:
+        move.start()
+    factors = fade.shape[0]
     same = eye(factors)
     arriving, summed = entered(draws + 1, True, climb[0], climb[1:])
-    sized = to_column(scale[...], same)
     columns = [to_column(arriving[d:d + 1, :], same) for d in range(draws)]
     for d in range(draws):
         density[d] = jnp.max(summed[d:d + 1, :]) * (1.0 / cells)
     for j in range(tiles):
         part = slice(j * LANES, (j + 1) * LANES)
-        a = decay[:, part]
-        weight = jnp.sqrt((1.0 - a) * (1.0 + a)) * sized
         for d in range(draws):
             rows = pl.ds(j * draws + d, factors, stride=tiles * draws)
-            adjoint = local[d, :, part] + tail[:, part] * columns[d]
-            out[rows, :] = weight * adjoint - innov[rows, :]
-    move.wait()
+            out[rows, :] = weight[:, part] * local[d, :, part] + fade[:, part] * columns[d] - innov[rows, :]
+    moves.append(pltpu.make_async_copy(out, near, sems.at[count]))
+    moves[-1].start()
+    for move in moves:
+        move.wait()
 
 
 def room(mebibytes):
     return pltpu.CompilerParams(vmem_limit_bytes=mebibytes << 20)
-
-
-def assemble_kernel(*refs):
-    pieces, out = refs[:-1], refs[-1]
-    rows = pieces[0].shape[0]
-    for key, piece in enumerate(pieces):
-        start = pl.multiple_of(((lax.axis_index("tm") // 2) ^ key) * rows, rows)
-        out[pl.ds(start, rows), :] = piece[...]
-
-
-def write_kernel(flip, value, *refs):
-    out, sem = refs[-2:]
-    half = value.shape[0]
-    move = pltpu.make_async_copy(value, out.at[pl.ds(pl.multiple_of(((lax.axis_index("tm") + flip) % 2) * half, half), half), :], sem)
-    move.start()
-    move.wait()
-
-
-def write_half(value, flip, out, size):
-    far = pl.BlockSpec(memory_space=pltpu.HBM)
-    specs = [pl.BlockSpec(memory_space=pltpu.VMEM)]
-    return pl.pallas_call(
-        functools.partial(write_kernel, flip),
-        out_shape=shape((size, LANES), f32),
-        in_specs=specs if out is None else specs + [far],
-        out_specs=far,
-        input_output_aliases={} if out is None else {1: 0},
-        scratch_shapes=[pltpu.SemaphoreType.DMA],
-        name="write_half",
-        compiler_params=room(4),
-    )(value, *([] if out is None else [out]))
 
 
 def shape(dims, kind):
@@ -409,9 +406,7 @@
     pairs = lax.axis_size("tm") // 2
     other = swap(summary, "tm", 1)
     whole = pl.pallas_call(
-        functools.partial(pair_kernel, rows, backward, 1),
-        out_shape=shape(summary.shape, f32),
-        compiler_params=room(1),
+        functools.partial(pair_kernel, rows, backward, 1), out_shape=shape(summary.shape, f32), compiler_params=room(1)
     )(summary, other)
     return [other, whole] + [swap(whole, "tm", 2 * key) for key in range(1, pairs)]
 
@@ -471,7 +466,7 @@
     noise = noise_scale.reshape(series // LANES, LANES)
     loads = loadings.transpose(1, 0, 2)
     loads_t = loadings.transpose(1, 2, 0)
-    rows = min(256, series // 2)
+    rows = min(512, series // 2)
     body = draws * tiles * factors
     still = lambda dims: pl.BlockSpec(dims, lambda i: (0,) * len(dims))
     size = series * wide
@@ -512,6 +507,7 @@
 
     chips = spans // 2
     whole = pl.BlockSpec(memory_space=pltpu.VMEM)
+    distant = pl.BlockSpec(memory_space=pltpu.HBM)
     other = swap(pick(load_share, far_core).astype(f16), "tm", 1).astype(f32)
     kept = pl.pallas_call(
         join_kernel,
@@ -532,36 +528,37 @@
     )(kept, *others)
     total = lax.optimization_barrier(total.astype(f16))
     totals = [total] + [swap(total, "tm", 2 * key) for key in range(1, chips)]
-    mine = pl.pallas_call(
-        assemble_kernel,
-        out_shape=shape((half, LANES), f32),
-        name="assemble",
-        compiler_params=room(4),
-    )(*[value.astype(f32) for value in totals])
-    theirs = swap(mine.astype(f16), "tm", 1).astype(f32) * factor
+    passed = [swap(value, "tm", 1) for value in totals]
     path_grads, leaving = pl.pallas_call(
         functools.partial(gather_kernel, draws, tiles, parts),
         out_shape=(shape((body, LANES), f32), shape((2 * draws + 1, factors), f32)),
         name="gather",
         compiler_params=room(4),
     )(running, summary, grads, *[value.astype(f32) for value in arrived])
-    local_adjoint, tail = pl.pallas_call(
+    levels = LANES.bit_length() - 1
+    flat = shape((factors, steps), f32)
+    gates, inner, weight, fade = pl.pallas_call(
+        functools.partial(unwind_kernel, tiles),
+        out_shape=(shape((levels, factors, steps), f32), flat, flat, flat),
+        name="unwind",
+        compiler_params=room(4),
+    )(decays, innov_scale.reshape(1, factors))
+    local_adjoint = pl.pallas_call(
         functools.partial(backward_kernel, draws, tiles),
-        out_shape=(shape((draws, factors, steps), f32), shape((factors, steps), f32)),
+        out_shape=shape((draws, factors, steps), f32),
         name="backward_scan",
-        compiler_params=room(3),
-    )(decays, path_grads)
+        compiler_params=room(4),
+    )(gates, inner, path_grads)
     climb = carried(leaving, draws + 1, True)
     grad_innov, log_density, grad_load = pl.pallas_call(
-        functools.partial(leave_kernel, draws, tiles, float(spans * parts)),
+        functools.partial(leave_kernel, draws, tiles, float(spans * parts), 2 * chips),
         out_shape=(shape(innov.shape, f32), shape((draws,), f32), shape((size, LANES), f32)),
-        in_specs=[whole] * (6 + len(climb)),
-        out_specs=(whole, pl.BlockSpec(memory_space=pltpu.SMEM), pl.BlockSpec(memory_space=pltpu.HBM)),
-        scratch_shapes=[pltpu.SemaphoreType.DMA],
+        in_specs=[whole] * (2 * chips + 4 + len(climb)),
+        out_specs=(distant, pl.BlockSpec(memory_space=pltpu.SMEM), distant),
+        scratch_shapes=[pltpu.VMEM(innov.shape, f32), pltpu.SemaphoreType.DMA((2 * chips + 1,))],
         name="leave",
-        compiler_params=room(4),
-    )(local_adjoint, tail, decays, innov_scale.reshape(1, factors), innov, mine * factor, *climb)
-    grad_load = write_half(theirs, 1, grad_load, size)
+        compiler_params=room(6),
+    )(*[value.astype(f32) * factor for value in totals + passed], local_adjoint, fade, weight, innov, *climb)
     grad_load = grad_load.reshape(series, all_factors // LANES, draws, LANES).transpose(0, 2, 1, 3)
     grad_load = grad_load.reshape(series, draws, all_factors)
     grad_innov = grad_innov.reshape(factors, tiles, draws, LANES).transpose(0, 2, 1, 3)

time: 77.1 us -> 61.9 us (0.80)
  waiting for transfers between devices: 35.1 us -> 22.2 us
  Pallas kernels: 12.7 us -> 10.8 us
    ppermute x22 -> x25, waiting for transfers between devices: 35.1 us -> 22.2 us  [swap(): return lax.ppermute(value, axis, [(i, i ^ key) for i in range(count)])]
    pallas_call x1, Pallas kernels: 5.5 us -> 4.46 us  [local(): pl.pallas_call(functools.partial(residual_kernel, draws, parts), out_shap...]
    pallas_call x1, Pallas kernels: 1.6 us -> 0.81 us  [local(): pl.pallas_call(functools.partial(backward_kernel, draws, tiles), out_shap...]
    ppermute x22 -> x25, starting transfers between devices: 24.7 us -> 24.4 us  [swap(): return lax.ppermute(value, axis, [(i, i ^ key) for i in range(count)])]
  transfers between devices with their start and end apart: 22 -> 25, of which waited for: 16 -> 15; matrix products, arithmetic and copies ran while one was open for 2% -> 3% of each run, Pallas kernels for 6% -> 5%
where the time goes in v2:
time: 61.9 us; the launch traced here: 61.7 us
  starting transfers between devices  24.4 us (39%)
  waiting for transfers between devices  22.2 us (36%)
  Pallas kernels  10.8 us (17%)
  local copies, waits for them, and re-layouts  2.81 us (5%)
  between operations  0.89 us (1%)
    ppermute x25, starting transfers between devices, swap(): return lax.ppermute(value, axis, [(i, i ^ key) for i in range(count)])  24.4 us
    ppermute x25, waiting for transfers between devices, swap(): return lax.ppermute(value, axis, [(i, i ^ key) for i in range(count)])  22.2 us
    pallas_call x1, Pallas kernels, local(): pl.pallas_call(functools.partial(residual_kernel, draws, parts), out_shap...  4.46 us
    unnamed x14, local copies, waits for them, and re-layouts  2.81 us
    pallas_call x1, Pallas kernels, local(): pl.pallas_call(functools.partial(leave_kernel, draws, tiles, float(spans...  2.01 us
    pallas_call x1, Pallas kernels, local(): pl.pallas_call(functools.partial(forward_kernel, draws, tiles), out_shape...  1.4 us
  transfers between devices with their start and end apart: 25, of which 15 were waited for; matrix products, arithmetic and copies ran while one was open for 3% of the time, Pallas kernels for 5%

profile of v2, /device:TPU:0, one launch (start us, length us, event | category | flops | bytes accessed | tf_op | source)
XLA Modules:
  0.0 61.7 jit_solution(9342931037921961733)
XLA Ops:
  0.7 0.9 %copy-done.4 = f32[64,512]{1,0:T(8,128)S(1)} copy-done((f32[64,512]{1,0:T(8,128)S(1)}, f32[64,512]{1,0:T(8,128)}, u32[]{:S(2)}) %copy-start.4) | copy-done | bytes 131096
  4.1 3.8 %collective-permute-start.3 = (f32[3,64]{1,0:T(4,128)S(1)}, f32[3,64]{1,0:T(4,128)S(1)}, u32[]{:S(2)}, u32[]{:S(2)}) collective-permute-start(f32[3,64]{1,0:T(4,128)S(1)} %shard_map.85.refs_0_), channel_id=1, source_target_pairs={{0,24},{4,28},{8,16},{12,20},{16,8},{20,12},{24,0},{28,4},{1,25},{... | collective-permute-start | bytes 2312 | tf_op jit(solution)/shard_map/ppermute | solution.py:22
  8.5 1.4 %forward_scan.1 = (f32[2,64,512]{2,1,0:T(8,128)S(1)}, f32[64,512]{1,0:T(8,128)S(1)}) custom-call(f32[64,512]{1,0:T(8,128)S(1)} %get-tuple-element.34.decay, f32[2,64,512]{2,1,0:T(8,128)S(1)} %get-tuple-element.38.pushed), custom_call_target="tpu_custom_call" | custom-call | tf_op jit(solution)/shard_map/forward_scan/pallas_call | solution.py:452
  9.9 1.5 %collective-permute-done.2.refs_2_ = f32[3,64]{1,0:T(4,128)S(1)} collective-permute-done((f32[3,64]{1,0:T(4,128)S(1)}, f32[3,64]{1,0:T(4,128)S(1)}, u32[]{:S(2)}, u32[]{:S(2)}) %collective-permute-start.2) | collective-permute-done | bytes 800 | tf_op jit(solution)/shard_map/ppermute | solution.py:22
  12.1 3.7 %collective-permute-start.6 = (bf16[2,64,512]{2,1,0:T(8,128)(2,1)S(1)}, bf16[2,64,512]{2,1,0:T(8,128)(2,1)S(1)}, u32[]{:S(2)}, u32[]{:S(2)}) collective-permute-start(bf16[2,64,512]{2,1,0:T(8,128)(2,1)S(1)} %enter.1.refs_0_), channel_id=1, source_target_pairs={{0,3},{1,2},{2,1},{3,0},{4,7},{5,6},{6,5},{7,4},{8,11},{9,10},{10,... | collective-permute-start | bytes 393224 | tf_op jit(solution)/shard_map/ppermute | solution.py:22
  16.5 1.4 %copy.11 = bf16[1024,2,256]{0,2,1:T(8,128)(2,1)S(1)} copy(bf16[1024,2,256]{2,1,0:T(2,128)(2,1)S(1)} %copy-done.5) | data formatting | bytes 2097152 | tf_op args[4]
  18.2 1.9 %collective-permute-done.6.refs_3_ = bf16[2,64,512]{2,1,0:T(8,128)(2,1)S(1)} collective-permute-done((bf16[2,64,512]{2,1,0:T(8,128)(2,1)S(1)}, bf16[2,64,512]{2,1,0:T(8,128)(2,1)S(1)}, u32[]{:S(2)}, u32[]{:S(2)}) %collective-permute-start.6) | collective-permute-done | bytes 131104 | tf_op jit(solution)/shard_map/ppermute | solution.py:22
  20.0 5.4 %collective-permute-done.5.refs_2_ = bf16[2,64,512]{2,1,0:T(8,128)(2,1)S(1)} collective-permute-done((bf16[2,64,512]{2,1,0:T(8,128)(2,1)S(1)}, bf16[2,64,512]{2,1,0:T(8,128)(2,1)S(1)}, u32[]{:S(2)}, u32[]{:S(2)}) %collective-permute-start.5) | collective-permute-done | bytes 131104 | tf_op jit(solution)/shard_map/ppermute | solution.py:22
  25.5 4.5 %residual.1 = (f32[4,528,128]{2,1,0:T(8,128)S(1)}, f32[2,2064,128]{2,1,0:T(8,128)S(1)}) custom-call(bf16[2,64,512]{2,1,0:T(8,128)(2,1)S(1)} %enter.1.refs_0_, bf16[2,64,512]{2,1,0:T(8,128)(2,1)S(1)} %collective-permute-done.4.refs_1_, bf16[2,64,512]{2,1,0:T(8,128)(2,1)S(1)} %collective-permute-done.5.refs_2_, ...), custom_call_target="tpu_custom_call" | custom-call | tf_op jit(solution)/shard_map/residual/pallas_call | solution.py:474
  30.1 1.9 %collective-permute-done.7 = f16[2064,128]{1,0:T(8,128)(2,1)S(1)} collective-permute-done((f16[2064,128]{1,0:T(8,128)(2,1)S(1)}, f16[2064,128]{1,0:T(8,128)(2,1)S(1)}, u32[]{:S(2)}, u32[]{:S(2)}) %collective-permute-start.7) | collective-permute-done | bytes 528416 | tf_op jit(solution)/shard_map/ppermute | solution.py:22
  32.3 1.9 %collective-permute-start.10 = (f16[528,128]{1,0:T(8,128)(2,1)S(1)}, f16[528,128]{1,0:T(8,128)(2,1)S(1)}, u32[]{:S(2)}, u32[]{:S(2)}) collective-permute-start(f16[528,128]{1,0:T(8,128)(2,1)S(1)} %get-tuple-element.66), channel_id=1, source_target_pairs={{0,24},{4,28},{8,16},{12,20},{16,8},{20,12},{24,0},{28,4},{1,25},{... | collective-permute-start | bytes 405512 | tf_op jit(solution)/shard_map/ppermute | solution.py:22
  34.7 1.2 %collective-permute-start.8 = (f16[528,128]{1,0:T(8,128)(2,1)S(1)}, f16[528,128]{1,0:T(8,128)(2,1)S(1)}, u32[]{:S(2)}, u32[]{:S(2)}) collective-permute-start(f16[528,128]{1,0:T(8,128)(2,1)S(1)} %get-tuple-element.68), channel_id=1, source_target_pairs={{0,8},{4,12},{8,0},{12,4},{16,24},{20,28},{24,16},{28,20},{1,9},{5... | collective-permute-start | bytes 405512 | tf_op jit(solution)/shard_map/ppermute | solution.py:22
  35.9 2.5 %collective-permute-start.20 = (f16[528,128]{1,0:T(8,128)(2,1)S(1)}, f16[528,128]{1,0:T(8,128)(2,1)S(1)}, u32[]{:S(2)}, u32[]{:S(2)}) collective-permute-start(f16[528,128]{1,0:T(8,128)(2,1)S(1)} %get-tuple-element.63), channel_id=1, source_target_pairs={{0,3},{1,2},{2,1},{3,0},{4,7},{5,6},{6,5},{7,4},{8,11},{9,10},{10,... | collective-permute-start | bytes 405512 | tf_op jit(solution)/shard_map/ppermute | solution.py:22
  38.5 1.3 %collective-permute-done.10 = f16[528,128]{1,0:T(8,128)(2,1)S(1)} collective-permute-done((f16[528,128]{1,0:T(8,128)(2,1)S(1)}, f16[528,128]{1,0:T(8,128)(2,1)S(1)}, u32[]{:S(2)}, u32[]{:S(2)}) %collective-permute-start.10) | collective-permute-done | bytes 135200 | tf_op jit(solution)/shard_map/ppermute | solution.py:22
  39.7 2.1 %collective-permute-done.9 = f16[528,128]{1,0:T(8,128)(2,1)S(1)} collective-permute-done((f16[528,128]{1,0:T(8,128)(2,1)S(1)}, f16[528,128]{1,0:T(8,128)(2,1)S(1)}, u32[]{:S(2)}, u32[]{:S(2)}) %collective-permute-start.9) | collective-permute-done | bytes 135200 | tf_op jit(solution)/shard_map/ppermute | solution.py:22
  42.3 1.6 %collective-permute-start.13 = (f16[512,128]{1,0:T(8,128)(2,1)S(1)}, f16[512,128]{1,0:T(8,128)(2,1)S(1)}, u32[]{:S(2)}, u32[]{:S(2)}) collective-permute-start(f16[512,128]{1,0:T(8,128)(2,1)S(1)} %convert_element_type.102), channel_id=1, source_target_pairs={{0,24},{4,28},{8,16},{12,20},{16,8},{20,12},{24,0},{28,4},{1,25},{... | collective-permute-start | bytes 393224 | tf_op jit(solution)/shard_map/ppermute | solution.py:22
  44.5 1.3 %collective-permute-start.11 = (f16[512,128]{1,0:T(8,128)(2,1)S(1)}, f16[512,128]{1,0:T(8,128)(2,1)S(1)}, u32[]{:S(2)}, u32[]{:S(2)}) collective-permute-start(f16[512,128]{1,0:T(8,128)(2,1)S(1)} %convert_element_type.102), channel_id=1, source_target_pairs={{0,8},{4,12},{8,0},{12,4},{16,24},{20,28},{24,16},{28,20},{1,9},{5... | collective-permute-start | bytes 393224 | tf_op jit(solution)/shard_map/ppermute | solution.py:22
  45.8 1.1 %collective-permute-start.18 = (f16[528,128]{1,0:T(8,128)(2,1)S(1)}, f16[528,128]{1,0:T(8,128)(2,1)S(1)}, u32[]{:S(2)}, u32[]{:S(2)}) collective-permute-start(f16[528,128]{1,0:T(8,128)(2,1)S(1)} %get-tuple-element.65), channel_id=1, source_target_pairs={{0,1},{1,0},{2,3},{3,2},{4,5},{5,4},{6,7},{7,6},{8,9},{9,8},{10,11... | collective-permute-start | bytes 405512 | tf_op jit(solution)/shard_map/ppermute | solution.py:22
  47.0 2.1 %collective-permute-done.19 = f16[528,128]{1,0:T(8,128)(2,1)S(1)} collective-permute-done((f16[528,128]{1,0:T(8,128)(2,1)S(1)}, f16[528,128]{1,0:T(8,128)(2,1)S(1)}, u32[]{:S(2)}, u32[]{:S(2)}) %collective-permute-start.19) | collective-permute-done | bytes 135200 | tf_op jit(solution)/shard_map/ppermute | solution.py:22
  49.6 1.7 %collective-permute-done.12 = f16[512,128]{1,0:T(8,128)(2,1)S(1)} collective-permute-done((f16[512,128]{1,0:T(8,128)(2,1)S(1)}, f16[512,128]{1,0:T(8,128)(2,1)S(1)}, u32[]{:S(2)}, u32[]{:S(2)}) %collective-permute-start.12) | collective-permute-done | bytes 131104 | tf_op jit(solution)/shard_map/ppermute | solution.py:22
  53.7 1.8 %collective-permute-start.24 = (f32[5,64]{1,0:T(8,128)S(1)}, f32[5,64]{1,0:T(8,128)S(1)}, u32[]{:S(2)}, u32[]{:S(2)}) collective-permute-start(f32[5,64]{1,0:T(8,128)S(1)} %shard_map.86.refs_13_), channel_id=1, source_target_pairs={{0,24},{4,28},{8,16},{12,20},{16,8},{20,12},{24,0},{28,4},{1,25},{... | collective-permute-start | bytes 3848 | tf_op jit(solution)/shard_map/ppermute | solution.py:22
  56.1 1.2 %collective-permute-start.22 = (f32[5,64]{1,0:T(8,128)S(1)}, f32[5,64]{1,0:T(8,128)S(1)}, u32[]{:S(2)}, u32[]{:S(2)}) collective-permute-start(f32[5,64]{1,0:T(8,128)S(1)} %shard_map.86.refs_13_), channel_id=1, source_target_pairs={{0,8},{4,12},{8,0},{12,4},{16,24},{20,28},{24,16},{28,20},{1,9},{5... | collective-permute-start | bytes 3848 | tf_op jit(solution)/shard_map/ppermute | solution.py:22
  58.3 0.9 %collective-permute-done.23.refs_15_ = f32[5,64]{1,0:T(8,128)S(1)} collective-permute-done((f32[5,64]{1,0:T(8,128)S(1)}, f32[5,64]{1,0:T(8,128)S(1)}, u32[]{:S(2)}, u32[]{:S(2)}) %collective-permute-start.23) | collective-permute-done | bytes 1312 | tf_op jit(solution)/shard_map/ppermute | solution.py:22
  59.7 2.0 %leave.1 = (f32[512,128]{1,0:T(8,128)}, f32[2]{0:T(128)}, f32[4096,128]{1,0:T(8,128)}) custom-call(f32[512,128]{1,0:T(8,128)S(1)} %get-tuple-element.76.refs_0_, f32[512,128]{1,0:T(8,128)S(1)} %get-tuple-element.70.refs_1_, f32[512,128]{1,0:T(8,128)S(1)} %get-tuple-element.71.refs_2_, f32[512,128]{1,0:T(8,128)S(1)} %get-tuple-element.72.refs_3_, ...), custom_call_target="tpu_custom_call" | custom-call | tf_op jit(solution)/shard_map/leave/pallas_call | solution.py:553
  (65 shorter events, 11.7 us)
Async XLA Ops:
  4.1 5.8 %collective-permute-start.3 = (f32[3,64]{1,0:T(4,128)S(1)}, f32[3,64]{1,0:T(4,128)S(1)}, u32[]{:S(2)}, u32[]{:S(2)}) collective-permute-start(f32[3,64]{1,0:T(4,128)S(1)} %shard_map.85.refs_0_), channel_id=1, source_target_pairs={{0,24},{4,28},{8,16},{12,20},{16,8},{20,12},{24,0},{28,4},{1,25},{... | collective-permute-start | bytes 2312 | tf_op jit(solution)/shard_map/ppermute | solution.py:22
  7.9 3.6 %collective-permute-start.2 = (f32[3,64]{1,0:T(4,128)S(1)}, f32[3,64]{1,0:T(4,128)S(1)}, u32[]{:S(2)}, u32[]{:S(2)}) collective-permute-start(f32[3,64]{1,0:T(4,128)S(1)} %shard_map.85.refs_0_), channel_id=1, source_target_pairs={{0,16},{4,20},{8,24},{12,28},{16,0},{20,4},{24,8},{28,12},{1,17},{... | collective-permute-start | bytes 2312 | tf_op jit(solution)/shard_map/ppermute | solution.py:22
  8.4 3.6 %collective-permute-start.1 = (f32[3,64]{1,0:T(4,128)S(1)}, f32[3,64]{1,0:T(4,128)S(1)}, u32[]{:S(2)}, u32[]{:S(2)}) collective-permute-start(f32[3,64]{1,0:T(4,128)S(1)} %shard_map.85.refs_0_), channel_id=1, source_target_pairs={{0,8},{4,12},{8,0},{12,4},{16,24},{20,28},{24,16},{28,20},{1,9},{5... | collective-permute-start | bytes 2312 | tf_op jit(solution)/shard_map/ppermute | solution.py:22
  12.1 8.0 %collective-permute-start.6 = (bf16[2,64,512]{2,1,0:T(8,128)(2,1)S(1)}, bf16[2,64,512]{2,1,0:T(8,128)(2,1)S(1)}, u32[]{:S(2)}, u32[]{:S(2)}) collective-permute-start(bf16[2,64,512]{2,1,0:T(8,128)(2,1)S(1)} %enter.1.refs_0_), channel_id=1, source_target_pairs={{0,3},{1,2},{2,1},{3,0},{4,7},{5,6},{6,5},{7,4},{8,11},{9,10},{10,... | collective-permute-start | bytes 393224 | tf_op jit(solution)/shard_map/ppermute | solution.py:22
  15.8 9.7 %collective-permute-start.5 = (bf16[2,64,512]{2,1,0:T(8,128)(2,1)S(1)}, bf16[2,64,512]{2,1,0:T(8,128)(2,1)S(1)}, u32[]{:S(2)}, u32[]{:S(2)}) collective-permute-start(bf16[2,64,512]{2,1,0:T(8,128)(2,1)S(1)} %enter.1.refs_0_), channel_id=1, source_target_pairs={{0,2},{1,3},{2,0},{3,1},{4,6},{5,7},{6,4},{7,5},{8,10},{9,11},{10,... | collective-permute-start | bytes 393224 | tf_op jit(solution)/shard_map/ppermute | solution.py:22
  15.8 9.7 %collective-permute-start.4 = (bf16[2,64,512]{2,1,0:T(8,128)(2,1)S(1)}, bf16[2,64,512]{2,1,0:T(8,128)(2,1)S(1)}, u32[]{:S(2)}, u32[]{:S(2)}) collective-permute-start(bf16[2,64,512]{2,1,0:T(8,128)(2,1)S(1)} %enter.1.refs_0_), channel_id=1, source_target_pairs={{0,1},{1,0},{2,3},{3,2},{4,5},{5,4},{6,7},{7,6},{8,9},{9,8},{10,11... | collective-permute-start | bytes 393224 | tf_op jit(solution)/shard_map/ppermute | solution.py:22
  30.0 2.0 %collective-permute-start.7 = (f16[2064,128]{1,0:T(8,128)(2,1)S(1)}, f16[2064,128]{1,0:T(8,128)(2,1)S(1)}, u32[]{:S(2)}, u32[]{:S(2)}) collective-permute-start(f16[2064,128]{1,0:T(8,128)(2,1)S(1)} %fusion), channel_id=1, source_target_pairs={{0,4},{4,0},{8,12},{12,8},{16,20},{20,16},{24,28},{28,24},{1,5},{5... | collective-permute-start | bytes 1585160 | tf_op jit(solution)/shard_map/ppermute | solution.py:22
  32.3 7.4 %collective-permute-start.10 = (f16[528,128]{1,0:T(8,128)(2,1)S(1)}, f16[528,128]{1,0:T(8,128)(2,1)S(1)}, u32[]{:S(2)}, u32[]{:S(2)}) collective-permute-start(f16[528,128]{1,0:T(8,128)(2,1)S(1)} %get-tuple-element.66), channel_id=1, source_target_pairs={{0,24},{4,28},{8,16},{12,20},{16,8},{20,12},{24,0},{28,4},{1,25},{... | collective-permute-start | bytes 405512 | tf_op jit(solution)/shard_map/ppermute | solution.py:22
  34.2 7.7 %collective-permute-start.9 = (f16[528,128]{1,0:T(8,128)(2,1)S(1)}, f16[528,128]{1,0:T(8,128)(2,1)S(1)}, u32[]{:S(2)}, u32[]{:S(2)}) collective-permute-start(f16[528,128]{1,0:T(8,128)(2,1)S(1)} %get-tuple-element.67), channel_id=1, source_target_pairs={{0,16},{4,20},{8,24},{12,28},{16,0},{20,4},{24,8},{28,12},{1,17},{... | collective-permute-start | bytes 405512 | tf_op jit(solution)/shard_map/ppermute | solution.py:22
  34.7 7.5 %collective-permute-start.8 = (f16[528,128]{1,0:T(8,128)(2,1)S(1)}, f16[528,128]{1,0:T(8,128)(2,1)S(1)}, u32[]{:S(2)}, u32[]{:S(2)}) collective-permute-start(f16[528,128]{1,0:T(8,128)(2,1)S(1)} %get-tuple-element.68), channel_id=1, source_target_pairs={{0,8},{4,12},{8,0},{12,4},{16,24},{20,28},{24,16},{28,20},{1,9},{5... | collective-permute-start | bytes 405512 | tf_op jit(solution)/shard_map/ppermute | solution.py:22
  35.9 9.9 %collective-permute-start.20 = (f16[528,128]{1,0:T(8,128)(2,1)S(1)}, f16[528,128]{1,0:T(8,128)(2,1)S(1)}, u32[]{:S(2)}, u32[]{:S(2)}) collective-permute-start(f16[528,128]{1,0:T(8,128)(2,1)S(1)} %get-tuple-element.63), channel_id=1, source_target_pairs={{0,3},{1,2},{2,1},{3,0},{4,7},{5,6},{6,5},{7,4},{8,11},{9,10},{10,... | collective-permute-start | bytes 405512 | tf_op jit(solution)/shard_map/ppermute | solution.py:22
  38.5 10.6 %collective-permute-start.19 = (f16[528,128]{1,0:T(8,128)(2,1)S(1)}, f16[528,128]{1,0:T(8,128)(2,1)S(1)}, u32[]{:S(2)}, u32[]{:S(2)}) collective-permute-start(f16[528,128]{1,0:T(8,128)(2,1)S(1)} %get-tuple-element.64), channel_id=1, source_target_pairs={{0,2},{1,3},{2,0},{3,1},{4,6},{5,7},{6,4},{7,5},{8,10},{9,11},{10,... | collective-permute-start | bytes 405512 | tf_op jit(solution)/shard_map/ppermute | solution.py:22
  42.3 7.3 %collective-permute-start.13 = (f16[512,128]{1,0:T(8,128)(2,1)S(1)}, f16[512,128]{1,0:T(8,128)(2,1)S(1)}, u32[]{:S(2)}, u32[]{:S(2)}) collective-permute-start(f16[512,128]{1,0:T(8,128)(2,1)S(1)} %convert_element_type.102), channel_id=1, source_target_pairs={{0,24},{4,28},{8,16},{12,20},{16,8},{20,12},{24,0},{28,4},{1,25},{... | collective-permute-start | bytes 393224 | tf_op jit(solution)/shard_map/ppermute | solution.py:22
  43.9 7.4 %collective-permute-start.12 = (f16[512,128]{1,0:T(8,128)(2,1)S(1)}, f16[512,128]{1,0:T(8,128)(2,1)S(1)}, u32[]{:S(2)}, u32[]{:S(2)}) collective-permute-start(f16[512,128]{1,0:T(8,128)(2,1)S(1)} %convert_element_type.102), channel_id=1, source_target_pairs={{0,16},{4,20},{8,24},{12,28},{16,0},{20,4},{24,8},{28,12},{1,17},{... | collective-permute-start | bytes 393224 | tf_op jit(solution)/shard_map/ppermute | solution.py:22
  44.5 6.8 %collective-permute-start.11 = (f16[512,128]{1,0:T(8,128)(2,1)S(1)}, f16[512,128]{1,0:T(8,128)(2,1)S(1)}, u32[]{:S(2)}, u32[]{:S(2)}) collective-permute-start(f16[512,128]{1,0:T(8,128)(2,1)S(1)} %convert_element_type.102), channel_id=1, source_target_pairs={{0,8},{4,12},{8,0},{12,4},{16,24},{20,28},{24,16},{28,20},{1,9},{5... | collective-permute-start | bytes 393224 | tf_op jit(solution)/shard_map/ppermute | solution.py:22
  45.8 6.0 %collective-permute-start.18 = (f16[528,128]{1,0:T(8,128)(2,1)S(1)}, f16[528,128]{1,0:T(8,128)(2,1)S(1)}, u32[]{:S(2)}, u32[]{:S(2)}) collective-permute-start(f16[528,128]{1,0:T(8,128)(2,1)S(1)} %get-tuple-element.65), channel_id=1, source_target_pairs={{0,1},{1,0},{2,3},{3,2},{4,5},{5,4},{6,7},{7,6},{8,9},{9,8},{10,11... | collective-permute-start | bytes 405512 | tf_op jit(solution)/shard_map/ppermute | solution.py:22
  49.0 6.5 %collective-permute-start.14 = (f16[512,128]{1,0:T(8,128)(2,1)S(1)}, f16[512,128]{1,0:T(8,128)(2,1)S(1)}, u32[]{:S(2)}, u32[]{:S(2)}) collective-permute-start(f16[512,128]{1,0:T(8,128)(2,1)S(1)} %convert_element_type.102), channel_id=1, source_target_pairs={{0,4},{4,0},{8,12},{12,8},{16,20},{20,16},{24,28},{28,24},{1,5},{5... | collective-permute-start | bytes 393224 | tf_op jit(solution)/shard_map/ppermute | solution.py:22
  49.5 6.5 %collective-permute-start.17 = (f16[512,128]{1,0:T(8,128)(2,1)S(1)}, f16[512,128]{1,0:T(8,128)(2,1)S(1)}, u32[]{:S(2)}, u32[]{:S(2)}) collective-permute-start(f16[512,128]{1,0:T(8,128)(2,1)S(1)} %collective-permute-done.13), channel_id=1, source_target_pairs={{0,4},{4,0},{8,12},{12,8},{16,20},{20,16},{24,28},{28,24},{1,5},{5... | collective-permute-start | bytes 393224 | tf_op jit(solution)/shard_map/ppermute | solution.py:22
  51.3 6.0 %collective-permute-start.16 = (f16[512,128]{1,0:T(8,128)(2,1)S(1)}, f16[512,128]{1,0:T(8,128)(2,1)S(1)}, u32[]{:S(2)}, u32[]{:S(2)}) collective-permute-start(f16[512,128]{1,0:T(8,128)(2,1)S(1)} %collective-permute-done.12), channel_id=1, source_target_pairs={{0,4},{4,0},{8,12},{12,8},{16,20},{20,16},{24,28},{28,24},{1,5},{5... | collective-permute-start | bytes 393224 | tf_op jit(solution)/shard_map/ppermute | solution.py:22
  51.3 6.0 %collective-permute-start.15 = (f16[512,128]{1,0:T(8,128)(2,1)S(1)}, f16[512,128]{1,0:T(8,128)(2,1)S(1)}, u32[]{:S(2)}, u32[]{:S(2)}) collective-permute-start(f16[512,128]{1,0:T(8,128)(2,1)S(1)} %collective-permute-done.11), channel_id=1, source_target_pairs={{0,4},{4,0},{8,12},{12,8},{16,20},{20,16},{24,28},{28,24},{1,5},{5... | collective-permute-start | bytes 393224 | tf_op jit(solution)/shard_map/ppermute | solution.py:22
  52.1 1.6 %collective-permute-start.21 = (f32[5,64]{1,0:T(8,128)S(1)}, f32[5,64]{1,0:T(8,128)S(1)}, u32[]{:S(2)}, u32[]{:S(2)}) collective-permute-start(f32[5,64]{1,0:T(8,128)S(1)} %get-tuple-element.59.summary), channel_id=1, source_target_pairs={{0,4},{4,0},{8,12},{12,8},{16,20},{20,16},{24,28},{28,24},{1,5},{5... | collective-permute-start | bytes 3848 | tf_op jit(solution)/shard_map/ppermute | solution.py:22
  53.7 4.6 %collective-permute-start.24 = (f32[5,64]{1,0:T(8,128)S(1)}, f32[5,64]{1,0:T(8,128)S(1)}, u32[]{:S(2)}, u32[]{:S(2)}) collective-permute-start(f32[5,64]{1,0:T(8,128)S(1)} %shard_map.86.refs_13_), channel_id=1, source_target_pairs={{0,24},{4,28},{8,16},{12,20},{16,8},{20,12},{24,0},{28,4},{1,25},{... | collective-permute-start | bytes 3848 | tf_op jit(solution)/shard_map/ppermute | solution.py:22
  55.6 3.6 %collective-permute-start.23 = (f32[5,64]{1,0:T(8,128)S(1)}, f32[5,64]{1,0:T(8,128)S(1)}, u32[]{:S(2)}, u32[]{:S(2)}) collective-permute-start(f32[5,64]{1,0:T(8,128)S(1)} %shard_map.86.refs_13_), channel_id=1, source_target_pairs={{0,16},{4,20},{8,24},{12,28},{16,0},{20,4},{24,8},{28,12},{1,17},{... | collective-permute-start | bytes 3848 | tf_op jit(solution)/shard_map/ppermute | solution.py:22
  56.1 3.6 %collective-permute-start.22 = (f32[5,64]{1,0:T(8,128)S(1)}, f32[5,64]{1,0:T(8,128)S(1)}, u32[]{:S(2)}, u32[]{:S(2)}) collective-permute-start(f32[5,64]{1,0:T(8,128)S(1)} %shard_map.86.refs_13_), channel_id=1, source_target_pairs={{0,8},{4,12},{8,0},{12,4},{16,24},{20,28},{24,16},{28,20},{1,9},{5... | collective-permute-start | bytes 3848 | tf_op jit(solution)/shard_map/ppermute | solution.py:22
  (7 other events, 33.4 us)

commit v3 on v2

--- a/solution.py
+++ b/solution.py
@@ -154,21 +154,26 @@
         path[d] = (local[d] + running[...] * column).astype(bf16)
 
 
-def residual_kernel(draws, parts, *refs):
+def when(condition):
+    return (lambda body: body()) if condition is True else pl.when(condition)
+
+
+def residual_kernel(draws, parts, count, *refs):
     pieces, (returns, loads, loads_t, noise, squares, grads, shares, paths, density, top) = refs[:parts], refs[parts:]
     factors = pieces[0].shape[1]
-    step = pl.program_id(0)
-    count = pl.num_programs(0)
+    step = 0 if count == 1 else pl.program_id(0)
     wide = paths.shape[1] // LANES
-    side = step // (count // 2)
-    base = (step % (count // 2)) * (returns.shape[1] * wide * draws)
-
-    @pl.when(step == 0)
+    share_rows = returns.shape[1] // 2 if count == 1 else returns.shape[1]
+    side = step // max(count // 2, 1)
+    base = (step % max(count // 2, 1)) * (share_rows * wide * draws)
+
+    @when(step == 0)
     def _():
         for n in range(parts):
             start = pl.multiple_of((lax.axis_index("series") ^ n) * factors, factors)
             paths[:, pl.ds(start, factors), :] = pieces[n][...]
-        grads[...] = jnp.zeros_like(grads)
+        if count > 1:
+            grads[...] = jnp.zeros_like(grads)
         density[...] = jnp.zeros_like(density)
         top[...] = jnp.zeros_like(top)
 
@@ -199,19 +204,22 @@
         for n in range(parts):
             for j in range(tiles):
                 to = slice((d * tiles + j) * factors, (d * tiles + j + 1) * factors)
-                grads[n, to, :] += product[n * factors:(n + 1) * factors, j * LANES:(j + 1) * LANES]
+                part = product[n * factors:(n + 1) * factors, j * LANES:(j + 1) * LANES]
+                grads[n, to, :] = part if count == 1 else grads[n, to, :] + part
         share = lax.dot_general(pulled, paths[d], (((1,), (1,)), ((), ())), preferred_element_type=f32)
         most = top[...]
         for j in range(wide):
             tile = share[:, j * LANES:(j + 1) * LANES]
-            shares[side, pl.ds(base + (j * draws + d), rows, stride=wide * draws), :] = tile
+            for part in range(rows // share_rows):
+                piece = tile[part * share_rows:(part + 1) * share_rows]
+                shares[side + part, pl.ds(base + (j * draws + d), share_rows, stride=wide * draws), :] = piece
             most = jnp.maximum(most, jnp.max(jnp.abs(tile).reshape(rows // 8, 8, LANES), axis=0))
         top[...] = most
 
-    @pl.when(step == pl.num_programs(0) - 1)
+    @when(step == count - 1)
     def _():
         body = draws * tiles * factors
-        cells = pl.num_programs(0) * rows * seen.shape[1]
+        cells = count * rows * seen.shape[1]
         peak = jnp.zeros((1, LANES), f32)
         for n in range(parts):
             peak = jnp.maximum(peak, jnp.max(jnp.abs(grads[n, :body, :]), axis=0, keepdims=True))
@@ -466,20 +474,20 @@
     noise = noise_scale.reshape(series // LANES, LANES)
     loads = loadings.transpose(1, 0, 2)
     loads_t = loadings.transpose(1, 2, 0)
-    rows = min(512, series // 2)
+    rows = min(1024, series)
     body = draws * tiles * factors
     still = lambda dims: pl.BlockSpec(dims, lambda i: (0,) * len(dims))
     size = series * wide
     half, piece = size // 2, size // spans
     grads, load_share = pl.pallas_call(
-        functools.partial(residual_kernel, draws, parts),
+        functools.partial(residual_kernel, draws, parts, series // rows),
         out_shape=(
             shape((parts, body + TAIL, LANES), f32),
             shape((2, half + TAIL, LANES), f32),
         ),
         grid_spec=pl.GridSpec(
-            grid=(series // rows,),
-            in_specs=[still((draws, factors, steps))] * parts
+            grid=() if rows == series else (series // rows,),
+            in_specs=[pl.BlockSpec(memory_space=pltpu.VMEM)] * (parts + 5) if rows == series else [still((draws, factors, steps))] * parts
             + [
                 pl.BlockSpec((steps, rows), lambda i: (0, i)),
                 pl.BlockSpec((draws, rows, all_factors), lambda i: (0, i, 0)),
@@ -487,7 +495,7 @@
                 still((series // LANES, LANES)),
                 still((draws, LANES)),
             ],
-            out_specs=[
+            out_specs=[pl.BlockSpec(memory_space=pltpu.VMEM)] * 2 if rows == series else [
                 still((parts, body + TAIL, LANES)),
                 still((2, half + TAIL, LANES)),
             ],
@@ -498,7 +506,7 @@
             ],
         ),
         name="residual",
-        compiler_params=room(16),
+        compiler_params=room(28),
     )(*pieces, returns, loads, loads_t, noise, squares)
 
     pick = lambda value, place: lax.dynamic_slice(value, (place, 0, 0), (1,) + value.shape[1:], allow_negative_indices=False)[0]

time: 61.9 us -> 61.1 us (0.987)
  Pallas kernels: 10.8 us -> 10.1 us
    pallas_call x1, Pallas kernels: 4.46 us -> 3.73 us  [local(): pl.pallas_call(functools.partial(residual_kernel, draws, parts, series //...]
where the time goes in v3:
time: 61.1 us; the launch traced here: 61 us
  starting transfers between devices  24.5 us (40%)
  waiting for transfers between devices  22.2 us (36%)
  Pallas kernels  10.1 us (17%)
  local copies, waits for them, and re-layouts  2.81 us (5%)
  between operations  0.89 us (1%)
    ppermute x25, starting transfers between devices, swap(): return lax.ppermute(value, axis, [(i, i ^ key) for i in range(count)])  24.5 us
    ppermute x25, waiting for transfers between devices, swap(): return lax.ppermute(value, axis, [(i, i ^ key) for i in range(count)])  22.2 us
    pallas_call x1, Pallas kernels, local(): pl.pallas_call(functools.partial(residual_kernel, draws, parts, series //...  3.73 us
    unnamed x14, local copies, waits for them, and re-layouts  2.81 us
    pallas_call x1, Pallas kernels, local(): pl.pallas_call(functools.partial(leave_kernel, draws, tiles, float(spans...  2.01 us
    pallas_call x1, Pallas kernels, local(): pl.pallas_call(functools.partial(forward_kernel, draws, tiles), out_shape...  1.4 us
  transfers between devices with their start and end apart: 25, of which 15 were waited for; matrix products, arithmetic and copies ran while one was open for 3% of the time, Pallas kernels for 5%

profile of v3, /device:TPU:0, one launch (start us, length us, event | category | flops | bytes accessed | tf_op | source)
XLA Modules:
  0.0 61.0 jit_solution(1806753007403309167)
XLA Ops:
  0.7 0.9 %copy-done.4 = f32[64,512]{1,0:T(8,128)S(1)} copy-done((f32[64,512]{1,0:T(8,128)S(1)}, f32[64,512]{1,0:T(8,128)}, u32[]{:S(2)}) %copy-start.4) | copy-done | bytes 131096
  4.1 3.8 %collective-permute-start.3 = (f32[3,64]{1,0:T(4,128)S(1)}, f32[3,64]{1,0:T(4,128)S(1)}, u32[]{:S(2)}, u32[]{:S(2)}) collective-permute-start(f32[3,64]{1,0:T(4,128)S(1)} %shard_map.85.refs_0_), channel_id=1, source_target_pairs={{0,24},{4,28},{8,16},{12,20},{16,8},{20,12},{24,0},{28,4},{1,25},{... | collective-permute-start | bytes 2312 | tf_op jit(solution)/shard_map/ppermute | solution.py:22
  8.5 1.4 %forward_scan.1 = (f32[2,64,512]{2,1,0:T(8,128)S(1)}, f32[64,512]{1,0:T(8,128)S(1)}) custom-call(f32[64,512]{1,0:T(8,128)S(1)} %get-tuple-element.34.decay, f32[2,64,512]{2,1,0:T(8,128)S(1)} %get-tuple-element.38.pushed), custom_call_target="tpu_custom_call" | custom-call | tf_op jit(solution)/shard_map/forward_scan/pallas_call | solution.py:460
  9.9 1.5 %collective-permute-done.2.refs_2_ = f32[3,64]{1,0:T(4,128)S(1)} collective-permute-done((f32[3,64]{1,0:T(4,128)S(1)}, f32[3,64]{1,0:T(4,128)S(1)}, u32[]{:S(2)}, u32[]{:S(2)}) %collective-permute-start.2) | collective-permute-done | bytes 800 | tf_op jit(solution)/shard_map/ppermute | solution.py:22
  12.1 3.7 %collective-permute-start.6 = (bf16[2,64,512]{2,1,0:T(8,128)(2,1)S(1)}, bf16[2,64,512]{2,1,0:T(8,128)(2,1)S(1)}, u32[]{:S(2)}, u32[]{:S(2)}) collective-permute-start(bf16[2,64,512]{2,1,0:T(8,128)(2,1)S(1)} %enter.1.refs_0_), channel_id=1, source_target_pairs={{0,3},{1,2},{2,1},{3,0},{4,7},{5,6},{6,5},{7,4},{8,11},{9,10},{10,... | collective-permute-start | bytes 393224 | tf_op jit(solution)/shard_map/ppermute | solution.py:22
  16.5 1.4 %copy.11 = bf16[1024,2,256]{0,2,1:T(8,128)(2,1)S(1)} copy(bf16[1024,2,256]{2,1,0:T(2,128)(2,1)S(1)} %copy-done.5) | data formatting | bytes 2097152 | tf_op args[4]
  18.2 1.9 %collective-permute-done.6.refs_3_ = bf16[2,64,512]{2,1,0:T(8,128)(2,1)S(1)} collective-permute-done((bf16[2,64,512]{2,1,0:T(8,128)(2,1)S(1)}, bf16[2,64,512]{2,1,0:T(8,128)(2,1)S(1)}, u32[]{:S(2)}, u32[]{:S(2)}) %collective-permute-start.6) | collective-permute-done | bytes 131104 | tf_op jit(solution)/shard_map/ppermute | solution.py:22
  20.0 5.4 %collective-permute-done.5.refs_2_ = bf16[2,64,512]{2,1,0:T(8,128)(2,1)S(1)} collective-permute-done((bf16[2,64,512]{2,1,0:T(8,128)(2,1)S(1)}, bf16[2,64,512]{2,1,0:T(8,128)(2,1)S(1)}, u32[]{:S(2)}, u32[]{:S(2)}) %collective-permute-start.5) | collective-permute-done | bytes 131104 | tf_op jit(solution)/shard_map/ppermute | solution.py:22
  25.5 3.7 %residual.1 = (f32[4,528,128]{2,1,0:T(8,128)S(1)}, f32[2,2064,128]{2,1,0:T(8,128)S(1)}) custom-call(bf16[2,64,512]{2,1,0:T(8,128)(2,1)S(1)} %enter.1.refs_0_, bf16[2,64,512]{2,1,0:T(8,128)(2,1)S(1)} %collective-permute-done.4.refs_1_, bf16[2,64,512]{2,1,0:T(8,128)(2,1)S(1)} %collective-permute-done.5.refs_2_, ...), custom_call_target="tpu_custom_call" | custom-call | tf_op jit(solution)/shard_map/residual/pallas_call | solution.py:482
  29.4 1.9 %collective-permute-done.7 = f16[2064,128]{1,0:T(8,128)(2,1)S(1)} collective-permute-done((f16[2064,128]{1,0:T(8,128)(2,1)S(1)}, f16[2064,128]{1,0:T(8,128)(2,1)S(1)}, u32[]{:S(2)}, u32[]{:S(2)}) %collective-permute-start.7) | collective-permute-done | bytes 528416 | tf_op jit(solution)/shard_map/ppermute | solution.py:22
  31.6 1.9 %collective-permute-start.10 = (f16[528,128]{1,0:T(8,128)(2,1)S(1)}, f16[528,128]{1,0:T(8,128)(2,1)S(1)}, u32[]{:S(2)}, u32[]{:S(2)}) collective-permute-start(f16[528,128]{1,0:T(8,128)(2,1)S(1)} %get-tuple-element.66), channel_id=1, source_target_pairs={{0,24},{4,28},{8,16},{12,20},{16,8},{20,12},{24,0},{28,4},{1,25},{... | collective-permute-start | bytes 405512 | tf_op jit(solution)/shard_map/ppermute | solution.py:22
  33.9 1.2 %collective-permute-start.8 = (f16[528,128]{1,0:T(8,128)(2,1)S(1)}, f16[528,128]{1,0:T(8,128)(2,1)S(1)}, u32[]{:S(2)}, u32[]{:S(2)}) collective-permute-start(f16[528,128]{1,0:T(8,128)(2,1)S(1)} %get-tuple-element.68), channel_id=1, source_target_pairs={{0,8},{4,12},{8,0},{12,4},{16,24},{20,28},{24,16},{28,20},{1,9},{5... | collective-permute-start | bytes 405512 | tf_op jit(solution)/shard_map/ppermute | solution.py:22
  35.2 2.5 %collective-permute-start.20 = (f16[528,128]{1,0:T(8,128)(2,1)S(1)}, f16[528,128]{1,0:T(8,128)(2,1)S(1)}, u32[]{:S(2)}, u32[]{:S(2)}) collective-permute-start(f16[528,128]{1,0:T(8,128)(2,1)S(1)} %get-tuple-element.63), channel_id=1, source_target_pairs={{0,3},{1,2},{2,1},{3,0},{4,7},{5,6},{6,5},{7,4},{8,11},{9,10},{10,... | collective-permute-start | bytes 405512 | tf_op jit(solution)/shard_map/ppermute | solution.py:22
  37.7 1.3 %collective-permute-done.10 = f16[528,128]{1,0:T(8,128)(2,1)S(1)} collective-permute-done((f16[528,128]{1,0:T(8,128)(2,1)S(1)}, f16[528,128]{1,0:T(8,128)(2,1)S(1)}, u32[]{:S(2)}, u32[]{:S(2)}) %collective-permute-start.10) | collective-permute-done | bytes 135200 | tf_op jit(solution)/shard_map/ppermute | solution.py:22
  39.0 2.1 %collective-permute-done.9 = f16[528,128]{1,0:T(8,128)(2,1)S(1)} collective-permute-done((f16[528,128]{1,0:T(8,128)(2,1)S(1)}, f16[528,128]{1,0:T(8,128)(2,1)S(1)}, u32[]{:S(2)}, u32[]{:S(2)}) %collective-permute-start.9) | collective-permute-done | bytes 135200 | tf_op jit(solution)/shard_map/ppermute | solution.py:22
  41.5 1.6 %collective-permute-start.13 = (f16[512,128]{1,0:T(8,128)(2,1)S(1)}, f16[512,128]{1,0:T(8,128)(2,1)S(1)}, u32[]{:S(2)}, u32[]{:S(2)}) collective-permute-start(f16[512,128]{1,0:T(8,128)(2,1)S(1)} %convert_element_type.102), channel_id=1, source_target_pairs={{0,24},{4,28},{8,16},{12,20},{16,8},{20,12},{24,0},{28,4},{1,25},{... | collective-permute-start | bytes 393224 | tf_op jit(solution)/shard_map/ppermute | solution.py:22
  43.8 1.3 %collective-permute-start.11 = (f16[512,128]{1,0:T(8,128)(2,1)S(1)}, f16[512,128]{1,0:T(8,128)(2,1)S(1)}, u32[]{:S(2)}, u32[]{:S(2)}) collective-permute-start(f16[512,128]{1,0:T(8,128)(2,1)S(1)} %convert_element_type.102), channel_id=1, source_target_pairs={{0,8},{4,12},{8,0},{12,4},{16,24},{20,28},{24,16},{28,20},{1,9},{5... | collective-permute-start | bytes 393224 | tf_op jit(solution)/shard_map/ppermute | solution.py:22
  45.1 1.2 %collective-permute-start.18 = (f16[528,128]{1,0:T(8,128)(2,1)S(1)}, f16[528,128]{1,0:T(8,128)(2,1)S(1)}, u32[]{:S(2)}, u32[]{:S(2)}) collective-permute-start(f16[528,128]{1,0:T(8,128)(2,1)S(1)} %get-tuple-element.65), channel_id=1, source_target_pairs={{0,1},{1,0},{2,3},{3,2},{4,5},{5,4},{6,7},{7,6},{8,9},{9,8},{10,11... | collective-permute-start | bytes 405512 | tf_op jit(solution)/shard_map/ppermute | solution.py:22
  46.3 2.0 %collective-permute-done.19 = f16[528,128]{1,0:T(8,128)(2,1)S(1)} collective-permute-done((f16[528,128]{1,0:T(8,128)(2,1)S(1)}, f16[528,128]{1,0:T(8,128)(2,1)S(1)}, u32[]{:S(2)}, u32[]{:S(2)}) %collective-permute-start.19) | collective-permute-done | bytes 135200 | tf_op jit(solution)/shard_map/ppermute | solution.py:22
  48.8 1.7 %collective-permute-done.12 = f16[512,128]{1,0:T(8,128)(2,1)S(1)} collective-permute-done((f16[512,128]{1,0:T(8,128)(2,1)S(1)}, f16[512,128]{1,0:T(8,128)(2,1)S(1)}, u32[]{:S(2)}, u32[]{:S(2)}) %collective-permute-start.12) | collective-permute-done | bytes 131104 | tf_op jit(solution)/shard_map/ppermute | solution.py:22
  53.0 1.8 %collective-permute-start.24 = (f32[5,64]{1,0:T(8,128)S(1)}, f32[5,64]{1,0:T(8,128)S(1)}, u32[]{:S(2)}, u32[]{:S(2)}) collective-permute-start(f32[5,64]{1,0:T(8,128)S(1)} %shard_map.86.refs_13_), channel_id=1, source_target_pairs={{0,24},{4,28},{8,16},{12,20},{16,8},{20,12},{24,0},{28,4},{1,25},{... | collective-permute-start | bytes 3848 | tf_op jit(solution)/shard_map/ppermute | solution.py:22
  55.4 1.2 %collective-permute-start.22 = (f32[5,64]{1,0:T(8,128)S(1)}, f32[5,64]{1,0:T(8,128)S(1)}, u32[]{:S(2)}, u32[]{:S(2)}) collective-permute-start(f32[5,64]{1,0:T(8,128)S(1)} %shard_map.86.refs_13_), channel_id=1, source_target_pairs={{0,8},{4,12},{8,0},{12,4},{16,24},{20,28},{24,16},{28,20},{1,9},{5... | collective-permute-start | bytes 3848 | tf_op jit(solution)/shard_map/ppermute | solution.py:22
  57.6 0.9 %collective-permute-done.23.refs_15_ = f32[5,64]{1,0:T(8,128)S(1)} collective-permute-done((f32[5,64]{1,0:T(8,128)S(1)}, f32[5,64]{1,0:T(8,128)S(1)}, u32[]{:S(2)}, u32[]{:S(2)}) %collective-permute-start.23) | collective-permute-done | bytes 1312 | tf_op jit(solution)/shard_map/ppermute | solution.py:22
  59.0 2.0 %leave.1 = (f32[512,128]{1,0:T(8,128)}, f32[2]{0:T(128)}, f32[4096,128]{1,0:T(8,128)}) custom-call(f32[512,128]{1,0:T(8,128)S(1)} %get-tuple-element.76.refs_0_, f32[512,128]{1,0:T(8,128)S(1)} %get-tuple-element.70.refs_1_, f32[512,128]{1,0:T(8,128)S(1)} %get-tuple-element.71.refs_2_, f32[512,128]{1,0:T(8,128)S(1)} %get-tuple-element.72.refs_3_, ...), custom_call_target="tpu_custom_call" | custom-call | tf_op jit(solution)/shard_map/leave/pallas_call | solution.py:561
  (65 shorter events, 11.7 us)
Async XLA Ops:
  4.1 5.8 %collective-permute-start.3 = (f32[3,64]{1,0:T(4,128)S(1)}, f32[3,64]{1,0:T(4,128)S(1)}, u32[]{:S(2)}, u32[]{:S(2)}) collective-permute-start(f32[3,64]{1,0:T(4,128)S(1)} %shard_map.85.refs_0_), channel_id=1, source_target_pairs={{0,24},{4,28},{8,16},{12,20},{16,8},{20,12},{24,0},{28,4},{1,25},{... | collective-permute-start | bytes 2312 | tf_op jit(solution)/shard_map/ppermute | solution.py:22
  7.9 3.6 %collective-permute-start.2 = (f32[3,64]{1,0:T(4,128)S(1)}, f32[3,64]{1,0:T(4,128)S(1)}, u32[]{:S(2)}, u32[]{:S(2)}) collective-permute-start(f32[3,64]{1,0:T(4,128)S(1)} %shard_map.85.refs_0_), channel_id=1, source_target_pairs={{0,16},{4,20},{8,24},{12,28},{16,0},{20,4},{24,8},{28,12},{1,17},{... | collective-permute-start | bytes 2312 | tf_op jit(solution)/shard_map/ppermute | solution.py:22
  8.4 3.6 %collective-permute-start.1 = (f32[3,64]{1,0:T(4,128)S(1)}, f32[3,64]{1,0:T(4,128)S(1)}, u32[]{:S(2)}, u32[]{:S(2)}) collective-permute-start(f32[3,64]{1,0:T(4,128)S(1)} %shard_map.85.refs_0_), channel_id=1, source_target_pairs={{0,8},{4,12},{8,0},{12,4},{16,24},{20,28},{24,16},{28,20},{1,9},{5... | collective-permute-start | bytes 2312 | tf_op jit(solution)/shard_map/ppermute | solution.py:22
  12.1 8.0 %collective-permute-start.6 = (bf16[2,64,512]{2,1,0:T(8,128)(2,1)S(1)}, bf16[2,64,512]{2,1,0:T(8,128)(2,1)S(1)}, u32[]{:S(2)}, u32[]{:S(2)}) collective-permute-start(bf16[2,64,512]{2,1,0:T(8,128)(2,1)S(1)} %enter.1.refs_0_), channel_id=1, source_target_pairs={{0,3},{1,2},{2,1},{3,0},{4,7},{5,6},{6,5},{7,4},{8,11},{9,10},{10,... | collective-permute-start | bytes 393224 | tf_op jit(solution)/shard_map/ppermute | solution.py:22
  15.8 9.7 %collective-permute-start.5 = (bf16[2,64,512]{2,1,0:T(8,128)(2,1)S(1)}, bf16[2,64,512]{2,1,0:T(8,128)(2,1)S(1)}, u32[]{:S(2)}, u32[]{:S(2)}) collective-permute-start(bf16[2,64,512]{2,1,0:T(8,128)(2,1)S(1)} %enter.1.refs_0_), channel_id=1, source_target_pairs={{0,2},{1,3},{2,0},{3,1},{4,6},{5,7},{6,4},{7,5},{8,10},{9,11},{10,... | collective-permute-start | bytes 393224 | tf_op jit(solution)/shard_map/ppermute | solution.py:22
  15.8 9.7 %collective-permute-start.4 = (bf16[2,64,512]{2,1,0:T(8,128)(2,1)S(1)}, bf16[2,64,512]{2,1,0:T(8,128)(2,1)S(1)}, u32[]{:S(2)}, u32[]{:S(2)}) collective-permute-start(bf16[2,64,512]{2,1,0:T(8,128)(2,1)S(1)} %enter.1.refs_0_), channel_id=1, source_target_pairs={{0,1},{1,0},{2,3},{3,2},{4,5},{5,4},{6,7},{7,6},{8,9},{9,8},{10,11... | collective-permute-start | bytes 393224 | tf_op jit(solution)/shard_map/ppermute | solution.py:22
  29.3 2.0 %collective-permute-start.7 = (f16[2064,128]{1,0:T(8,128)(2,1)S(1)}, f16[2064,128]{1,0:T(8,128)(2,1)S(1)}, u32[]{:S(2)}, u32[]{:S(2)}) collective-permute-start(f16[2064,128]{1,0:T(8,128)(2,1)S(1)} %fusion), channel_id=1, source_target_pairs={{0,4},{4,0},{8,12},{12,8},{16,20},{20,16},{24,28},{28,24},{1,5},{5... | collective-permute-start | bytes 1585160 | tf_op jit(solution)/shard_map/ppermute | solution.py:22
  31.6 7.4 %collective-permute-start.10 = (f16[528,128]{1,0:T(8,128)(2,1)S(1)}, f16[528,128]{1,0:T(8,128)(2,1)S(1)}, u32[]{:S(2)}, u32[]{:S(2)}) collective-permute-start(f16[528,128]{1,0:T(8,128)(2,1)S(1)} %get-tuple-element.66), channel_id=1, source_target_pairs={{0,24},{4,28},{8,16},{12,20},{16,8},{20,12},{24,0},{28,4},{1,25},{... | collective-permute-start | bytes 405512 | tf_op jit(solution)/shard_map/ppermute | solution.py:22
  33.4 7.7 %collective-permute-start.9 = (f16[528,128]{1,0:T(8,128)(2,1)S(1)}, f16[528,128]{1,0:T(8,128)(2,1)S(1)}, u32[]{:S(2)}, u32[]{:S(2)}) collective-permute-start(f16[528,128]{1,0:T(8,128)(2,1)S(1)} %get-tuple-element.67), channel_id=1, source_target_pairs={{0,16},{4,20},{8,24},{12,28},{16,0},{20,4},{24,8},{28,12},{1,17},{... | collective-permute-start | bytes 405512 | tf_op jit(solution)/shard_map/ppermute | solution.py:22
  33.9 7.5 %collective-permute-start.8 = (f16[528,128]{1,0:T(8,128)(2,1)S(1)}, f16[528,128]{1,0:T(8,128)(2,1)S(1)}, u32[]{:S(2)}, u32[]{:S(2)}) collective-permute-start(f16[528,128]{1,0:T(8,128)(2,1)S(1)} %get-tuple-element.68), channel_id=1, source_target_pairs={{0,8},{4,12},{8,0},{12,4},{16,24},{20,28},{24,16},{28,20},{1,9},{5... | collective-permute-start | bytes 405512 | tf_op jit(solution)/shard_map/ppermute | solution.py:22
  35.2 9.9 %collective-permute-start.20 = (f16[528,128]{1,0:T(8,128)(2,1)S(1)}, f16[528,128]{1,0:T(8,128)(2,1)S(1)}, u32[]{:S(2)}, u32[]{:S(2)}) collective-permute-start(f16[528,128]{1,0:T(8,128)(2,1)S(1)} %get-tuple-element.63), channel_id=1, source_target_pairs={{0,3},{1,2},{2,1},{3,0},{4,7},{5,6},{6,5},{7,4},{8,11},{9,10},{10,... | collective-permute-start | bytes 405512 | tf_op jit(solution)/shard_map/ppermute | solution.py:22
  37.7 10.6 %collective-permute-start.19 = (f16[528,128]{1,0:T(8,128)(2,1)S(1)}, f16[528,128]{1,0:T(8,128)(2,1)S(1)}, u32[]{:S(2)}, u32[]{:S(2)}) collective-permute-start(f16[528,128]{1,0:T(8,128)(2,1)S(1)} %get-tuple-element.64), channel_id=1, source_target_pairs={{0,2},{1,3},{2,0},{3,1},{4,6},{5,7},{6,4},{7,5},{8,10},{9,11},{10,... | collective-permute-start | bytes 405512 | tf_op jit(solution)/shard_map/ppermute | solution.py:22
  41.5 7.3 %collective-permute-start.13 = (f16[512,128]{1,0:T(8,128)(2,1)S(1)}, f16[512,128]{1,0:T(8,128)(2,1)S(1)}, u32[]{:S(2)}, u32[]{:S(2)}) collective-permute-start(f16[512,128]{1,0:T(8,128)(2,1)S(1)} %convert_element_type.102), channel_id=1, source_target_pairs={{0,24},{4,28},{8,16},{12,20},{16,8},{20,12},{24,0},{28,4},{1,25},{... | collective-permute-start | bytes 393224 | tf_op jit(solution)/shard_map/ppermute | solution.py:22
  43.1 7.4 %collective-permute-start.12 = (f16[512,128]{1,0:T(8,128)(2,1)S(1)}, f16[512,128]{1,0:T(8,128)(2,1)S(1)}, u32[]{:S(2)}, u32[]{:S(2)}) collective-permute-start(f16[512,128]{1,0:T(8,128)(2,1)S(1)} %convert_element_type.102), channel_id=1, source_target_pairs={{0,16},{4,20},{8,24},{12,28},{16,0},{20,4},{24,8},{28,12},{1,17},{... | collective-permute-start | bytes 393224 | tf_op jit(solution)/shard_map/ppermute | solution.py:22
  43.8 6.8 %collective-permute-start.11 = (f16[512,128]{1,0:T(8,128)(2,1)S(1)}, f16[512,128]{1,0:T(8,128)(2,1)S(1)}, u32[]{:S(2)}, u32[]{:S(2)}) collective-permute-start(f16[512,128]{1,0:T(8,128)(2,1)S(1)} %convert_element_type.102), channel_id=1, source_target_pairs={{0,8},{4,12},{8,0},{12,4},{16,24},{20,28},{24,16},{28,20},{1,9},{5... | collective-permute-start | bytes 393224 | tf_op jit(solution)/shard_map/ppermute | solution.py:22
  45.1 6.0 %collective-permute-start.18 = (f16[528,128]{1,0:T(8,128)(2,1)S(1)}, f16[528,128]{1,0:T(8,128)(2,1)S(1)}, u32[]{:S(2)}, u32[]{:S(2)}) collective-permute-start(f16[528,128]{1,0:T(8,128)(2,1)S(1)} %get-tuple-element.65), channel_id=1, source_target_pairs={{0,1},{1,0},{2,3},{3,2},{4,5},{5,4},{6,7},{7,6},{8,9},{9,8},{10,11... | collective-permute-start | bytes 405512 | tf_op jit(solution)/shard_map/ppermute | solution.py:22
  48.3 6.5 %collective-permute-start.14 = (f16[512,128]{1,0:T(8,128)(2,1)S(1)}, f16[512,128]{1,0:T(8,128)(2,1)S(1)}, u32[]{:S(2)}, u32[]{:S(2)}) collective-permute-start(f16[512,128]{1,0:T(8,128)(2,1)S(1)} %convert_element_type.102), channel_id=1, source_target_pairs={{0,4},{4,0},{8,12},{12,8},{16,20},{20,16},{24,28},{28,24},{1,5},{5... | collective-permute-start | bytes 393224 | tf_op jit(solution)/shard_map/ppermute | solution.py:22
  48.8 6.5 %collective-permute-start.17 = (f16[512,128]{1,0:T(8,128)(2,1)S(1)}, f16[512,128]{1,0:T(8,128)(2,1)S(1)}, u32[]{:S(2)}, u32[]{:S(2)}) collective-permute-start(f16[512,128]{1,0:T(8,128)(2,1)S(1)} %collective-permute-done.13), channel_id=1, source_target_pairs={{0,4},{4,0},{8,12},{12,8},{16,20},{20,16},{24,28},{28,24},{1,5},{5... | collective-permute-start | bytes 393224 | tf_op jit(solution)/shard_map/ppermute | solution.py:22
  50.5 6.0 %collective-permute-start.16 = (f16[512,128]{1,0:T(8,128)(2,1)S(1)}, f16[512,128]{1,0:T(8,128)(2,1)S(1)}, u32[]{:S(2)}, u32[]{:S(2)}) collective-permute-start(f16[512,128]{1,0:T(8,128)(2,1)S(1)} %collective-permute-done.12), channel_id=1, source_target_pairs={{0,4},{4,0},{8,12},{12,8},{16,20},{20,16},{24,28},{28,24},{1,5},{5... | collective-permute-start | bytes 393224 | tf_op jit(solution)/shard_map/ppermute | solution.py:22
  50.5 6.0 %collective-permute-start.15 = (f16[512,128]{1,0:T(8,128)(2,1)S(1)}, f16[512,128]{1,0:T(8,128)(2,1)S(1)}, u32[]{:S(2)}, u32[]{:S(2)}) collective-permute-start(f16[512,128]{1,0:T(8,128)(2,1)S(1)} %collective-permute-done.11), channel_id=1, source_target_pairs={{0,4},{4,0},{8,12},{12,8},{16,20},{20,16},{24,28},{28,24},{1,5},{5... | collective-permute-start | bytes 393224 | tf_op jit(solution)/shard_map/ppermute | solution.py:22
  51.3 1.6 %collective-permute-start.21 = (f32[5,64]{1,0:T(8,128)S(1)}, f32[5,64]{1,0:T(8,128)S(1)}, u32[]{:S(2)}, u32[]{:S(2)}) collective-permute-start(f32[5,64]{1,0:T(8,128)S(1)} %get-tuple-element.59.summary), channel_id=1, source_target_pairs={{0,4},{4,0},{8,12},{12,8},{16,20},{20,16},{24,28},{28,24},{1,5},{5... | collective-permute-start | bytes 3848 | tf_op jit(solution)/shard_map/ppermute | solution.py:22
  53.0 4.6 %collective-permute-start.24 = (f32[5,64]{1,0:T(8,128)S(1)}, f32[5,64]{1,0:T(8,128)S(1)}, u32[]{:S(2)}, u32[]{:S(2)}) collective-permute-start(f32[5,64]{1,0:T(8,128)S(1)} %shard_map.86.refs_13_), channel_id=1, source_target_pairs={{0,24},{4,28},{8,16},{12,20},{16,8},{20,12},{24,0},{28,4},{1,25},{... | collective-permute-start | bytes 3848 | tf_op jit(solution)/shard_map/ppermute | solution.py:22
  54.8 3.6 %collective-permute-start.23 = (f32[5,64]{1,0:T(8,128)S(1)}, f32[5,64]{1,0:T(8,128)S(1)}, u32[]{:S(2)}, u32[]{:S(2)}) collective-permute-start(f32[5,64]{1,0:T(8,128)S(1)} %shard_map.86.refs_13_), channel_id=1, source_target_pairs={{0,16},{4,20},{8,24},{12,28},{16,0},{20,4},{24,8},{28,12},{1,17},{... | collective-permute-start | bytes 3848 | tf_op jit(solution)/shard_map/ppermute | solution.py:22
  55.4 3.6 %collective-permute-start.22 = (f32[5,64]{1,0:T(8,128)S(1)}, f32[5,64]{1,0:T(8,128)S(1)}, u32[]{:S(2)}, u32[]{:S(2)}) collective-permute-start(f32[5,64]{1,0:T(8,128)S(1)} %shard_map.86.refs_13_), channel_id=1, source_target_pairs={{0,8},{4,12},{8,0},{12,4},{16,24},{20,28},{24,16},{28,20},{1,9},{5... | collective-permute-start | bytes 3848 | tf_op jit(solution)/shard_map/ppermute | solution.py:22
  (7 other events, 33.4 us)

commit v4 on v3

--- a/solution.py
+++ b/solution.py
@@ -375,7 +375,7 @@
 
 def leave_kernel(draws, tiles, cells, count, *refs):
     pieces, refs = refs[:count], refs[count:]
-    (local, fade, weight, innov), climb, (near, density, far, out, sems) = refs[:4], refs[4:-5], refs[-5:]
+    (local, fade, weight, innov), climb, (near, told, far, out, density, sems) = refs[:4], refs[4:-6], refs[-6:]
     lines, chips = pieces[0].shape[0], count // 2
     mine = lax.axis_index("tm")
     moves = []
@@ -391,6 +391,8 @@
     columns = [to_column(arriving[d:d + 1, :], same) for d in range(draws)]
     for d in range(draws):
         density[d] = jnp.max(summed[d:d + 1, :]) * (1.0 / cells)
+    moves.append(pltpu.make_async_copy(density, told, sems.at[count + 1]))
+    moves[-1].start()
     for j in range(tiles):
         part = slice(j * LANES, (j + 1) * LANES)
         for d in range(draws):
@@ -562,8 +564,8 @@
         functools.partial(leave_kernel, draws, tiles, float(spans * parts), 2 * chips),
         out_shape=(shape(innov.shape, f32), shape((draws,), f32), shape((size, LANES), f32)),
         in_specs=[whole] * (2 * chips + 4 + len(climb)),
-        out_specs=(distant, pl.BlockSpec(memory_space=pltpu.SMEM), distant),
-        scratch_shapes=[pltpu.VMEM(innov.shape, f32), pltpu.SemaphoreType.DMA((2 * chips + 1,))],
+        out_specs=(distant, distant, distant),
+        scratch_shapes=[pltpu.VMEM(innov.shape, f32), pltpu.SMEM((draws,), f32), pltpu.SemaphoreType.DMA((2 * chips + 2,))],
         name="leave",
         compiler_params=room(6),
     )(*[value.astype(f32) * factor for value in totals + passed], local_adjoint, fade, weight, innov, *climb)

time: 61.1 us -> 60.6 us (level)
  no operation moved by 1% of the time
where the time goes in v4:
time: 60.6 us; the launch traced here: 60.5 us
  starting transfers between devices  24.5 us (40%)
  waiting for transfers between devices  22.2 us (37%)
  Pallas kernels  9.56 us (16%)
  local copies, waits for them, and re-layouts  2.81 us (5%)
  between operations  0.89 us (1%)
    ppermute x25, starting transfers between devices, swap(): return lax.ppermute(value, axis, [(i, i ^ key) for i in range(count)])  24.5 us
    ppermute x25, waiting for transfers between devices, swap(): return lax.ppermute(value, axis, [(i, i ^ key) for i in range(count)])  22.2 us
    pallas_call x1, Pallas kernels, local(): pl.pallas_call(functools.partial(residual_kernel, draws, parts, series //...  3.73 us
    unnamed x14, local copies, waits for them, and re-layouts  2.81 us
    pallas_call x1, Pallas kernels, local(): pl.pallas_call(functools.partial(leave_kernel, draws, tiles, float(spans...  1.5 us
    pallas_call x1, Pallas kernels, local(): pl.pallas_call(functools.partial(forward_kernel, draws, tiles), out_shape...  1.4 us
  transfers between devices with their start and end apart: 25, of which 15 were waited for; matrix products, arithmetic and copies ran while one was open for 3% of the time, Pallas kernels for 5%

profile of v4, /device:TPU:0, one launch (start us, length us, event | category | flops | bytes accessed | tf_op | source)
XLA Modules:
  0.0 60.5 jit_solution(10915527085100902720)
XLA Ops:
  0.7 0.9 %copy-done.4 = f32[64,512]{1,0:T(8,128)S(1)} copy-done((f32[64,512]{1,0:T(8,128)S(1)}, f32[64,512]{1,0:T(8,128)}, u32[]{:S(2)}) %copy-start.4) | copy-done | bytes 131096
  4.1 3.8 %collective-permute-start.3 = (f32[3,64]{1,0:T(4,128)S(1)}, f32[3,64]{1,0:T(4,128)S(1)}, u32[]{:S(2)}, u32[]{:S(2)}) collective-permute-start(f32[3,64]{1,0:T(4,128)S(1)} %shard_map.85.refs_0_), channel_id=1, source_target_pairs={{0,24},{4,28},{8,16},{12,20},{16,8},{20,12},{24,0},{28,4},{1,25},{... | collective-permute-start | bytes 2312 | tf_op jit(solution)/shard_map/ppermute | solution.py:22
  8.5 1.4 %forward_scan.1 = (f32[2,64,512]{2,1,0:T(8,128)S(1)}, f32[64,512]{1,0:T(8,128)S(1)}) custom-call(f32[64,512]{1,0:T(8,128)S(1)} %get-tuple-element.34.decay, f32[2,64,512]{2,1,0:T(8,128)S(1)} %get-tuple-element.38.pushed), custom_call_target="tpu_custom_call" | custom-call | tf_op jit(solution)/shard_map/forward_scan/pallas_call | solution.py:462
  9.9 1.5 %collective-permute-done.2.refs_2_ = f32[3,64]{1,0:T(4,128)S(1)} collective-permute-done((f32[3,64]{1,0:T(4,128)S(1)}, f32[3,64]{1,0:T(4,128)S(1)}, u32[]{:S(2)}, u32[]{:S(2)}) %collective-permute-start.2) | collective-permute-done | bytes 800 | tf_op jit(solution)/shard_map/ppermute | solution.py:22
  12.1 3.7 %collective-permute-start.6 = (bf16[2,64,512]{2,1,0:T(8,128)(2,1)S(1)}, bf16[2,64,512]{2,1,0:T(8,128)(2,1)S(1)}, u32[]{:S(2)}, u32[]{:S(2)}) collective-permute-start(bf16[2,64,512]{2,1,0:T(8,128)(2,1)S(1)} %enter.1.refs_0_), channel_id=1, source_target_pairs={{0,3},{1,2},{2,1},{3,0},{4,7},{5,6},{6,5},{7,4},{8,11},{9,10},{10,... | collective-permute-start | bytes 393224 | tf_op jit(solution)/shard_map/ppermute | solution.py:22
  16.5 1.4 %copy.11 = bf16[1024,2,256]{0,2,1:T(8,128)(2,1)S(1)} copy(bf16[1024,2,256]{2,1,0:T(2,128)(2,1)S(1)} %copy-done.5) | data formatting | bytes 2097152 | tf_op args[4]
  18.2 1.9 %collective-permute-done.6.refs_3_ = bf16[2,64,512]{2,1,0:T(8,128)(2,1)S(1)} collective-permute-done((bf16[2,64,512]{2,1,0:T(8,128)(2,1)S(1)}, bf16[2,64,512]{2,1,0:T(8,128)(2,1)S(1)}, u32[]{:S(2)}, u32[]{:S(2)}) %collective-permute-start.6) | collective-permute-done | bytes 131104 | tf_op jit(solution)/shard_map/ppermute | solution.py:22
  20.0 5.4 %collective-permute-done.5.refs_2_ = bf16[2,64,512]{2,1,0:T(8,128)(2,1)S(1)} collective-permute-done((bf16[2,64,512]{2,1,0:T(8,128)(2,1)S(1)}, bf16[2,64,512]{2,1,0:T(8,128)(2,1)S(1)}, u32[]{:S(2)}, u32[]{:S(2)}) %collective-permute-start.5) | collective-permute-done | bytes 131104 | tf_op jit(solution)/shard_map/ppermute | solution.py:22
  25.5 3.7 %residual.1 = (f32[4,528,128]{2,1,0:T(8,128)S(1)}, f32[2,2064,128]{2,1,0:T(8,128)S(1)}) custom-call(bf16[2,64,512]{2,1,0:T(8,128)(2,1)S(1)} %enter.1.refs_0_, bf16[2,64,512]{2,1,0:T(8,128)(2,1)S(1)} %collective-permute-done.4.refs_1_, bf16[2,64,512]{2,1,0:T(8,128)(2,1)S(1)} %collective-permute-done.5.refs_2_, ...), custom_call_target="tpu_custom_call" | custom-call | tf_op jit(solution)/shard_map/residual/pallas_call | solution.py:484
  29.4 1.9 %collective-permute-done.7 = f16[2064,128]{1,0:T(8,128)(2,1)S(1)} collective-permute-done((f16[2064,128]{1,0:T(8,128)(2,1)S(1)}, f16[2064,128]{1,0:T(8,128)(2,1)S(1)}, u32[]{:S(2)}, u32[]{:S(2)}) %collective-permute-start.7) | collective-permute-done | bytes 528416 | tf_op jit(solution)/shard_map/ppermute | solution.py:22
  31.6 1.9 %collective-permute-start.10 = (f16[528,128]{1,0:T(8,128)(2,1)S(1)}, f16[528,128]{1,0:T(8,128)(2,1)S(1)}, u32[]{:S(2)}, u32[]{:S(2)}) collective-permute-start(f16[528,128]{1,0:T(8,128)(2,1)S(1)} %get-tuple-element.66), channel_id=1, source_target_pairs={{0,24},{4,28},{8,16},{12,20},{16,8},{20,12},{24,0},{28,4},{1,25},{... | collective-permute-start | bytes 405512 | tf_op jit(solution)/shard_map/ppermute | solution.py:22
  33.9 1.2 %collective-permute-start.8 = (f16[528,128]{1,0:T(8,128)(2,1)S(1)}, f16[528,128]{1,0:T(8,128)(2,1)S(1)}, u32[]{:S(2)}, u32[]{:S(2)}) collective-permute-start(f16[528,128]{1,0:T(8,128)(2,1)S(1)} %get-tuple-element.68), channel_id=1, source_target_pairs={{0,8},{4,12},{8,0},{12,4},{16,24},{20,28},{24,16},{28,20},{1,9},{5... | collective-permute-start | bytes 405512 | tf_op jit(solution)/shard_map/ppermute | solution.py:22
  35.2 2.5 %collective-permute-start.20 = (f16[528,128]{1,0:T(8,128)(2,1)S(1)}, f16[528,128]{1,0:T(8,128)(2,1)S(1)}, u32[]{:S(2)}, u32[]{:S(2)}) collective-permute-start(f16[528,128]{1,0:T(8,128)(2,1)S(1)} %get-tuple-element.63), channel_id=1, source_target_pairs={{0,3},{1,2},{2,1},{3,0},{4,7},{5,6},{6,5},{7,4},{8,11},{9,10},{10,... | collective-permute-start | bytes 405512 | tf_op jit(solution)/shard_map/ppermute | solution.py:22
  37.7 1.3 %collective-permute-done.10 = f16[528,128]{1,0:T(8,128)(2,1)S(1)} collective-permute-done((f16[528,128]{1,0:T(8,128)(2,1)S(1)}, f16[528,128]{1,0:T(8,128)(2,1)S(1)}, u32[]{:S(2)}, u32[]{:S(2)}) %collective-permute-start.10) | collective-permute-done | bytes 135200 | tf_op jit(solution)/shard_map/ppermute | solution.py:22
  39.0 2.1 %collective-permute-done.9 = f16[528,128]{1,0:T(8,128)(2,1)S(1)} collective-permute-done((f16[528,128]{1,0:T(8,128)(2,1)S(1)}, f16[528,128]{1,0:T(8,128)(2,1)S(1)}, u32[]{:S(2)}, u32[]{:S(2)}) %collective-permute-start.9) | collective-permute-done | bytes 135200 | tf_op jit(solution)/shard_map/ppermute | solution.py:22
  41.5 1.6 %collective-permute-start.13 = (f16[512,128]{1,0:T(8,128)(2,1)S(1)}, f16[512,128]{1,0:T(8,128)(2,1)S(1)}, u32[]{:S(2)}, u32[]{:S(2)}) collective-permute-start(f16[512,128]{1,0:T(8,128)(2,1)S(1)} %convert_element_type.102), channel_id=1, source_target_pairs={{0,24},{4,28},{8,16},{12,20},{16,8},{20,12},{24,0},{28,4},{1,25},{... | collective-permute-start | bytes 393224 | tf_op jit(solution)/shard_map/ppermute | solution.py:22
  43.8 1.3 %collective-permute-start.11 = (f16[512,128]{1,0:T(8,128)(2,1)S(1)}, f16[512,128]{1,0:T(8,128)(2,1)S(1)}, u32[]{:S(2)}, u32[]{:S(2)}) collective-permute-start(f16[512,128]{1,0:T(8,128)(2,1)S(1)} %convert_element_type.102), channel_id=1, source_target_pairs={{0,8},{4,12},{8,0},{12,4},{16,24},{20,28},{24,16},{28,20},{1,9},{5... | collective-permute-start | bytes 393224 | tf_op jit(solution)/shard_map/ppermute | solution.py:22
  45.1 1.2 %collective-permute-start.18 = (f16[528,128]{1,0:T(8,128)(2,1)S(1)}, f16[528,128]{1,0:T(8,128)(2,1)S(1)}, u32[]{:S(2)}, u32[]{:S(2)}) collective-permute-start(f16[528,128]{1,0:T(8,128)(2,1)S(1)} %get-tuple-element.65), channel_id=1, source_target_pairs={{0,1},{1,0},{2,3},{3,2},{4,5},{5,4},{6,7},{7,6},{8,9},{9,8},{10,11... | collective-permute-start | bytes 405512 | tf_op jit(solution)/shard_map/ppermute | solution.py:22
  46.3 2.0 %collective-permute-done.19 = f16[528,128]{1,0:T(8,128)(2,1)S(1)} collective-permute-done((f16[528,128]{1,0:T(8,128)(2,1)S(1)}, f16[528,128]{1,0:T(8,128)(2,1)S(1)}, u32[]{:S(2)}, u32[]{:S(2)}) %collective-permute-start.19) | collective-permute-done | bytes 135200 | tf_op jit(solution)/shard_map/ppermute | solution.py:22
  48.8 1.7 %collective-permute-done.12 = f16[512,128]{1,0:T(8,128)(2,1)S(1)} collective-permute-done((f16[512,128]{1,0:T(8,128)(2,1)S(1)}, f16[512,128]{1,0:T(8,128)(2,1)S(1)}, u32[]{:S(2)}, u32[]{:S(2)}) %collective-permute-start.12) | collective-permute-done | bytes 131104 | tf_op jit(solution)/shard_map/ppermute | solution.py:22
  53.0 1.8 %collective-permute-start.24 = (f32[5,64]{1,0:T(8,128)S(1)}, f32[5,64]{1,0:T(8,128)S(1)}, u32[]{:S(2)}, u32[]{:S(2)}) collective-permute-start(f32[5,64]{1,0:T(8,128)S(1)} %shard_map.86.refs_13_), channel_id=1, source_target_pairs={{0,24},{4,28},{8,16},{12,20},{16,8},{20,12},{24,0},{28,4},{1,25},{... | collective-permute-start | bytes 3848 | tf_op jit(solution)/shard_map/ppermute | solution.py:22
  55.4 1.2 %collective-permute-start.22 = (f32[5,64]{1,0:T(8,128)S(1)}, f32[5,64]{1,0:T(8,128)S(1)}, u32[]{:S(2)}, u32[]{:S(2)}) collective-permute-start(f32[5,64]{1,0:T(8,128)S(1)} %shard_map.86.refs_13_), channel_id=1, source_target_pairs={{0,8},{4,12},{8,0},{12,4},{16,24},{20,28},{24,16},{28,20},{1,9},{5... | collective-permute-start | bytes 3848 | tf_op jit(solution)/shard_map/ppermute | solution.py:22
  57.6 0.9 %collective-permute-done.23.refs_15_ = f32[5,64]{1,0:T(8,128)S(1)} collective-permute-done((f32[5,64]{1,0:T(8,128)S(1)}, f32[5,64]{1,0:T(8,128)S(1)}, u32[]{:S(2)}, u32[]{:S(2)}) %collective-permute-start.23) | collective-permute-done | bytes 1312 | tf_op jit(solution)/shard_map/ppermute | solution.py:22
  59.0 1.5 %leave.1 = (f32[512,128]{1,0:T(8,128)}, f32[2]{0:T(128)}, f32[4096,128]{1,0:T(8,128)}) custom-call(f32[512,128]{1,0:T(8,128)S(1)} %get-tuple-element.76.refs_0_, f32[512,128]{1,0:T(8,128)S(1)} %get-tuple-element.70.refs_1_, f32[512,128]{1,0:T(8,128)S(1)} %get-tuple-element.71.refs_2_, f32[512,128]{1,0:T(8,128)S(1)} %get-tuple-element.72.refs_3_, ...), custom_call_target="tpu_custom_call" | custom-call | tf_op jit(solution)/shard_map/leave/pallas_call | solution.py:563
  (65 shorter events, 11.7 us)
Async XLA Ops:
  4.1 5.8 %collective-permute-start.3 = (f32[3,64]{1,0:T(4,128)S(1)}, f32[3,64]{1,0:T(4,128)S(1)}, u32[]{:S(2)}, u32[]{:S(2)}) collective-permute-start(f32[3,64]{1,0:T(4,128)S(1)} %shard_map.85.refs_0_), channel_id=1, source_target_pairs={{0,24},{4,28},{8,16},{12,20},{16,8},{20,12},{24,0},{28,4},{1,25},{... | collective-permute-start | bytes 2312 | tf_op jit(solution)/shard_map/ppermute | solution.py:22
  7.9 3.6 %collective-permute-start.2 = (f32[3,64]{1,0:T(4,128)S(1)}, f32[3,64]{1,0:T(4,128)S(1)}, u32[]{:S(2)}, u32[]{:S(2)}) collective-permute-start(f32[3,64]{1,0:T(4,128)S(1)} %shard_map.85.refs_0_), channel_id=1, source_target_pairs={{0,16},{4,20},{8,24},{12,28},{16,0},{20,4},{24,8},{28,12},{1,17},{... | collective-permute-start | bytes 2312 | tf_op jit(solution)/shard_map/ppermute | solution.py:22
  8.4 3.6 %collective-permute-start.1 = (f32[3,64]{1,0:T(4,128)S(1)}, f32[3,64]{1,0:T(4,128)S(1)}, u32[]{:S(2)}, u32[]{:S(2)}) collective-permute-start(f32[3,64]{1,0:T(4,128)S(1)} %shard_map.85.refs_0_), channel_id=1, source_target_pairs={{0,8},{4,12},{8,0},{12,4},{16,24},{20,28},{24,16},{28,20},{1,9},{5... | collective-permute-start | bytes 2312 | tf_op jit(solution)/shard_map/ppermute | solution.py:22
  12.1 8.0 %collective-permute-start.6 = (bf16[2,64,512]{2,1,0:T(8,128)(2,1)S(1)}, bf16[2,64,512]{2,1,0:T(8,128)(2,1)S(1)}, u32[]{:S(2)}, u32[]{:S(2)}) collective-permute-start(bf16[2,64,512]{2,1,0:T(8,128)(2,1)S(1)} %enter.1.refs_0_), channel_id=1, source_target_pairs={{0,3},{1,2},{2,1},{3,0},{4,7},{5,6},{6,5},{7,4},{8,11},{9,10},{10,... | collective-permute-start | bytes 393224 | tf_op jit(solution)/shard_map/ppermute | solution.py:22
  15.8 9.7 %collective-permute-start.5 = (bf16[2,64,512]{2,1,0:T(8,128)(2,1)S(1)}, bf16[2,64,512]{2,1,0:T(8,128)(2,1)S(1)}, u32[]{:S(2)}, u32[]{:S(2)}) collective-permute-start(bf16[2,64,512]{2,1,0:T(8,128)(2,1)S(1)} %enter.1.refs_0_), channel_id=1, source_target_pairs={{0,2},{1,3},{2,0},{3,1},{4,6},{5,7},{6,4},{7,5},{8,10},{9,11},{10,... | collective-permute-start | bytes 393224 | tf_op jit(solution)/shard_map/ppermute | solution.py:22
  15.8 9.7 %collective-permute-start.4 = (bf16[2,64,512]{2,1,0:T(8,128)(2,1)S(1)}, bf16[2,64,512]{2,1,0:T(8,128)(2,1)S(1)}, u32[]{:S(2)}, u32[]{:S(2)}) collective-permute-start(bf16[2,64,512]{2,1,0:T(8,128)(2,1)S(1)} %enter.1.refs_0_), channel_id=1, source_target_pairs={{0,1},{1,0},{2,3},{3,2},{4,5},{5,4},{6,7},{7,6},{8,9},{9,8},{10,11... | collective-permute-start | bytes 393224 | tf_op jit(solution)/shard_map/ppermute | solution.py:22
  29.3 2.0 %collective-permute-start.7 = (f16[2064,128]{1,0:T(8,128)(2,1)S(1)}, f16[2064,128]{1,0:T(8,128)(2,1)S(1)}, u32[]{:S(2)}, u32[]{:S(2)}) collective-permute-start(f16[2064,128]{1,0:T(8,128)(2,1)S(1)} %fusion), channel_id=1, source_target_pairs={{0,4},{4,0},{8,12},{12,8},{16,20},{20,16},{24,28},{28,24},{1,5},{5... | collective-permute-start | bytes 1585160 | tf_op jit(solution)/shard_map/ppermute | solution.py:22
  31.6 7.4 %collective-permute-start.10 = (f16[528,128]{1,0:T(8,128)(2,1)S(1)}, f16[528,128]{1,0:T(8,128)(2,1)S(1)}, u32[]{:S(2)}, u32[]{:S(2)}) collective-permute-start(f16[528,128]{1,0:T(8,128)(2,1)S(1)} %get-tuple-element.66), channel_id=1, source_target_pairs={{0,24},{4,28},{8,16},{12,20},{16,8},{20,12},{24,0},{28,4},{1,25},{... | collective-permute-start | bytes 405512 | tf_op jit(solution)/shard_map/ppermute | solution.py:22
  33.4 7.7 %collective-permute-start.9 = (f16[528,128]{1,0:T(8,128)(2,1)S(1)}, f16[528,128]{1,0:T(8,128)(2,1)S(1)}, u32[]{:S(2)}, u32[]{:S(2)}) collective-permute-start(f16[528,128]{1,0:T(8,128)(2,1)S(1)} %get-tuple-element.67), channel_id=1, source_target_pairs={{0,16},{4,20},{8,24},{12,28},{16,0},{20,4},{24,8},{28,12},{1,17},{... | collective-permute-start | bytes 405512 | tf_op jit(solution)/shard_map/ppermute | solution.py:22
  33.9 7.5 %collective-permute-start.8 = (f16[528,128]{1,0:T(8,128)(2,1)S(1)}, f16[528,128]{1,0:T(8,128)(2,1)S(1)}, u32[]{:S(2)}, u32[]{:S(2)}) collective-permute-start(f16[528,128]{1,0:T(8,128)(2,1)S(1)} %get-tuple-element.68), channel_id=1, source_target_pairs={{0,8},{4,12},{8,0},{12,4},{16,24},{20,28},{24,16},{28,20},{1,9},{5... | collective-permute-start | bytes 405512 | tf_op jit(solution)/shard_map/ppermute | solution.py:22
  35.2 9.9 %collective-permute-start.20 = (f16[528,128]{1,0:T(8,128)(2,1)S(1)}, f16[528,128]{1,0:T(8,128)(2,1)S(1)}, u32[]{:S(2)}, u32[]{:S(2)}) collective-permute-start(f16[528,128]{1,0:T(8,128)(2,1)S(1)} %get-tuple-element.63), channel_id=1, source_target_pairs={{0,3},{1,2},{2,1},{3,0},{4,7},{5,6},{6,5},{7,4},{8,11},{9,10},{10,... | collective-permute-start | bytes 405512 | tf_op jit(solution)/shard_map/ppermute | solution.py:22
  37.7 10.6 %collective-permute-start.19 = (f16[528,128]{1,0:T(8,128)(2,1)S(1)}, f16[528,128]{1,0:T(8,128)(2,1)S(1)}, u32[]{:S(2)}, u32[]{:S(2)}) collective-permute-start(f16[528,128]{1,0:T(8,128)(2,1)S(1)} %get-tuple-element.64), channel_id=1, source_target_pairs={{0,2},{1,3},{2,0},{3,1},{4,6},{5,7},{6,4},{7,5},{8,10},{9,11},{10,... | collective-permute-start | bytes 405512 | tf_op jit(solution)/shard_map/ppermute | solution.py:22
  41.5 7.3 %collective-permute-start.13 = (f16[512,128]{1,0:T(8,128)(2,1)S(1)}, f16[512,128]{1,0:T(8,128)(2,1)S(1)}, u32[]{:S(2)}, u32[]{:S(2)}) collective-permute-start(f16[512,128]{1,0:T(8,128)(2,1)S(1)} %convert_element_type.102), channel_id=1, source_target_pairs={{0,24},{4,28},{8,16},{12,20},{16,8},{20,12},{24,0},{28,4},{1,25},{... | collective-permute-start | bytes 393224 | tf_op jit(solution)/shard_map/ppermute | solution.py:22
  43.1 7.4 %collective-permute-start.12 = (f16[512,128]{1,0:T(8,128)(2,1)S(1)}, f16[512,128]{1,0:T(8,128)(2,1)S(1)}, u32[]{:S(2)}, u32[]{:S(2)}) collective-permute-start(f16[512,128]{1,0:T(8,128)(2,1)S(1)} %convert_element_type.102), channel_id=1, source_target_pairs={{0,16},{4,20},{8,24},{12,28},{16,0},{20,4},{24,8},{28,12},{1,17},{... | collective-permute-start | bytes 393224 | tf_op jit(solution)/shard_map/ppermute | solution.py:22
  43.8 6.8 %collective-permute-start.11 = (f16[512,128]{1,0:T(8,128)(2,1)S(1)}, f16[512,128]{1,0:T(8,128)(2,1)S(1)}, u32[]{:S(2)}, u32[]{:S(2)}) collective-permute-start(f16[512,128]{1,0:T(8,128)(2,1)S(1)} %convert_element_type.102), channel_id=1, source_target_pairs={{0,8},{4,12},{8,0},{12,4},{16,24},{20,28},{24,16},{28,20},{1,9},{5... | collective-permute-start | bytes 393224 | tf_op jit(solution)/shard_map/ppermute | solution.py:22
  45.1 6.0 %collective-permute-start.18 = (f16[528,128]{1,0:T(8,128)(2,1)S(1)}, f16[528,128]{1,0:T(8,128)(2,1)S(1)}, u32[]{:S(2)}, u32[]{:S(2)}) collective-permute-start(f16[528,128]{1,0:T(8,128)(2,1)S(1)} %get-tuple-element.65), channel_id=1, source_target_pairs={{0,1},{1,0},{2,3},{3,2},{4,5},{5,4},{6,7},{7,6},{8,9},{9,8},{10,11... | collective-permute-start | bytes 405512 | tf_op jit(solution)/shard_map/ppermute | solution.py:22
  48.3 6.5 %collective-permute-start.14 = (f16[512,128]{1,0:T(8,128)(2,1)S(1)}, f16[512,128]{1,0:T(8,128)(2,1)S(1)}, u32[]{:S(2)}, u32[]{:S(2)}) collective-permute-start(f16[512,128]{1,0:T(8,128)(2,1)S(1)} %convert_element_type.102), channel_id=1, source_target_pairs={{0,4},{4,0},{8,12},{12,8},{16,20},{20,16},{24,28},{28,24},{1,5},{5... | collective-permute-start | bytes 393224 | tf_op jit(solution)/shard_map/ppermute | solution.py:22
  48.8 6.5 %collective-permute-start.17 = (f16[512,128]{1,0:T(8,128)(2,1)S(1)}, f16[512,128]{1,0:T(8,128)(2,1)S(1)}, u32[]{:S(2)}, u32[]{:S(2)}) collective-permute-start(f16[512,128]{1,0:T(8,128)(2,1)S(1)} %collective-permute-done.13), channel_id=1, source_target_pairs={{0,4},{4,0},{8,12},{12,8},{16,20},{20,16},{24,28},{28,24},{1,5},{5... | collective-permute-start | bytes 393224 | tf_op jit(solution)/shard_map/ppermute | solution.py:22
  50.5 6.0 %collective-permute-start.16 = (f16[512,128]{1,0:T(8,128)(2,1)S(1)}, f16[512,128]{1,0:T(8,128)(2,1)S(1)}, u32[]{:S(2)}, u32[]{:S(2)}) collective-permute-start(f16[512,128]{1,0:T(8,128)(2,1)S(1)} %collective-permute-done.12), channel_id=1, source_target_pairs={{0,4},{4,0},{8,12},{12,8},{16,20},{20,16},{24,28},{28,24},{1,5},{5... | collective-permute-start | bytes 393224 | tf_op jit(solution)/shard_map/ppermute | solution.py:22
  50.5 6.0 %collective-permute-start.15 = (f16[512,128]{1,0:T(8,128)(2,1)S(1)}, f16[512,128]{1,0:T(8,128)(2,1)S(1)}, u32[]{:S(2)}, u32[]{:S(2)}) collective-permute-start(f16[512,128]{1,0:T(8,128)(2,1)S(1)} %collective-permute-done.11), channel_id=1, source_target_pairs={{0,4},{4,0},{8,12},{12,8},{16,20},{20,16},{24,28},{28,24},{1,5},{5... | collective-permute-start | bytes 393224 | tf_op jit(solution)/shard_map/ppermute | solution.py:22
  51.3 1.6 %collective-permute-start.21 = (f32[5,64]{1,0:T(8,128)S(1)}, f32[5,64]{1,0:T(8,128)S(1)}, u32[]{:S(2)}, u32[]{:S(2)}) collective-permute-start(f32[5,64]{1,0:T(8,128)S(1)} %get-tuple-element.59.summary), channel_id=1, source_target_pairs={{0,4},{4,0},{8,12},{12,8},{16,20},{20,16},{24,28},{28,24},{1,5},{5... | collective-permute-start | bytes 3848 | tf_op jit(solution)/shard_map/ppermute | solution.py:22
  53.0 4.6 %collective-permute-start.24 = (f32[5,64]{1,0:T(8,128)S(1)}, f32[5,64]{1,0:T(8,128)S(1)}, u32[]{:S(2)}, u32[]{:S(2)}) collective-permute-start(f32[5,64]{1,0:T(8,128)S(1)} %shard_map.86.refs_13_), channel_id=1, source_target_pairs={{0,24},{4,28},{8,16},{12,20},{16,8},{20,12},{24,0},{28,4},{1,25},{... | collective-permute-start | bytes 3848 | tf_op jit(solution)/shard_map/ppermute | solution.py:22
  54.8 3.6 %collective-permute-start.23 = (f32[5,64]{1,0:T(8,128)S(1)}, f32[5,64]{1,0:T(8,128)S(1)}, u32[]{:S(2)}, u32[]{:S(2)}) collective-permute-start(f32[5,64]{1,0:T(8,128)S(1)} %shard_map.86.refs_13_), channel_id=1, source_target_pairs={{0,16},{4,20},{8,24},{12,28},{16,0},{20,4},{24,8},{28,12},{1,17},{... | collective-permute-start | bytes 3848 | tf_op jit(solution)/shard_map/ppermute | solution.py:22
  55.4 3.6 %collective-permute-start.22 = (f32[5,64]{1,0:T(8,128)S(1)}, f32[5,64]{1,0:T(8,128)S(1)}, u32[]{:S(2)}, u32[]{:S(2)}) collective-permute-start(f32[5,64]{1,0:T(8,128)S(1)} %shard_map.86.refs_13_), channel_id=1, source_target_pairs={{0,8},{4,12},{8,0},{12,4},{16,24},{20,28},{24,16},{28,20},{1,9},{5... | collective-permute-start | bytes 3848 | tf_op jit(solution)/shard_map/ppermute | solution.py:22
  (7 other events, 33.4 us)

commit v5 on v4

--- a/solution.py
+++ b/solution.py
@@ -393,13 +393,19 @@
         density[d] = jnp.max(summed[d:d + 1, :]) * (1.0 / cells)
     moves.append(pltpu.make_async_copy(density, told, sems.at[count + 1]))
     moves[-1].start()
-    for j in range(tiles):
-        part = slice(j * LANES, (j + 1) * LANES)
-        for d in range(draws):
-            rows = pl.ds(j * draws + d, factors, stride=tiles * draws)
-            out[rows, :] = weight[:, part] * local[d, :, part] + fade[:, part] * columns[d] - innov[rows, :]
-    moves.append(pltpu.make_async_copy(out, near, sems.at[count]))
-    moves[-1].start()
+    share = factors // 2
+    deep = share * tiles * draws
+    for side in range(2):
+        some = slice(side * share, (side + 1) * share)
+        for j in range(tiles):
+            part = slice(j * LANES, (j + 1) * LANES)
+            for d in range(draws):
+                rows = pl.ds(side * deep + j * draws + d, share, stride=tiles * draws)
+                value = weight[some, part] * local[d, some, part] + fade[some, part] * columns[d][some]
+                out[rows, :] = value - innov[rows, :]
+        block = pl.ds(side * deep, deep)
+        moves.append(pltpu.make_async_copy(out.at[block, :], near.at[block, :], sems.at[count + 2 * side]))
+        moves[-1].start()
     for move in moves:
         move.wait()
 
@@ -565,7 +571,7 @@
         out_shape=(shape(innov.shape, f32), shape((draws,), f32), shape((size, LANES), f32)),
         in_specs=[whole] * (2 * chips + 4 + len(climb)),
         out_specs=(distant, distant, distant),
-        scratch_shapes=[pltpu.VMEM(innov.shape, f32), pltpu.SMEM((draws,), f32), pltpu.SemaphoreType.DMA((2 * chips + 2,))],
+        scratch_shapes=[pltpu.VMEM(innov.shape, f32), pltpu.SMEM((draws,), f32), pltpu.SemaphoreType.DMA((2 * chips + 3,))],
         name="leave",
         compiler_params=room(6),
     )(*[value.astype(f32) * factor for value in totals + passed], local_adjoint, fade, weight, innov, *climb)

time: 60.6 us -> 60.6 us (level)
  no operation moved by 1% of the time
where the time goes in v5:
time: 60.6 us; the launch traced here: 60.5 us
  starting transfers between devices  24.5 us (40%)
  waiting for transfers between devices  22.2 us (37%)
  Pallas kernels  9.56 us (16%)
  local copies, waits for them, and re-layouts  2.81 us (5%)
  between operations  0.89 us (1%)
    ppermute x25, starting transfers between devices, swap(): return lax.ppermute(value, axis, [(i, i ^ key) for i in range(count)])  24.5 us
    ppermute x25, waiting for transfers between devices, swap(): return lax.ppermute(value, axis, [(i, i ^ key) for i in range(count)])  22.2 us
    pallas_call x1, Pallas kernels, local(): pl.pallas_call(functools.partial(residual_kernel, draws, parts, series //...  3.73 us
    unnamed x14, local copies, waits for them, and re-layouts  2.81 us
    pallas_call x1, Pallas kernels, local(): pl.pallas_call(functools.partial(leave_kernel, draws, tiles, float(spans...  1.51 us
    pallas_call x1, Pallas kernels, local(): pl.pallas_call(functools.partial(forward_kernel, draws, tiles), out_shape...  1.4 us
  transfers between devices with their start and end apart: 25, of which 15 were waited for; matrix products, arithmetic and copies ran while one was open for 3% of the time, Pallas kernels for 5%

profile of v5, /device:TPU:0, one launch (start us, length us, event | category | flops | bytes accessed | tf_op | source)
XLA Modules:
  0.0 60.5 jit_solution(8156467398045496223)
XLA Ops:
  0.7 0.9 %copy-done.4 = f32[64,512]{1,0:T(8,128)S(1)} copy-done((f32[64,512]{1,0:T(8,128)S(1)}, f32[64,512]{1,0:T(8,128)}, u32[]{:S(2)}) %copy-start.4) | copy-done | bytes 131096
  4.1 3.8 %collective-permute-start.3 = (f32[3,64]{1,0:T(4,128)S(1)}, f32[3,64]{1,0:T(4,128)S(1)}, u32[]{:S(2)}, u32[]{:S(2)}) collective-permute-start(f32[3,64]{1,0:T(4,128)S(1)} %shard_map.85.refs_0_), channel_id=1, source_target_pairs={{0,24},{4,28},{8,16},{12,20},{16,8},{20,12},{24,0},{28,4},{1,25},{... | collective-permute-start | bytes 2312 | tf_op jit(solution)/shard_map/ppermute | solution.py:22
  8.5 1.4 %forward_scan.1 = (f32[2,64,512]{2,1,0:T(8,128)S(1)}, f32[64,512]{1,0:T(8,128)S(1)}) custom-call(f32[64,512]{1,0:T(8,128)S(1)} %get-tuple-element.34.decay, f32[2,64,512]{2,1,0:T(8,128)S(1)} %get-tuple-element.38.pushed), custom_call_target="tpu_custom_call" | custom-call | tf_op jit(solution)/shard_map/forward_scan/pallas_call | solution.py:468
  9.9 1.5 %collective-permute-done.2.refs_2_ = f32[3,64]{1,0:T(4,128)S(1)} collective-permute-done((f32[3,64]{1,0:T(4,128)S(1)}, f32[3,64]{1,0:T(4,128)S(1)}, u32[]{:S(2)}, u32[]{:S(2)}) %collective-permute-start.2) | collective-permute-done | bytes 800 | tf_op jit(solution)/shard_map/ppermute | solution.py:22
  12.1 3.7 %collective-permute-start.6 = (bf16[2,64,512]{2,1,0:T(8,128)(2,1)S(1)}, bf16[2,64,512]{2,1,0:T(8,128)(2,1)S(1)}, u32[]{:S(2)}, u32[]{:S(2)}) collective-permute-start(bf16[2,64,512]{2,1,0:T(8,128)(2,1)S(1)} %enter.1.refs_0_), channel_id=1, source_target_pairs={{0,3},{1,2},{2,1},{3,0},{4,7},{5,6},{6,5},{7,4},{8,11},{9,10},{10,... | collective-permute-start | bytes 393224 | tf_op jit(solution)/shard_map/ppermute | solution.py:22
  16.5 1.4 %copy.11 = bf16[1024,2,256]{0,2,1:T(8,128)(2,1)S(1)} copy(bf16[1024,2,256]{2,1,0:T(2,128)(2,1)S(1)} %copy-done.5) | data formatting | bytes 2097152 | tf_op args[4]
  18.2 1.9 %collective-permute-done.6.refs_3_ = bf16[2,64,512]{2,1,0:T(8,128)(2,1)S(1)} collective-permute-done((bf16[2,64,512]{2,1,0:T(8,128)(2,1)S(1)}, bf16[2,64,512]{2,1,0:T(8,128)(2,1)S(1)}, u32[]{:S(2)}, u32[]{:S(2)}) %collective-permute-start.6) | collective-permute-done | bytes 131104 | tf_op jit(solution)/shard_map/ppermute | solution.py:22
  20.0 5.4 %collective-permute-done.5.refs_2_ = bf16[2,64,512]{2,1,0:T(8,128)(2,1)S(1)} collective-permute-done((bf16[2,64,512]{2,1,0:T(8,128)(2,1)S(1)}, bf16[2,64,512]{2,1,0:T(8,128)(2,1)S(1)}, u32[]{:S(2)}, u32[]{:S(2)}) %collective-permute-start.5) | collective-permute-done | bytes 131104 | tf_op jit(solution)/shard_map/ppermute | solution.py:22
  25.5 3.7 %residual.1 = (f32[4,528,128]{2,1,0:T(8,128)S(1)}, f32[2,2064,128]{2,1,0:T(8,128)S(1)}) custom-call(bf16[2,64,512]{2,1,0:T(8,128)(2,1)S(1)} %enter.1.refs_0_, bf16[2,64,512]{2,1,0:T(8,128)(2,1)S(1)} %collective-permute-done.4.refs_1_, bf16[2,64,512]{2,1,0:T(8,128)(2,1)S(1)} %collective-permute-done.5.refs_2_, ...), custom_call_target="tpu_custom_call" | custom-call | tf_op jit(solution)/shard_map/residual/pallas_call | solution.py:490
  29.4 1.9 %collective-permute-done.7 = f16[2064,128]{1,0:T(8,128)(2,1)S(1)} collective-permute-done((f16[2064,128]{1,0:T(8,128)(2,1)S(1)}, f16[2064,128]{1,0:T(8,128)(2,1)S(1)}, u32[]{:S(2)}, u32[]{:S(2)}) %collective-permute-start.7) | collective-permute-done | bytes 528416 | tf_op jit(solution)/shard_map/ppermute | solution.py:22
  31.6 1.9 %collective-permute-start.10 = (f16[528,128]{1,0:T(8,128)(2,1)S(1)}, f16[528,128]{1,0:T(8,128)(2,1)S(1)}, u32[]{:S(2)}, u32[]{:S(2)}) collective-permute-start(f16[528,128]{1,0:T(8,128)(2,1)S(1)} %get-tuple-element.66), channel_id=1, source_target_pairs={{0,24},{4,28},{8,16},{12,20},{16,8},{20,12},{24,0},{28,4},{1,25},{... | collective-permute-start | bytes 405512 | tf_op jit(solution)/shard_map/ppermute | solution.py:22
  33.9 1.2 %collective-permute-start.8 = (f16[528,128]{1,0:T(8,128)(2,1)S(1)}, f16[528,128]{1,0:T(8,128)(2,1)S(1)}, u32[]{:S(2)}, u32[]{:S(2)}) collective-permute-start(f16[528,128]{1,0:T(8,128)(2,1)S(1)} %get-tuple-element.68), channel_id=1, source_target_pairs={{0,8},{4,12},{8,0},{12,4},{16,24},{20,28},{24,16},{28,20},{1,9},{5... | collective-permute-start | bytes 405512 | tf_op jit(solution)/shard_map/ppermute | solution.py:22
  35.2 2.5 %collective-permute-start.20 = (f16[528,128]{1,0:T(8,128)(2,1)S(1)}, f16[528,128]{1,0:T(8,128)(2,1)S(1)}, u32[]{:S(2)}, u32[]{:S(2)}) collective-permute-start(f16[528,128]{1,0:T(8,128)(2,1)S(1)} %get-tuple-element.63), channel_id=1, source_target_pairs={{0,3},{1,2},{2,1},{3,0},{4,7},{5,6},{6,5},{7,4},{8,11},{9,10},{10,... | collective-permute-start | bytes 405512 | tf_op jit(solution)/shard_map/ppermute | solution.py:22
  37.7 1.3 %collective-permute-done.10 = f16[528,128]{1,0:T(8,128)(2,1)S(1)} collective-permute-done((f16[528,128]{1,0:T(8,128)(2,1)S(1)}, f16[528,128]{1,0:T(8,128)(2,1)S(1)}, u32[]{:S(2)}, u32[]{:S(2)}) %collective-permute-start.10) | collective-permute-done | bytes 135200 | tf_op jit(solution)/shard_map/ppermute | solution.py:22
  39.0 2.1 %collective-permute-done.9 = f16[528,128]{1,0:T(8,128)(2,1)S(1)} collective-permute-done((f16[528,128]{1,0:T(8,128)(2,1)S(1)}, f16[528,128]{1,0:T(8,128)(2,1)S(1)}, u32[]{:S(2)}, u32[]{:S(2)}) %collective-permute-start.9) | collective-permute-done | bytes 135200 | tf_op jit(solution)/shard_map/ppermute | solution.py:22
  41.5 1.6 %collective-permute-start.13 = (f16[512,128]{1,0:T(8,128)(2,1)S(1)}, f16[512,128]{1,0:T(8,128)(2,1)S(1)}, u32[]{:S(2)}, u32[]{:S(2)}) collective-permute-start(f16[512,128]{1,0:T(8,128)(2,1)S(1)} %convert_element_type.102), channel_id=1, source_target_pairs={{0,24},{4,28},{8,16},{12,20},{16,8},{20,12},{24,0},{28,4},{1,25},{... | collective-permute-start | bytes 393224 | tf_op jit(solution)/shard_map/ppermute | solution.py:22
  43.8 1.3 %collective-permute-start.11 = (f16[512,128]{1,0:T(8,128)(2,1)S(1)}, f16[512,128]{1,0:T(8,128)(2,1)S(1)}, u32[]{:S(2)}, u32[]{:S(2)}) collective-permute-start(f16[512,128]{1,0:T(8,128)(2,1)S(1)} %convert_element_type.102), channel_id=1, source_target_pairs={{0,8},{4,12},{8,0},{12,4},{16,24},{20,28},{24,16},{28,20},{1,9},{5... | collective-permute-start | bytes 393224 | tf_op jit(solution)/shard_map/ppermute | solution.py:22
  45.1 1.2 %collective-permute-start.18 = (f16[528,128]{1,0:T(8,128)(2,1)S(1)}, f16[528,128]{1,0:T(8,128)(2,1)S(1)}, u32[]{:S(2)}, u32[]{:S(2)}) collective-permute-start(f16[528,128]{1,0:T(8,128)(2,1)S(1)} %get-tuple-element.65), channel_id=1, source_target_pairs={{0,1},{1,0},{2,3},{3,2},{4,5},{5,4},{6,7},{7,6},{8,9},{9,8},{10,11... | collective-permute-start | bytes 405512 | tf_op jit(solution)/shard_map/ppermute | solution.py:22
  46.3 2.0 %collective-permute-done.19 = f16[528,128]{1,0:T(8,128)(2,1)S(1)} collective-permute-done((f16[528,128]{1,0:T(8,128)(2,1)S(1)}, f16[528,128]{1,0:T(8,128)(2,1)S(1)}, u32[]{:S(2)}, u32[]{:S(2)}) %collective-permute-start.19) | collective-permute-done | bytes 135200 | tf_op jit(solution)/shard_map/ppermute | solution.py:22
  48.8 1.7 %collective-permute-done.12 = f16[512,128]{1,0:T(8,128)(2,1)S(1)} collective-permute-done((f16[512,128]{1,0:T(8,128)(2,1)S(1)}, f16[512,128]{1,0:T(8,128)(2,1)S(1)}, u32[]{:S(2)}, u32[]{:S(2)}) %collective-permute-start.12) | collective-permute-done | bytes 131104 | tf_op jit(solution)/shard_map/ppermute | solution.py:22
  53.0 1.8 %collective-permute-start.24 = (f32[5,64]{1,0:T(8,128)S(1)}, f32[5,64]{1,0:T(8,128)S(1)}, u32[]{:S(2)}, u32[]{:S(2)}) collective-permute-start(f32[5,64]{1,0:T(8,128)S(1)} %shard_map.86.refs_13_), channel_id=1, source_target_pairs={{0,24},{4,28},{8,16},{12,20},{16,8},{20,12},{24,0},{28,4},{1,25},{... | collective-permute-start | bytes 3848 | tf_op jit(solution)/shard_map/ppermute | solution.py:22
  55.4 1.2 %collective-permute-start.22 = (f32[5,64]{1,0:T(8,128)S(1)}, f32[5,64]{1,0:T(8,128)S(1)}, u32[]{:S(2)}, u32[]{:S(2)}) collective-permute-start(f32[5,64]{1,0:T(8,128)S(1)} %shard_map.86.refs_13_), channel_id=1, source_target_pairs={{0,8},{4,12},{8,0},{12,4},{16,24},{20,28},{24,16},{28,20},{1,9},{5... | collective-permute-start | bytes 3848 | tf_op jit(solution)/shard_map/ppermute | solution.py:22
  57.6 0.9 %collective-permute-done.23.refs_15_ = f32[5,64]{1,0:T(8,128)S(1)} collective-permute-done((f32[5,64]{1,0:T(8,128)S(1)}, f32[5,64]{1,0:T(8,128)S(1)}, u32[]{:S(2)}, u32[]{:S(2)}) %collective-permute-start.23) | collective-permute-done | bytes 1312 | tf_op jit(solution)/shard_map/ppermute | solution.py:22
  59.0 1.5 %leave.1 = (f32[512,128]{1,0:T(8,128)}, f32[2]{0:T(128)}, f32[4096,128]{1,0:T(8,128)}) custom-call(f32[512,128]{1,0:T(8,128)S(1)} %get-tuple-element.76.refs_0_, f32[512,128]{1,0:T(8,128)S(1)} %get-tuple-element.70.refs_1_, f32[512,128]{1,0:T(8,128)S(1)} %get-tuple-element.71.refs_2_, f32[512,128]{1,0:T(8,128)S(1)} %get-tuple-element.72.refs_3_, ...), custom_call_target="tpu_custom_call" | custom-call | tf_op jit(solution)/shard_map/leave/pallas_call | solution.py:569
  (65 shorter events, 11.7 us)
Async XLA Ops:
  4.1 5.8 %collective-permute-start.3 = (f32[3,64]{1,0:T(4,128)S(1)}, f32[3,64]{1,0:T(4,128)S(1)}, u32[]{:S(2)}, u32[]{:S(2)}) collective-permute-start(f32[3,64]{1,0:T(4,128)S(1)} %shard_map.85.refs_0_), channel_id=1, source_target_pairs={{0,24},{4,28},{8,16},{12,20},{16,8},{20,12},{24,0},{28,4},{1,25},{... | collective-permute-start | bytes 2312 | tf_op jit(solution)/shard_map/ppermute | solution.py:22
  7.9 3.6 %collective-permute-start.2 = (f32[3,64]{1,0:T(4,128)S(1)}, f32[3,64]{1,0:T(4,128)S(1)}, u32[]{:S(2)}, u32[]{:S(2)}) collective-permute-start(f32[3,64]{1,0:T(4,128)S(1)} %shard_map.85.refs_0_), channel_id=1, source_target_pairs={{0,16},{4,20},{8,24},{12,28},{16,0},{20,4},{24,8},{28,12},{1,17},{... | collective-permute-start | bytes 2312 | tf_op jit(solution)/shard_map/ppermute | solution.py:22
  8.4 3.6 %collective-permute-start.1 = (f32[3,64]{1,0:T(4,128)S(1)}, f32[3,64]{1,0:T(4,128)S(1)}, u32[]{:S(2)}, u32[]{:S(2)}) collective-permute-start(f32[3,64]{1,0:T(4,128)S(1)} %shard_map.85.refs_0_), channel_id=1, source_target_pairs={{0,8},{4,12},{8,0},{12,4},{16,24},{20,28},{24,16},{28,20},{1,9},{5... | collective-permute-start | bytes 2312 | tf_op jit(solution)/shard_map/ppermute | solution.py:22
  12.1 8.0 %collective-permute-start.6 = (bf16[2,64,512]{2,1,0:T(8,128)(2,1)S(1)}, bf16[2,64,512]{2,1,0:T(8,128)(2,1)S(1)}, u32[]{:S(2)}, u32[]{:S(2)}) collective-permute-start(bf16[2,64,512]{2,1,0:T(8,128)(2,1)S(1)} %enter.1.refs_0_), channel_id=1, source_target_pairs={{0,3},{1,2},{2,1},{3,0},{4,7},{5,6},{6,5},{7,4},{8,11},{9,10},{10,... | collective-permute-start | bytes 393224 | tf_op jit(solution)/shard_map/ppermute | solution.py:22
  15.8 9.7 %collective-permute-start.5 = (bf16[2,64,512]{2,1,0:T(8,128)(2,1)S(1)}, bf16[2,64,512]{2,1,0:T(8,128)(2,1)S(1)}, u32[]{:S(2)}, u32[]{:S(2)}) collective-permute-start(bf16[2,64,512]{2,1,0:T(8,128)(2,1)S(1)} %enter.1.refs_0_), channel_id=1, source_target_pairs={{0,2},{1,3},{2,0},{3,1},{4,6},{5,7},{6,4},{7,5},{8,10},{9,11},{10,... | collective-permute-start | bytes 393224 | tf_op jit(solution)/shard_map/ppermute | solution.py:22
  15.8 9.7 %collective-permute-start.4 = (bf16[2,64,512]{2,1,0:T(8,128)(2,1)S(1)}, bf16[2,64,512]{2,1,0:T(8,128)(2,1)S(1)}, u32[]{:S(2)}, u32[]{:S(2)}) collective-permute-start(bf16[2,64,512]{2,1,0:T(8,128)(2,1)S(1)} %enter.1.refs_0_), channel_id=1, source_target_pairs={{0,1},{1,0},{2,3},{3,2},{4,5},{5,4},{6,7},{7,6},{8,9},{9,8},{10,11... | collective-permute-start | bytes 393224 | tf_op jit(solution)/shard_map/ppermute | solution.py:22
  29.3 2.0 %collective-permute-start.7 = (f16[2064,128]{1,0:T(8,128)(2,1)S(1)}, f16[2064,128]{1,0:T(8,128)(2,1)S(1)}, u32[]{:S(2)}, u32[]{:S(2)}) collective-permute-start(f16[2064,128]{1,0:T(8,128)(2,1)S(1)} %fusion), channel_id=1, source_target_pairs={{0,4},{4,0},{8,12},{12,8},{16,20},{20,16},{24,28},{28,24},{1,5},{5... | collective-permute-start | bytes 1585160 | tf_op jit(solution)/shard_map/ppermute | solution.py:22
  31.6 7.4 %collective-permute-start.10 = (f16[528,128]{1,0:T(8,128)(2,1)S(1)}, f16[528,128]{1,0:T(8,128)(2,1)S(1)}, u32[]{:S(2)}, u32[]{:S(2)}) collective-permute-start(f16[528,128]{1,0:T(8,128)(2,1)S(1)} %get-tuple-element.66), channel_id=1, source_target_pairs={{0,24},{4,28},{8,16},{12,20},{16,8},{20,12},{24,0},{28,4},{1,25},{... | collective-permute-start | bytes 405512 | tf_op jit(solution)/shard_map/ppermute | solution.py:22
  33.4 7.7 %collective-permute-start.9 = (f16[528,128]{1,0:T(8,128)(2,1)S(1)}, f16[528,128]{1,0:T(8,128)(2,1)S(1)}, u32[]{:S(2)}, u32[]{:S(2)}) collective-permute-start(f16[528,128]{1,0:T(8,128)(2,1)S(1)} %get-tuple-element.67), channel_id=1, source_target_pairs={{0,16},{4,20},{8,24},{12,28},{16,0},{20,4},{24,8},{28,12},{1,17},{... | collective-permute-start | bytes 405512 | tf_op jit(solution)/shard_map/ppermute | solution.py:22
  33.9 7.5 %collective-permute-start.8 = (f16[528,128]{1,0:T(8,128)(2,1)S(1)}, f16[528,128]{1,0:T(8,128)(2,1)S(1)}, u32[]{:S(2)}, u32[]{:S(2)}) collective-permute-start(f16[528,128]{1,0:T(8,128)(2,1)S(1)} %get-tuple-element.68), channel_id=1, source_target_pairs={{0,8},{4,12},{8,0},{12,4},{16,24},{20,28},{24,16},{28,20},{1,9},{5... | collective-permute-start | bytes 405512 | tf_op jit(solution)/shard_map/ppermute | solution.py:22
  35.2 9.9 %collective-permute-start.20 = (f16[528,128]{1,0:T(8,128)(2,1)S(1)}, f16[528,128]{1,0:T(8,128)(2,1)S(1)}, u32[]{:S(2)}, u32[]{:S(2)}) collective-permute-start(f16[528,128]{1,0:T(8,128)(2,1)S(1)} %get-tuple-element.63), channel_id=1, source_target_pairs={{0,3},{1,2},{2,1},{3,0},{4,7},{5,6},{6,5},{7,4},{8,11},{9,10},{10,... | collective-permute-start | bytes 405512 | tf_op jit(solution)/shard_map/ppermute | solution.py:22
  37.7 10.6 %collective-permute-start.19 = (f16[528,128]{1,0:T(8,128)(2,1)S(1)}, f16[528,128]{1,0:T(8,128)(2,1)S(1)}, u32[]{:S(2)}, u32[]{:S(2)}) collective-permute-start(f16[528,128]{1,0:T(8,128)(2,1)S(1)} %get-tuple-element.64), channel_id=1, source_target_pairs={{0,2},{1,3},{2,0},{3,1},{4,6},{5,7},{6,4},{7,5},{8,10},{9,11},{10,... | collective-permute-start | bytes 405512 | tf_op jit(solution)/shard_map/ppermute | solution.py:22
  41.5 7.3 %collective-permute-start.13 = (f16[512,128]{1,0:T(8,128)(2,1)S(1)}, f16[512,128]{1,0:T(8,128)(2,1)S(1)}, u32[]{:S(2)}, u32[]{:S(2)}) collective-permute-start(f16[512,128]{1,0:T(8,128)(2,1)S(1)} %convert_element_type.102), channel_id=1, source_target_pairs={{0,24},{4,28},{8,16},{12,20},{16,8},{20,12},{24,0},{28,4},{1,25},{... | collective-permute-start | bytes 393224 | tf_op jit(solution)/shard_map/ppermute | solution.py:22
  43.1 7.4 %collective-permute-start.12 = (f16[512,128]{1,0:T(8,128)(2,1)S(1)}, f16[512,128]{1,0:T(8,128)(2,1)S(1)}, u32[]{:S(2)}, u32[]{:S(2)}) collective-permute-start(f16[512,128]{1,0:T(8,128)(2,1)S(1)} %convert_element_type.102), channel_id=1, source_target_pairs={{0,16},{4,20},{8,24},{12,28},{16,0},{20,4},{24,8},{28,12},{1,17},{... | collective-permute-start | bytes 393224 | tf_op jit(solution)/shard_map/ppermute | solution.py:22
  43.8 6.8 %collective-permute-start.11 = (f16[512,128]{1,0:T(8,128)(2,1)S(1)}, f16[512,128]{1,0:T(8,128)(2,1)S(1)}, u32[]{:S(2)}, u32[]{:S(2)}) collective-permute-start(f16[512,128]{1,0:T(8,128)(2,1)S(1)} %convert_element_type.102), channel_id=1, source_target_pairs={{0,8},{4,12},{8,0},{12,4},{16,24},{20,28},{24,16},{28,20},{1,9},{5... | collective-permute-start | bytes 393224 | tf_op jit(solution)/shard_map/ppermute | solution.py:22
  45.1 6.0 %collective-permute-start.18 = (f16[528,128]{1,0:T(8,128)(2,1)S(1)}, f16[528,128]{1,0:T(8,128)(2,1)S(1)}, u32[]{:S(2)}, u32[]{:S(2)}) collective-permute-start(f16[528,128]{1,0:T(8,128)(2,1)S(1)} %get-tuple-element.65), channel_id=1, source_target_pairs={{0,1},{1,0},{2,3},{3,2},{4,5},{5,4},{6,7},{7,6},{8,9},{9,8},{10,11... | collective-permute-start | bytes 405512 | tf_op jit(solution)/shard_map/ppermute | solution.py:22
  48.3 6.5 %collective-permute-start.14 = (f16[512,128]{1,0:T(8,128)(2,1)S(1)}, f16[512,128]{1,0:T(8,128)(2,1)S(1)}, u32[]{:S(2)}, u32[]{:S(2)}) collective-permute-start(f16[512,128]{1,0:T(8,128)(2,1)S(1)} %convert_element_type.102), channel_id=1, source_target_pairs={{0,4},{4,0},{8,12},{12,8},{16,20},{20,16},{24,28},{28,24},{1,5},{5... | collective-permute-start | bytes 393224 | tf_op jit(solution)/shard_map/ppermute | solution.py:22
  48.8 6.5 %collective-permute-start.17 = (f16[512,128]{1,0:T(8,128)(2,1)S(1)}, f16[512,128]{1,0:T(8,128)(2,1)S(1)}, u32[]{:S(2)}, u32[]{:S(2)}) collective-permute-start(f16[512,128]{1,0:T(8,128)(2,1)S(1)} %collective-permute-done.13), channel_id=1, source_target_pairs={{0,4},{4,0},{8,12},{12,8},{16,20},{20,16},{24,28},{28,24},{1,5},{5... | collective-permute-start | bytes 393224 | tf_op jit(solution)/shard_map/ppermute | solution.py:22
  50.5 6.0 %collective-permute-start.16 = (f16[512,128]{1,0:T(8,128)(2,1)S(1)}, f16[512,128]{1,0:T(8,128)(2,1)S(1)}, u32[]{:S(2)}, u32[]{:S(2)}) collective-permute-start(f16[512,128]{1,0:T(8,128)(2,1)S(1)} %collective-permute-done.12), channel_id=1, source_target_pairs={{0,4},{4,0},{8,12},{12,8},{16,20},{20,16},{24,28},{28,24},{1,5},{5... | collective-permute-start | bytes 393224 | tf_op jit(solution)/shard_map/ppermute | solution.py:22
  50.5 6.0 %collective-permute-start.15 = (f16[512,128]{1,0:T(8,128)(2,1)S(1)}, f16[512,128]{1,0:T(8,128)(2,1)S(1)}, u32[]{:S(2)}, u32[]{:S(2)}) collective-permute-start(f16[512,128]{1,0:T(8,128)(2,1)S(1)} %collective-permute-done.11), channel_id=1, source_target_pairs={{0,4},{4,0},{8,12},{12,8},{16,20},{20,16},{24,28},{28,24},{1,5},{5... | collective-permute-start | bytes 393224 | tf_op jit(solution)/shard_map/ppermute | solution.py:22
  51.3 1.6 %collective-permute-start.21 = (f32[5,64]{1,0:T(8,128)S(1)}, f32[5,64]{1,0:T(8,128)S(1)}, u32[]{:S(2)}, u32[]{:S(2)}) collective-permute-start(f32[5,64]{1,0:T(8,128)S(1)} %get-tuple-element.59.summary), channel_id=1, source_target_pairs={{0,4},{4,0},{8,12},{12,8},{16,20},{20,16},{24,28},{28,24},{1,5},{5... | collective-permute-start | bytes 3848 | tf_op jit(solution)/shard_map/ppermute | solution.py:22
  53.0 4.6 %collective-permute-start.24 = (f32[5,64]{1,0:T(8,128)S(1)}, f32[5,64]{1,0:T(8,128)S(1)}, u32[]{:S(2)}, u32[]{:S(2)}) collective-permute-start(f32[5,64]{1,0:T(8,128)S(1)} %shard_map.86.refs_13_), channel_id=1, source_target_pairs={{0,24},{4,28},{8,16},{12,20},{16,8},{20,12},{24,0},{28,4},{1,25},{... | collective-permute-start | bytes 3848 | tf_op jit(solution)/shard_map/ppermute | solution.py:22
  54.8 3.6 %collective-permute-start.23 = (f32[5,64]{1,0:T(8,128)S(1)}, f32[5,64]{1,0:T(8,128)S(1)}, u32[]{:S(2)}, u32[]{:S(2)}) collective-permute-start(f32[5,64]{1,0:T(8,128)S(1)} %shard_map.86.refs_13_), channel_id=1, source_target_pairs={{0,16},{4,20},{8,24},{12,28},{16,0},{20,4},{24,8},{28,12},{1,17},{... | collective-permute-start | bytes 3848 | tf_op jit(solution)/shard_map/ppermute | solution.py:22
  55.4 3.6 %collective-permute-start.22 = (f32[5,64]{1,0:T(8,128)S(1)}, f32[5,64]{1,0:T(8,128)S(1)}, u32[]{:S(2)}, u32[]{:S(2)}) collective-permute-start(f32[5,64]{1,0:T(8,128)S(1)} %shard_map.86.refs_13_), channel_id=1, source_target_pairs={{0,8},{4,12},{8,0},{12,4},{16,24},{20,28},{24,16},{28,20},{1,9},{5... | collective-permute-start | bytes 3848 | tf_op jit(solution)/shard_map/ppermute | solution.py:22
  (7 other events, 33.4 us)
